TPU v7x, 32 devices: a whole 2x2x4 slice. The times are simulated.
32 devices in a mesh: dp: 16 (over z, x, core), tensor: 2 (over y).
Axes of the slice: x: 2, y: 2, z: 4, core: 2. Of those that a mesh axis runs over, the one named last changes fastest.
Arguments:
- tokens: bfloat16 [2048, 2048], P('dp'), may hold values from -6 to 6
- cotangent: bfloat16 [2048, 2048], P('dp'), may hold values from -6 to 6
- owner_slot: int32 [2048], replicated, may hold values from 0 to 2047, as said below
- sequence_lengths: int32 [32, 3], P('dp'), may hold values from 1 to 32, 64 in all within a row
- norm_gain: bfloat16 [2048], P('dp'), may hold values from 0.25 to 1.75
- inner_weight: bfloat16 [2048, 2, 4096], P('dp', None, 'tensor'), may hold values from -0.125 to 0.125
- filter_weight: float32 [4, 4096], P(None, 'tensor'), may hold values from -3 to 3
- convolution_bias: float32 [4096], P('tensor'), may hold values from -3 to 3
- select_weight: bfloat16 [4096, 160], P('tensor'), may hold values from -0.09375 to 0.09375
- step_weight: bfloat16 [128, 4096], P(None, 'tensor'), may hold values from -0.5 to 0.5
- step_bias: float32 [4096], P('tensor'), may hold values from -6 to -2
- decay_log: float32 [16, 4096], P(None, 'tensor'), may hold values from -1 to 2.77
- skip_weight: float32 [4096], P('tensor'), may hold values from 0.5 to 1.5
- output_weight: bfloat16 [4096, 2048], P('tensor', 'dp'), may hold values from -0.25 to 0.25
Outputs:
- output: bfloat16 [2048, 2048], P('dp')
- input_grad: float32 [2048, 2048], P('dp')
- norm_gain_grad: float32 [2048], P('dp')
- inner_weight_grad: float32 [2048, 2, 4096], P('dp', None, 'tensor')
- filter_weight_grad: float32 [4, 4096], P(None, 'tensor')
- filter_bias_grad: float32 [4096], P('tensor')
- select_weight_grad: float32 [4096, 160], P('tensor')
- step_weight_grad: float32 [128, 4096], P(None, 'tensor')
- step_bias_grad: float32 [4096], P('tensor')
- decay_log_grad: float32 [16, 4096], P(None, 'tensor')
- skip_weight_grad: float32 [4096], P('tensor')
- output_weight_grad: float32 [4096, 2048], P('tensor', 'dp')
Inputs may be any that keep to these rules, and one draw needn't show every extreme that they name: `owner_slot`: a permutation; the input rows of each index of dp (blocks of 128) send exactly 8 tokens to the owner block of every index. `sequence_lengths`: each row sums to 64; its largest entry is 32.
All inputs are finite; a program needn't handle non-finite values.
Results may differ from a plain program's by a relative error of at most 0.0098.
Values may be sent and summed in bfloat16 or wider, within the bound.
No kernel may reach another device: no remote copies, remote signals or barrier semaphores. Data moves between devices by JAX's collectives and lax.ppermute only.
A program may use at most 96 MiB of HBM per device.

v0:
```python
from functools import partial

import jax
import jax.numpy as jnp
from jax import lax
from jax.sharding import PartitionSpec as P

MB = 2


EPSILON = 1e-05


def positions(lengths_table, segment_rows):
    starts = jnp.cumsum(lengths_table, axis=1, dtype=jnp.int32) - lengths_table
    index_row = jnp.arange(segment_rows, dtype=jnp.int32)
    begins = jnp.max(
        jnp.where(starts[:, None, :] <= index_row[None, :, None], starts[:, None, :], 0), axis=2
    )
    return index_row[None, :] - begins


def conv_silu(stream, filter_weight, convolution_bias, position):
    row_count = stream.shape[0]
    total = jnp.zeros(stream.shape, jnp.float32) + convolution_bias[None, :]
    for lag_steps in range(filter_weight.shape[0]):
        shifted = jnp.pad(stream, ((lag_steps, 0), (0, 0)))[:row_count]
        valid = (position >= lag_steps)[:, None]
        total = total + filter_weight[filter_weight.shape[0] - 1 - lag_steps][None, :] * jnp.where(
            valid, shifted, jnp.zeros_like(shifted)
        )
    return jax.nn.silu(total)


def mixer_scan(
    activated, gate_in, step_pre, coupling_in, coupling_out, decay_log, skip_weight, keep_mask
):
    step_rate = jax.nn.softplus(step_pre)
    decay_rate = -jnp.exp(decay_log)
    row_count, channels = activated.shape
    block_size = 8
    block_count = row_count // block_size
    lower = jnp.arange(block_size)[:, None] >= jnp.arange(block_size)[None, :]

    def advance(carried, pieces):
        act_block, rate_block, in_block, out_block, keep_block = pieces
        log_steps = rate_block[:, None, :] * decay_rate[None, :, :]
        running = jnp.cumsum(log_steps, axis=0)
        resets = jnp.cumsum(1.0 - keep_block)
        linked = jnp.logical_and(resets[:, None] == resets[None, :], lower)
        spread = jnp.minimum(running[:, None] - running[None, :], 0.0)
        weight_table = jnp.where(linked[:, :, None, None], jnp.exp(spread), 0.0)
        incoming_rows = in_block[:, :, None] * (rate_block * act_block)[:, None, :]
        hidden_states = jnp.einsum("lhyj,hyj->lyj", weight_table, incoming_rows)
        carry_keep = (resets == 0.0).astype(jnp.float32)[:, None, None]
        hidden_states = hidden_states + carry_keep * jnp.exp(running) * carried[None]
        outputs = jnp.sum(out_block[:, :, None] * hidden_states, axis=1)
        return (hidden_states[-1], outputs)

    pieces = (
        activated.reshape(block_count, block_size, channels),
        step_rate.reshape(block_count, block_size, channels),
        coupling_in.reshape(block_count, block_size, -1),
        coupling_out.reshape(block_count, block_size, -1),
        keep_mask.reshape(block_count, block_size),
    )
    initial = jnp.zeros(decay_rate.shape, jnp.float32)
    _, scan_result = lax.scan(jax.checkpoint(advance), initial, pieces)
    mixed_out = scan_result.reshape(row_count, channels) + skip_weight[None, :] * activated
    return mixed_out * jax.nn.silu(gate_in)


def body(
    tokens,
    cotangent,
    owner_slot,
    sequence_lengths,
    norm_gain,
    inner_weight,
    filter_weight,
    convolution_bias,
    select_weight,
    step_weight,
    step_bias,
    decay_log,
    skip_weight,
    output_weight,
):
    devices = lax.axis_size("dp")
    device_index = lax.axis_index("dp")
    local_rows = tokens.shape[0]
    share_rows = local_rows // devices
    width = tokens.shape[1]
    rank_width = step_weight.shape[0]
    state_width = decay_log.shape[0]
    every_slot = owner_slot.reshape(devices, local_rows)
    own_slots = lax.dynamic_index_in_dim(every_slot, device_index, 0, keepdims=False)
    send_order = jnp.argsort(own_slots // local_rows, stable=True)
    outgoing = (
        tokens[send_order].reshape(devices, share_rows, width),
        cotangent[send_order].reshape(devices, share_rows, width),
    )
    incoming = (
        lax.all_to_all(outgoing[0], "dp", split_axis=0, concat_axis=0, tiled=True),
        lax.all_to_all(outgoing[1], "dp", split_axis=0, concat_axis=0, tiled=True),
    )
    foreign = (every_slot // local_rows != device_index).astype(jnp.int32)
    picked = jnp.argsort(foreign, axis=1, stable=True)[:, :share_rows]
    arrived_slots = (
        jnp.take_along_axis(every_slot, picked, axis=1) - device_index * local_rows
    ).reshape(-1)
    arrival_order = jnp.argsort(arrived_slots)
    owned_tokens = incoming[0].reshape(-1, width)[arrival_order]
    owned_cotangent = incoming[1].reshape(-1, width)[arrival_order]
    batch_rows = local_rows // MB
    position_table = positions(sequence_lengths, batch_rows)
    inner_acc = jnp.zeros(inner_weight.shape, jnp.float32)
    output_acc = jnp.zeros((output_weight.shape[0], width), jnp.float32)
    gain_acc = jnp.zeros((width,), jnp.float32)
    filter_acc = jnp.zeros(filter_weight.shape, jnp.float32)
    fbias_acc = jnp.zeros(convolution_bias.shape, jnp.float32)
    select_acc = jnp.zeros(select_weight.shape, jnp.float32)
    stepw_acc = jnp.zeros(step_weight.shape, jnp.float32)
    stepb_acc = jnp.zeros(step_bias.shape, jnp.float32)
    decay_acc = jnp.zeros(decay_log.shape, jnp.float32)
    skip_acc = jnp.zeros(skip_weight.shape, jnp.float32)
    result_rows = []
    grad_rows = []
    for batch_index in range(MB):
        full_inner, full_gain, full_output = (
            lax.all_gather(inner_weight, "dp", axis=0, tiled=True),
            lax.all_gather(norm_gain, "dp", axis=0, tiled=True),
            lax.all_gather(output_weight, "dp", axis=1, tiled=True),
        )
        first_row = batch_index * batch_rows
        inputs = owned_tokens[first_row : first_row + batch_rows].astype(jnp.float32)
        upstream = owned_cotangent[first_row : first_row + batch_rows]
        position = position_table[batch_index]
        keep_mask = (position > 0).astype(jnp.float32)
        gain_float = full_gain.astype(jnp.float32)
        square_mean = jnp.mean(inputs * inputs, axis=1, keepdims=True)
        inverse_rms = lax.rsqrt(square_mean + EPSILON)
        normed_hat = inputs * inverse_rms
        normed = (normed_hat * gain_float[None, :]).astype(jnp.bfloat16)
        projected = jnp.einsum(
            "rd,dce->rce", normed, full_inner, preferred_element_type=jnp.float32
        )
        stream = projected[:, 0]
        gate_in = projected[:, 1]
        activated, conv_pull = jax.vjp(
            partial(conv_silu, position=position), stream, filter_weight, convolution_bias
        )
        activated_low = activated.astype(jnp.bfloat16)
        selected = lax.psum(
            jnp.dot(activated_low, select_weight, preferred_element_type=jnp.float32), "tensor"
        )
        rate_low = selected[:, :rank_width].astype(jnp.bfloat16)
        step_pre = (
            jnp.dot(rate_low, step_weight, preferred_element_type=jnp.float32) + step_bias[None, :]
        )
        gated, mix_pull = jax.vjp(
            partial(mixer_scan, keep_mask=keep_mask),
            activated,
            gate_in,
            step_pre,
            selected[:, rank_width : rank_width + state_width],
            selected[:, rank_width + state_width :],
            decay_log,
            skip_weight,
        )
        gated_low = gated.astype(jnp.bfloat16)
        branch = lax.psum(
            jnp.dot(gated_low, full_output, preferred_element_type=jnp.float32), "tensor"
        )
        result_rows.append((inputs + branch).astype(jnp.bfloat16))
        output_acc = output_acc + jnp.einsum(
            "re,rd->ed", gated_low, upstream, preferred_element_type=jnp.float32
        )
        gated_grad = jnp.einsum(
            "rd,ed->re", upstream, full_output, preferred_element_type=jnp.float32
        )
        act_scan_grad, gate_grad, step_grad, in_grad, out_grad, decay_grad, skip_grad = mix_pull(
            gated_grad
        )
        decay_acc = decay_acc + decay_grad
        skip_acc = skip_acc + skip_grad
        stepb_acc = stepb_acc + jnp.sum(step_grad, axis=0)
        step_grad_low = step_grad.astype(jnp.bfloat16)
        rank_grad = jnp.einsum(
            "re,ke->rk", step_grad_low, step_weight, preferred_element_type=jnp.float32
        )
        stepw_acc = stepw_acc + jnp.einsum(
            "rk,re->ke", rate_low, step_grad_low, preferred_element_type=jnp.float32
        )
        selected_grad = lax.psum(jnp.concatenate([rank_grad, in_grad, out_grad], axis=1), "tensor")
        selected_reduced = selected_grad.astype(jnp.bfloat16)
        activated_grad = act_scan_grad + jnp.einsum(
            "rk,ek->re", selected_reduced, select_weight, preferred_element_type=jnp.float32
        )
        select_acc = select_acc + jnp.einsum(
            "re,rk->ek", activated_low, selected_reduced, preferred_element_type=jnp.float32
        )
        stream_grad, filter_grad, fbias_grad = conv_pull(activated_grad)
        filter_acc = filter_acc + filter_grad
        fbias_acc = fbias_acc + fbias_grad
        projected_grad = jnp.stack([stream_grad, gate_grad], axis=1).astype(jnp.bfloat16)
        normed_grad = lax.psum(
            jnp.einsum(
                "rce,dce->rd", projected_grad, full_inner, preferred_element_type=jnp.float32
            ),
            "tensor",
        )

        def inner_term(start_row, row_count, normed=normed, projected_grad=projected_grad):
            return jnp.einsum(
                "rd,rce->dce", normed, projected_grad, preferred_element_type=jnp.float32
            )

        inner_acc = inner_acc + lax.psum_scatter(
            inner_term(jnp.int32(0), lax.axis_size("dp") * inner_weight.shape[0]),
            "dp",
            scatter_dimension=0,
            tiled=True,
        )
        gain_acc = gain_acc + jnp.sum(normed_grad * normed_hat, axis=0)
        hat_grad = normed_grad * gain_float[None, :]
        input_part = inverse_rms * (
            hat_grad - normed_hat * jnp.mean(hat_grad * normed_hat, axis=1, keepdims=True)
        )
        grad_rows.append(upstream.astype(jnp.float32) + input_part)
    output_part, gain_part = (
        lax.psum_scatter(output_acc, "dp", scatter_dimension=1, tiled=True),
        lax.psum_scatter(gain_acc, "dp", scatter_dimension=0, tiled=True),
    )
    small_sums = lax.psum(
        (filter_acc, fbias_acc, select_acc, stepw_acc, stepb_acc, decay_acc, skip_acc), "dp"
    )
    owned_output_rows = jnp.concatenate(result_rows, axis=0).astype(jnp.float32)
    owned_grad = jnp.concatenate(grad_rows, axis=0)
    leaving = (
        owned_output_rows[arrived_slots].reshape(devices, share_rows, width),
        owned_grad[arrived_slots].reshape(devices, share_rows, width),
    )
    returned = (
        lax.all_to_all(leaving[0], "dp", split_axis=0, concat_axis=0, tiled=True),
        lax.all_to_all(leaving[1], "dp", split_axis=0, concat_axis=0, tiled=True),
    )
    undo_order = jnp.argsort(send_order)
    output = returned[0].reshape(-1, width)[undo_order].astype(jnp.bfloat16)
    input_grad = returned[1].reshape(-1, width)[undo_order]
    return (
        output,
        input_grad,
        gain_part,
        inner_acc,
        small_sums[0],
        small_sums[1],
        small_sums[2],
        small_sums[3],
        small_sums[4],
        small_sums[5],
        small_sums[6],
        output_part,
    )


def solution(mesh):
    in_specs = (
        P("dp", None),
        P("dp", None),
        P(),
        P("dp", None),
        P("dp"),
        P("dp", None, "tensor"),
        P(None, "tensor"),
        P("tensor"),
        P("tensor", None),
        P(None, "tensor"),
        P("tensor"),
        P(None, "tensor"),
        P("tensor"),
        P("tensor", "dp"),
    )
    out_specs = (
        P("dp", None),
        P("dp", None),
        P("dp"),
        P("dp", None, "tensor"),
        P(None, "tensor"),
        P("tensor"),
        P("tensor", None),
        P(None, "tensor"),
        P("tensor"),
        P(None, "tensor"),
        P("tensor"),
        P("tensor", "dp"),
    )
    return jax.shard_map(body, mesh=mesh, in_specs=in_specs, out_specs=out_specs, check_vma=False)
```

profile of v0, /device:TPU:0, one launch (start us, length us, event | category | flops | bytes accessed | tf_op | source)
XLA Modules:
  0.0 1715.5 jit_solution(6533566420203053050)
XLA Ops:
  20.0 7.4 all-to-all-start.2
  29.1 29.4 %all-gather = bf16[16,1,128]{2,1,0:T(2,128)(2,1)S(1)} all-gather(bf16[1,1,128]{2,1,0:T(2,128)(2,1)S(1)} %bitcast.559), channel_id=1, replica_groups=mesh['dp'=16,'tensor'=2] {'dp'}, dimensions={0}, use_global_device_ids=true | all-gather | bytes 4352 | tf_op jit(solution)/shard_map/all_gather | solution.py:132
  60.5 8.4 all-to-all-start
  75.3 16.6 all-to-all-done
  93.1 19.4 %all-gather.6.cloned.1.call-done = bf16[2048,2048]{1,0:T(8,128)(2,1)} async-done(((bf16[2048,128]{1,0:T(8,128)(2,1)}), bf16[2048,2048]{1,0:T(8,128)(2,1)}) %all-gather.6.cloned.1.call-update) | async-done | bytes 8388624 | tf_op jit(solution)/shard_map/all_gather | solution.py:133
  122.9 119.8 %all-gather.4.cloned.1.call-done = bf16[2048,2,2048]{2,0,1:T(8,128)(2,1)} async-done(((bf16[128,2,2048]{2,0,1:T(8,128)(2,1)}), bf16[2048,2,2048]{2,0,1:T(8,128)(2,1)}) %all-gather.4.cloned.1.call-update) | async-done | bytes 16777232 | tf_op jit(solution)/shard_map/all_gather | solution.py:131
  242.6 9.0 fusion.169
  267.0 18.3 %all-reduce.37.cloned.1.call-done = (f32[64,160]{1,0:T(8,128)}, f32[64,160]{1,0:T(8,128)}) async-done(((f32[64,160]{1,0:T(8,128)}, f32[64,160]{1,0:T(8,128)}), (f32[64,160]{1,0:T(8,128)}, f32[64,160]{1,0:T(8,128)})) %all-reduce.37.cloned.1.call-update) | async-done | bytes 81936 | tf_op jit(solution)/shard_map/psum | solution.py:154
  294.3 64.4 %while.83 = (s32[]{:T(128)}, f32[16,2048]{1,0:T(8,128)S(1)}, f32[8,8,2048]{2,1,0:T(8,128)}, f32[8,16,2048]{2,1,0:T(8,128)}, f32[8,8,16]{2,1,0:T(8,128)}, /*index...) while((s32[]{:T(128)}, f32[16,2048]{1,0:T(8,128)S(1)}, ...), condition=%wide.region_19.21_spmd.clone, body=%wide.region_15.20_spmd.clone.sunk | while | flops 13893906 | bytes 9834009 | solution.py:68
  361.6 183.4 %while.85 = (s32[]{:T(128)}, f32[16,2048]{1,0:T(8,128)}, f32[16,2048]{1,0:T(8,128)S(1)}, f32[8,8,2048]{2,1,0:T(8,128)}, f32[8,8,2048]{2,1,0:T(8,128)}, /*index=5...) while((s32[]{:T(128)}, f32[16,2048]{1,0:T(8,128)}, ...), condition=%wide.region_50.52_spmd.clone, body=%wide.region_38.51_spmd.clone.sunk | while | flops 55869456 | bytes 28654568 | solution.py:68
  553.4 64.5 %while.82 = (s32[]{:T(128)}, f32[16,2048]{1,0:T(8,128)S(1)}, f32[8,8,2048]{2,1,0:T(8,128)}, f32[8,16,2048]{2,1,0:T(8,128)}, f32[8,8,16]{2,1,0:T(8,128)}, /*index...) while((s32[]{:T(128)}, f32[16,2048]{1,0:T(8,128)S(1)}, ...), condition=%wide.region_11.13_spmd.clone, body=%wide.region_7.12_spmd.clone.sunk | while | flops 13893906 | bytes 9834009 | solution.py:68
  620.8 239.6 %while.84 = (s32[]{:T(128)}, f32[16,2048]{1,0:T(8,128)}, f32[16,2048]{1,0:T(8,128)S(1)}, f32[8,8,2048]{2,1,0:T(8,128)}, f32[8,8,2048]{2,1,0:T(8,128)}, /*index=5...) while((s32[]{:T(128)}, f32[16,2048]{1,0:T(8,128)}, ...), condition=%wide.region_34.36_spmd.clone, body=%wide.region_22.35_spmd.clone.sunk | while | flops 55869456 | bytes 39140356 | solution.py:68
  867.2 9.7 all-reduce.25
  891.3 11.8 convolution_bitcast_fusion
  903.1 12.2 convolution_bitcast_fusion.1
  917.9 13.9 fusion.151
  931.8 48.7 %all-reduce.39.cloned.1.call-done = (f32[64,2048]{1,0:T(8,128)}, f32[64,2048]{1,0:T(8,128)}, f32[64,2048]{1,0:T(8,128)}, f32[64,2048]{1,0:T(8,128)}) async-done(((f32[64,2048]{1,0:T(8,128)}, f32[64,2048]{1,0:T(8,128)}, f32[64,2048]{1,0:T(8,128)}, f32[64,2048]{1,0:T(8,128)}), (f32[64,2048]{1,0:T(8,128)}, f32[64,2048]{1,0:T(8,128)}, f32[64,2048]{1,0:T(8,128)}, ...) | async-done | bytes 2097168 | tf_op jit(solution)/shard_map/psum | solution.py:172
  983.4 21.4 %convolution_add_fusion = f32[2048,2,2048]{2,0,1:T(8,128)} fusion(f32[2048,2,2048]{2,0,1:T(8,128)} %fusion.151, bf16[64,1,2048]{2,0,1:T(8,128)(2,1)S(1)} %copy-done.29, bf16[64,1,2048]{2,0,1:T(8,128)(2,1)S(1)} %get-tuple-element.1315, f32[64]{0:T(128)S(1)} %copy-done.70, f32[2048]{0:T(1024)S(1)} %bitcast.527, bf16[128,2048]{1,0:T(8,128)(2,1)S(1)} %copy-done.10), kind=kOutput, calls=%fused_computation.179 | convolution fusion | flops 1083703296 | bytes 67904000 | tf_op jit(solution)/shard_map/rd,rce->dce/dot_general | solution.py:215
  1015.4 8.1 convolution_add_fusion.1
  1036.1 12.6 all-to-all-done.1
  1056.6 17.8 %all-reduce.33.cloned.1.call-done = (f32[2048]{0:T(1024)}, f32[4,2048]{1,0:T(4,128)}, f32[2048]{0:T(1024)}, f32[2048]{0:T(1024)}, f32[2048]{0:T(1024)}) async-done(((f32[2048]{0:T(1024)}, f32[4,2048]{1,0:T(4,128)}, f32[2048]{0:T(1024)}, f32[2048]{0:T(1024)}, f32[2048]{0:T(1024)}), (f32[2048]{0:T(1024)}, f32[4,2048]{1,0:T(4,128)}, f32[2048]{0:T(1024)}, f32[2048]{0:T(1024)}, ...) | async-done | bytes 65552
  1079.3 333.8 %reduce-scatter.5.cloned.1.call-done = f32[128,2,2048]{2,0,1:T(8,128)} async-done(((f32[2048,2,2048]{2,0,1:T(8,128)}), f32[128,2,2048]{2,0,1:T(8,128)}) %reduce-scatter.5.cloned.1.call-update) | async-done | bytes 2097168 | tf_op jit(solution)/shard_map/reduce_scatter | solution.py:219
  1417.6 100.2 %all-reduce.35.cloned.1.call-done = (f32[2048,160]{0,1:T(8,128)}, f32[128,2048]{1,0:T(8,128)}, f32[16,2048]{1,0:T(8,128)}) async-done(((f32[2048,160]{0,1:T(8,128)}, f32[128,2048]{1,0:T(8,128)}, f32[16,2048]{1,0:T(8,128)}), (f32[2048,160]{0,1:T(8,128)}, f32[128,2048]{1,0:T(8,128)}, f32[16,2048]{1,0:T(8,128)})) %all-reduce.35.cloned.1.call-update) | async-done | bytes 2490384 | tf_op jit(solution)/shard_map/psum | solution.py:235
  1517.8 181.6 %reduce-scatter.3.cloned.1.call-done = f32[2048,128]{1,0:T(8,128)} async-done(((f32[2048,2048]{1,0:T(8,128)}), f32[2048,128]{1,0:T(8,128)}) %reduce-scatter.3.cloned.1.call-update) | async-done | bytes 1048592 | tf_op jit(solution)/shard_map/reduce_scatter | solution.py:232
  (1023 shorter events, 695.7 us)
Async XLA Ops:
  8.0 251.0 %copy-start = (bf16[2048,160]{0,1:T(8,128)(2,1)S(1)}, bf16[2048,160]{0,1:T(8,128)(2,1)}, u32[]{:S(2)}) copy-start(bf16[2048,160]{0,1:T(8,128)(2,1)} %param.31) | copy-start | bytes 1966084
  10.2 102.3 %all-gather.6.cloned.1.call-start = ((), (), s32[]{:S(2)}) async-start(), calls=%async_computation.7 | async-start | bytes 8912896 | tf_op jit(solution)/shard_map/all_gather | solution.py:133
  10.7 231.9 %all-gather.4.cloned.1.call-start = ((), (), s32[]{:S(2)}) async-start(), calls=%async_computation.6 | async-start | bytes 17825792 | tf_op jit(solution)/shard_map/all_gather | solution.py:131
  20.0 40.5 %all-to-all-start.2 = ((bf16[16,8,2048]{2,1,0:T(8,128)(2,1)}), bf16[16,8,2048]{2,1,0:T(8,128)(2,1)S(1)}, u32[]{:S(2)}, u32[]{:S(2)}) async-start(bf16[16,8,2048]{2,1,0:T(8,128)(2,1)} %bitcast.49), calls=%async_computation.2 | async-start | bytes 1048576 | tf_op jit(solution)/shard_map/all_to_all | solution.py:105
  58.9 201.1 %copy-start.76 = (pred[64]{0:T(512)(128)(4,1)}, pred[64]{0:T(512)(128)(4,1)S(1)}, u32[]{:S(2)}) copy-start(pred[64]{0:T(512)(128)(4,1)S(1)} %get-tuple-element.1318) | copy-start | bytes 196
  58.9 201.1 %copy-start.80 = (pred[64]{0:T(512)(128)(4,1)}, pred[64]{0:T(512)(128)(4,1)S(1)}, u32[]{:S(2)}) copy-start(pred[64]{0:T(512)(128)(4,1)S(1)} %get-tuple-element.1319) | copy-start | bytes 196
  58.9 201.1 %copy-start.82 = (pred[64]{0:T(512)(128)(4,1)}, pred[64]{0:T(512)(128)(4,1)S(1)}, u32[]{:S(2)}) copy-start(pred[64]{0:T(512)(128)(4,1)S(1)} %get-tuple-element.1320) | copy-start | bytes 196
  59.0 201.1 %copy-start.84 = (pred[64]{0:T(512)(128)(4,1)}, pred[64]{0:T(512)(128)(4,1)S(1)}, u32[]{:S(2)}) copy-start(pred[64]{0:T(512)(128)(4,1)S(1)} %get-tuple-element.1324) | copy-start | bytes 196
  60.4 199.7 %copy-start.45 = (f32[1,2048]{1,0:T(1,128)}, f32[1,2048]{1,0:T(1,128)S(1)}, u32[]{:S(2)}) copy-start(f32[1,2048]{1,0:T(1,128)S(1)} %get-tuple-element.1311) | copy-start | bytes 24580
  60.4 199.7 %copy-start.47 = (f32[1,2048]{1,0:T(1,128)}, f32[1,2048]{1,0:T(1,128)S(1)}, u32[]{:S(2)}) copy-start(f32[1,2048]{1,0:T(1,128)S(1)} %get-tuple-element.1313) | copy-start | bytes 24580
  60.5 31.4 %all-to-all-start = ((bf16[16,8,2048]{2,1,0:T(8,128)(2,1)}), bf16[16,8,2048]{2,1,0:T(8,128)(2,1)S(1)}, u32[]{:S(2)}, u32[]{:S(2)}) async-start(bf16[16,8,2048]{2,1,0:T(8,128)(2,1)} %bitcast.12), calls=%async_computation | async-start | bytes 1048576 | tf_op jit(solution)/shard_map/all_to_all | solution.py:104
  68.9 216.5 %all-reduce.37.cloned.1.call-start = ((), (), s32[]{:S(2)}) async-start(), calls=%async_computation.12 | async-start | bytes 262144 | tf_op jit(solution)/shard_map/psum | solution.py:154
  265.5 715.1 %all-reduce.39.cloned.1.call-start = ((), (), s32[]{:S(2)}) async-start(), calls=%async_computation.13 | async-start | bytes 4194304 | tf_op jit(solution)/shard_map/psum | solution.py:172
  915.4 159.0 %all-reduce.33.cloned.1.call-start = ((), (), s32[]{:S(2)}) async-start(), calls=%async_computation.10 | async-start | bytes 131072
  983.3 429.8 %reduce-scatter.5.cloned.1.call-start = ((), (), s32[]{:S(2)}) async-start(), calls=%async_computation.9 | async-start | bytes 35651584 | tf_op jit(solution)/shard_map/reduce_scatter | solution.py:219
  1004.8 513.0 %all-reduce.35.cloned.1.call-start = ((), (), s32[]{:S(2)}) async-start(), calls=%async_computation.11 | async-start | bytes 4980736 | tf_op jit(solution)/shard_map/psum | solution.py:235
  1012.9 686.4 %reduce-scatter.3.cloned.1.call-start = ((), (), s32[]{:S(2)}) async-start(), calls=%async_computation.8 | async-start | bytes 17825792 | tf_op jit(solution)/shard_map/reduce_scatter | solution.py:232
  1028.1 20.5 %all-to-all-start.1 = ((bf16[16,8,2048]{2,1,0:T(8,128)(2,1)}), bf16[16,8,2048]{2,1,0:T(8,128)(2,1)S(1)}, u32[]{:S(2)}, u32[]{:S(2)}) async-start(bf16[16,8,2048]{2,1,0:T(8,128)(2,1)} %bitcast.47), calls=%async_computation.1 | async-start | bytes 1048576 | tf_op jit(solution)/shard_map/all_to_all | solution.py:245
  1048.6 28.7 %all-to-all-start.3 = ((f32[16,8,2048]{2,1,0:T(8,128)}), f32[16,8,2048]{2,1,0:T(8,128)S(1)}, u32[]{:S(2)}, u32[]{:S(2)}) async-start(f32[16,8,2048]{2,1,0:T(8,128)} %bitcast.67), calls=%async_computation.3 | async-start | bytes 2097152 | tf_op jit(solution)/shard_map/all_to_all | solution.py:246
  1075.7 623.7 %copy-start.68 = (f32[4,2048]{1,0:T(4,128)S(1)}, f32[4,2048]{1,0:T(4,128)}, u32[]{:S(2)}) copy-start(f32[4,2048]{1,0:T(4,128)} %get-tuple-element.1943) | copy-start | bytes 98308
  1075.7 624.3 %copy-start.75 = (f32[2048]{0:T(1024)S(1)}, f32[2048]{0:T(1024)}, u32[]{:S(2)}) copy-start(f32[2048]{0:T(1024)} %get-tuple-element.1944) | copy-start | bytes 24580
  1077.4 630.8 %copy-start.1 = (bf16[2048,160]{0,1:T(8,128)(2,1)S(1)}, bf16[2048,160]{0,1:T(8,128)(2,1)}, u32[]{:S(2)}) copy-start(bf16[2048,160]{0,1:T(8,128)(2,1)} %param.31) | copy-start | bytes 1966084
  1077.4 628.0 %copy-start.74 = (f32[2048]{0:T(1024)S(1)}, f32[2048]{0:T(1024)}, u32[]{:S(2)}) copy-start(f32[2048]{0:T(1024)} %get-tuple-element.1947) | copy-start | bytes 24580
  1077.4 630.2 %copy-start.73 = (f32[2048]{0:T(1024)S(1)}, f32[2048]{0:T(1024)}, u32[]{:S(2)}) copy-start(f32[2048]{0:T(1024)} %get-tuple-element.1949) | copy-start | bytes 24580
  (110 other events, 3141.7 us)
Sparse Core Ops, SparseCore 0:
  12.3 2.0 sort.72.cloned.1.call-done
  265.6 19.7 all-reduce.36
  915.5 65.0 all-reduce.38
  (1 shorter events, 0.0 us)
Sparse Core Ops, SparseCore 1:
  13.0 99.3 all-gather.5
  115.3 127.3 all-gather.3
  983.4 90.9 all-reduce.32
  1079.3 333.8 reduce-scatter.4
  1418.6 99.1 all-reduce.34
  1523.1 176.2 reduce-scatter.2
where the time goes:
time: 1730 us; the launch traced here: 1720 us
  waiting for transfers between devices  869 us (50%)
  other arithmetic  431 us (25%)
  local copies, waits for them, and re-layouts  215 us (12%)
  matrix products  114 us (7%)
  blocking collectives  39.1 us (2%)
  starting transfers between devices  26.8 us (2%)
  between operations  17.3 us (1%)
    reduce_scatter x1, waiting for transfers between devices, body(): lax.psum_scatter(inner_term(jnp.int32(0), lax.axis_size('dp') * inner_wei...  334 us
    reduce_scatter x1, waiting for transfers between devices, body(): lax.psum_scatter(output_acc, 'dp', scatter_dimension=1, tiled=True)  182 us
    all_gather x1, waiting for transfers between devices, body(): lax.all_gather(inner_weight, 'dp', axis=0, tiled=True)  120 us
    psum x1, waiting for transfers between devices, body(): lax.psum((filter_acc, fbias_acc, select_acc, stepw_acc, stepb_acc, decay_...  100 us
    dot_general x32, other arithmetic, advance(): hidden_states = jnp.einsum('lhyj,hyj->lyj', weight_table, incoming_rows)  83.9 us
    reduce_sum x16, other arithmetic, advance(): spread = jnp.minimum(running[:, None] - running[None, :], 0.0)  80.9 us
    squeeze x96, local copies, waits for them, and re-layouts, mixer_scan(): _, scan_result = lax.scan(jax.checkpoint(advance), initial, pieces)  77.8 us
    while x32, other arithmetic  66.7 us
  transfers between devices with their start and end apart: 12, of which 10 were waited for; matrix products, arithmetic and copies ran while one was open for 6% of the time, Pallas kernels for 0%

commit v1 on v0

v1 whole, which is shorter than its diff:
```python
from functools import partial

import jax
import jax.numpy as jnp
from jax import lax
from jax.experimental import pallas as pl
from jax.experimental.pallas import tpu as pltpu
from jax.sharding import Mesh, PartitionSpec as P

MB = 2
EPSILON = 1e-05
ZK = ("z", "k")
DP = ("r", "z", "x", "k")
SWAP = [(0, 1), (1, 0)]
LOG2E = 1.4426950408889634
RESET_RATE = 1e30
LANES = 128
SUBLANES = 8
F32 = jnp.float32
BF16 = jnp.bfloat16
NT = ((1,), (1,))
TN = ((0,), (0,))


def dot(lhs, rhs, contract=((1,), (0,))):
    return lax.dot_general(lhs, rhs, (contract, ((), ())), preferred_element_type=F32)


def split_dot(lhs, rhs, contract=((1,), (0,))):
    high = lhs.astype(BF16)
    rest = (lhs - high.astype(F32)).astype(BF16)
    return dot(high, rhs, contract) + dot(rest, rhs, contract)


def shape(dims, dtype):
    return jax.ShapeDtypeStruct(dims, dtype)


def whole(kernel, name, scalars, arrays, outs, scratch=(), flops=0):
    scalars = [jnp.reshape(v, (1,)).astype(jnp.int32) for v in scalars]
    size = sum(v.size * v.dtype.itemsize for v in (*arrays, *outs))
    few, many = len(scalars), len(arrays)

    def copied(*refs):
        inputs, rest = refs[few : few + many], refs[few + many : -many - 1]
        held, semaphores = refs[-many - 1 : -1], refs[-1]
        copies = [
            pltpu.make_async_copy(source, target, semaphores.at[i])
            for i, (source, target) in enumerate(zip(inputs, held))
        ]
        for copy in copies:
            copy.start()
        for copy in copies:
            copy.wait()
        kernel(*refs[:few], *held, *rest)

    return pl.pallas_call(
        copied,
        in_specs=[pl.BlockSpec(memory_space=pltpu.SMEM)] * few
        + [pl.BlockSpec(memory_space=pl.ANY)] * many,
        out_specs=[pl.BlockSpec(memory_space=pltpu.VMEM)] * len(outs),
        out_shape=list(outs),
        scratch_shapes=[
            *scratch,
            *(pltpu.VMEM(v.shape, v.dtype) for v in arrays),
            pltpu.SemaphoreType.DMA((many,)),
        ],
        compiler_params=pltpu.CompilerParams(vmem_limit_bytes=40 << 20),
        cost_estimate=pl.CostEstimate(flops=flops, bytes_accessed=size, transcendentals=0),
        name=name,
    )(*scalars, *arrays)


def row_matches(places, count):
    rows = lax.broadcasted_iota(jnp.int32, (count, places.shape[1]), 0)
    return (rows == places).astype(F32).astype(BF16)


def column_matches(places, count):
    columns = lax.broadcasted_iota(jnp.int32, (places.shape[0], count), 1)
    return (columns == places).astype(F32).astype(BF16)


def tiles(count, size):
    return [slice(i, i + size) for i in range(0, count, size)]


def prep_kernel(x_ref, place_ref, tok_ref, cot_ref, note_ref, tok_keep, tok_send, cot_keep, cot_send):
    share = tok_keep.shape[0]
    width = tok_ref.shape[1]
    half = width // 2
    order = row_matches(place_ref[...], 2 * share)
    for source, outs in ((tok_ref, (tok_keep, tok_send)), (cot_ref, (cot_keep, cot_send))):
        rows = dot(order, source[...])
        for side in (0, 1):
            part = rows[side * share : (side + 1) * share]
            for x in (0, 1):
                same = x_ref[0] == (x ^ side)
                for zk in range(half // LANES):
                    place = (zk // 2) * 4 + zk % 2
                    zero = part[:, place * LANES : (place + 1) * LANES]
                    one = part[:, (place + 2) * LANES : (place + 3) * LANES]
                    to = slice(x * half + zk * LANES, x * half + (zk + 1) * LANES)
                    outs[side][:, to] = jnp.where(same, zero, one).astype(BF16)
    tok_keep[:, width:] = note_ref[...]
    tok_send[:, width:] = note_ref[...]


def place_rows(x_ref, place_ref, near_ref, far_ref):
    share = near_ref.shape[0] // 2
    width = near_ref.shape[1]
    half = width // 2
    order = column_matches(place_ref[...], 4 * share)
    total = None
    for group in range(4):
        source = (near_ref, far_ref)[group // 2]
        rows = slice((group % 2) * share, (group % 2 + 1) * share)
        blocks = []
        for block in range(width // LANES):
            z, x, k = block // 4, (block // 2) % 2, block % 2
            same = x_ref[0] == (x ^ (group % 2))
            at = (z * 2 + k) * LANES
            first = source[rows, at : at + LANES].astype(F32)
            second = source[rows, half + at : half + at + LANES].astype(F32)
            blocks.append(jnp.where(same, first, second).astype(BF16))
        piece = dot(order[:, group * share : (group + 1) * share], jnp.concatenate(blocks, 1))
        total = piece if total is None else total + piece
    return total


def output_kernel(x_ref, place_ref, near_ref, far_ref, tok_ref, out_ref):
    rows = place_rows(x_ref, place_ref, near_ref, far_ref)
    out_ref[...] = (tok_ref[...].astype(F32) + rows).astype(BF16)


def input_kernel(x_ref, place_ref, near_ref, far_ref, tok_ref, cot_ref, gain_ref, out_ref):
    rows = place_rows(x_ref, place_ref, near_ref, far_ref)
    x = tok_ref[...].astype(F32)
    inverse = lax.rsqrt(jnp.mean(x * x, axis=1, keepdims=True) + EPSILON)
    hat = x * inverse
    half = gain_ref.shape[1] // 2
    gains = []
    for block in range(x.shape[1] // LANES):
        z, side, k = block // 4, (block // 2) % 2, block % 2
        at = (z * 2 + k) * LANES
        gains.append(
            jnp.where(
                x_ref[0] == side,
                gain_ref[0:1, at : at + LANES],
                gain_ref[0:1, half + at : half + at + LANES],
            )
        )
    grad = rows * jnp.concatenate(gains, 1)
    out_ref[...] = cot_ref[...].astype(F32) + inverse * (
        grad - hat * jnp.mean(grad * hat, axis=1, keepdims=True)
    )


def column_sum(rows_ref, pieces):
    own, by_x, by_t, *diagonal = pieces
    depth = own.shape[0]
    near, far = rows_ref[:, :depth], rows_ref[:, depth:]
    a = dot(near, own[...]) + dot(far, by_x[...])
    b = dot(near, by_t[...])
    for i, at in enumerate(tiles(depth, diagonal[0].shape[0])):
        b = b + dot(far[:, at], diagonal[i][...])
    return a, b


def z_block(z_ref, step, size):
    return lax.rem(z_ref[0] + (size - step), size)


def row_sum(z_ref, sides, out_refs):
    depth = sides[0][1][0].shape[0]
    rows = sides[0][0].shape[0] // 2
    block = 2 * LANES
    for base in range(0, 2 * depth, block):
        at = slice(base % depth, base % depth + block)
        value = None
        for lhs, (own, by_x, by_t, *diagonal) in sides:
            part = lhs.shape[1] // 2
            if base < depth:
                near, far = own[at, :], by_t[at, :]
            else:
                size = diagonal[0].shape[0]
                inner = slice(at.start % size, at.start % size + block)
                near, far = by_x[at, :], diagonal[at.start // size][inner, :]
            term = dot(lhs[:, :part], near, NT) + dot(lhs[:, part:], far, NT)
            value = term if value is None else value + term
        place = z_block(z_ref, at.start // block, depth // block) * block
        to = pl.ds(pl.multiple_of(base // depth * depth + place, block), block)
        for i, out in enumerate(out_refs):
            out[:, to] = value[i * rows : (i + 1) * rows].astype(BF16)


def reorder_rows(z_ref, order, source, out):
    block = 2 * LANES
    half = out.shape[1] // 2
    for base in range(0, 2 * half, block):
        step = base % half // block
        place = base // half * half + z_block(z_ref, step, half // block) * block
        at = pl.ds(pl.multiple_of(place, block), block)
        out[:, base : base + block] = dot(order, source[:, at]).astype(BF16)


def grad_pieces(z_ref, channels_t, rows_ref, outs):
    part = channels_t.shape[0] // 2
    depth = rows_ref.shape[1] // 2
    for at in tiles(2 * depth, 2 * LANES):
        value = dot(channels_t, rows_ref[:, at])
        near_out, far_out = (outs[0], outs[2]) if at.start < depth else (outs[1], outs[3])
        block = 2 * z_block(z_ref, (at.start % depth) // (2 * LANES), depth // (2 * LANES))
        for i in (0, 1):
            lanes = value[:, i * LANES : (i + 1) * LANES].astype(BF16)
            for refs, rows in ((near_out, lanes[:part]), (far_out, lanes[part:])):
                size = part // len(refs)
                for j, ref in enumerate(refs):
                    ref[block + i, :, :] = rows[j * size : (j + 1) * size]


def first_pack_kernel(z_ref, k_ref, stream, gate, outer, keep, send):
    count = keep.shape[0] // 3
    part = keep.shape[2]
    for i, source in enumerate((stream, gate, outer)):
        for step in range(count):
            z = lax.rem(z_ref[0] + step, count)
            for out, core in ((keep, k_ref[0]), (send, 1 - k_ref[0])):
                at = pl.ds(pl.multiple_of((z * 2 + core) * part, part), part)
                out[i * count + step] = source[:, at]


def second_pack_kernel(k_ref, kept, got, *outs):
    first = k_ref[0] == 0
    height = kept.shape[1]
    for i, out in enumerate(outs):
        mine, other = kept[i].astype(F32), got[i].astype(F32)
        out[:height, :] = jnp.where(first, mine, other).astype(BF16)
        out[height:, :] = jnp.where(first, other, mine).astype(BF16)


def down(value, count):
    if count == 0:
        return value
    return jnp.concatenate([jnp.zeros((count, value.shape[1]), value.dtype), value[:-count]], 0)


def up(value, count):
    if count == 0:
        return value
    return jnp.concatenate([value[count:], jnp.zeros((count, value.shape[1]), value.dtype)], 0)


def lag_masks(place, taps):
    return [None] + [place >= lag for lag in range(1, taps)]


def masked(value, mask):
    return value if mask is None else jnp.where(mask, value, 0.0)


def filter_sum(stream, masks, weights):
    taps = len(masks)
    total = weights[taps : taps + 1, :] + weights[taps - 1 : taps, :] * stream
    for lag in range(1, taps):
        total = total + weights[taps - 1 - lag : taps - lag, :] * masked(
            down(stream, SUBLANES * lag), masks[lag]
        )
    return total


def places(notes, rows, per_device):
    segments = len(notes) * MB
    zero = lax.broadcasted_iota(jnp.int32, (segments, LANES), 0) % MB
    lane = lax.broadcasted_iota(jnp.int32, (segments, LANES), 1)
    table = jnp.concatenate([v for v in notes for _ in range(MB)], 0)
    begin = jnp.zeros((segments, 1), F32)
    step = lax.broadcasted_iota(jnp.int32, (rows, LANES), 0) // segments
    step = step.astype(F32)
    latest = jnp.zeros((rows, LANES), F32)
    for i in range(per_device - 1):
        picked = jnp.where(lane == zero * per_device + i, table, 0.0)
        begin = begin + jnp.sum(picked, axis=1, keepdims=True)
        every = jnp.concatenate(
            [jnp.broadcast_to(begin, (segments, LANES))] * (rows // segments), 0
        )
        latest = jnp.where(every <= step, every, latest)
    return step - latest


def front_kernel(
    sizes, core_ref, tensor_ref, z_ref, x_ref, place_ref, own, by_x, by_t, low, high, par_ref, sel_ref,
    n_ref, stream_ref, act_ref, mine_ref, other_ref, pos_ref, gain_ref, nrm, act_low,
):
    taps, per_device = sizes
    rows = x_ref.shape[0]
    width = n_ref.shape[1]
    depth = width // 2
    part = own.shape[1]
    members = depth // LANES
    share = rows // (2 * members)
    note = slice(width, width + LANES)
    for side in (0, 1):
        for member in range(members):
            row = member * 2 * share + side * share
            at = side * depth + member * LANES
            gain_ref[0:1, at : at + LANES] = x_ref[row : row + 16, note].astype(F32)[0:1]
    notes = []
    for z in range(members // 2):
        two = [
            x_ref[m * 2 * share : m * 2 * share + 16, note].astype(F32)[1:2]
            for m in (2 * z, 2 * z + 1)
        ]
        notes.append(jnp.where(tensor_ref[0] == 0, two[0], two[1]))
    place = places(notes, rows, per_device)
    pos_ref[...] = place

    def norm(i, _):
        at = pl.ds(pl.multiple_of(i * 64, 64), 64)
        x = x_ref[at, :width].astype(F32)
        inverse = lax.rsqrt(jnp.mean(x * x, axis=1, keepdims=True) + EPSILON)
        nrm[at, :] = (x * inverse * gain_ref[0:1, :]).astype(BF16)
        return 0

    lax.fori_loop(0, rows // 64, norm, 0)
    reorder_rows(z_ref, row_matches(place_ref[...], rows), nrm, n_ref)
    near, far = column_sum(n_ref, (own, by_x, by_t, low, high))
    stream_ref[:, :part] = near
    stream_ref[:, part:] = far
    masks = lag_masks(place, taps)
    for at in tiles(2 * part, LANES):
        filtered = filter_sum(stream_ref[:, at], masks, par_ref[:, at])
        act = filtered * jax.nn.sigmoid(filtered)
        act_ref[:, at] = act
        act_low[:, at] = act.astype(BF16)
    selected = dot(sel_ref[...], act_low[...], NT)
    first = core_ref[0] == 0
    mine_ref[...] = jnp.where(first, selected[:, : rows // 2], selected[:, rows // 2 :])
    other_ref[...] = jnp.where(first, selected[:, rows // 2 :], selected[:, : rows // 2])


def late_kernel(z_ref, cot_ref, place_ref, n_ref, *refs):
    gate_pieces, out_pieces = refs[:4], refs[4:8]
    up_ref, gate_ref, gg_ref = refs[8:]
    part = gate_pieces[0].shape[1]
    reorder_rows(z_ref, row_matches(place_ref[...], cot_ref.shape[0]), cot_ref, up_ref)
    for source, out, pieces in ((n_ref, gate_ref, gate_pieces), (up_ref, gg_ref, out_pieces)):
        near, far = column_sum(source, pieces)
        out[:, :part] = near
        out[:, part:] = far


def out_kernel(z_ref, place_ref, gated_ref, *refs):
    order = column_matches(place_ref[...], gated_ref.shape[0])
    rows = dot(order, gated_ref[...]).astype(BF16)
    row_sum(z_ref, [(rows, refs[:4])], refs[4:])


def late_grad_kernel(z_ref, n_ref, up_ref, gate_grad_ref, gated_ref, *outs):
    for i, (source, rows_ref) in enumerate(((gate_grad_ref, n_ref), (gated_ref, up_ref))):
        grad_pieces(
            z_ref, source[...].astype(F32).T.astype(BF16), rows_ref, [[v] for v in outs[4 * i : 4 * i + 4]]
        )


def back_kernel(
    taps, core_ref, z_ref, total_ref, rest_ref, pos_ref, stream_ref, sact_ref, par_ref, sel_ref, n_ref,
    low_ref, small_ref, *refs,
):
    *outs, act_low, grad_t = refs
    rows, channels = stream_ref.shape
    first = core_ref[0] == 0
    total, rest = total_ref[...], rest_ref[...]
    selected_t = jnp.concatenate(
        [jnp.where(first, total, rest), jnp.where(first, rest, total)], 1
    )
    selected_low = selected_t.astype(BF16)
    count = selected_t.shape[0]
    padded = jnp.concatenate(
        [selected_t, jnp.zeros((-count % LANES, rows), F32)], 0
    )
    selected = padded.T.astype(BF16)
    masks = lag_masks(pos_ref[...], taps)
    spare = jnp.zeros((SUBLANES - taps - 1, LANES), F32)
    for at in tiles(channels, LANES):
        stream = stream_ref[:, at]
        weights = par_ref[:, at]
        filtered = filter_sum(stream, masks, weights)
        slope = jax.nn.sigmoid(filtered)
        act_low[:, at] = (filtered * slope).astype(BF16)
        select = jnp.concatenate(
            [sel_ref[:, at], jnp.zeros((-count % LANES, LANES), BF16)], 0
        )
        act_grad = sact_ref[:, at] + dot(selected, select)
        grad = act_grad * (slope * (1.0 + filtered * (1.0 - slope)))
        stream_grad = weights[taps - 1 : taps, :] * grad
        sums = [jnp.sum(grad * stream, axis=0, keepdims=True)]
        for lag in range(1, taps):
            part_grad = masked(grad, masks[lag])
            sums.append(
                jnp.sum(part_grad * down(stream, SUBLANES * lag), axis=0, keepdims=True)
            )
            stream_grad = stream_grad + weights[taps - 1 - lag : taps - lag, :] * up(
                part_grad, SUBLANES * lag
            )
        sums = sums[::-1] + [jnp.sum(grad, axis=0, keepdims=True), spare]
        small_ref[count:, at] = jnp.concatenate(sums, 0).astype(BF16)
        low_ref[:, at] = stream_grad.astype(BF16)
        grad_t[at, :] = stream_grad.T.astype(BF16)
    small_ref[:count, :] = dot(selected_low, act_low[...]).astype(BF16)
    grad_pieces(z_ref, grad_t[...], n_ref, [outs[2 * i : 2 * i + 2] for i in range(4)])


def in_kernel(z_ref, place_ref, low_ref, gate_grad_ref, *refs):
    stream_pieces, gate_pieces, outs, stage = refs[:5], refs[5:9], refs[9:11], refs[11]
    channels = low_ref.shape[1]
    order = column_matches(place_ref[...], low_ref.shape[0])
    stage[:, :channels] = dot(order, low_ref[...]).astype(BF16)
    stage[:, channels:] = dot(order, gate_grad_ref[...]).astype(BF16)
    row_sum(
        z_ref, [(stage[:, :channels], stream_pieces), (stage[:, channels:], gate_pieces)], outs
    )


def small_kernel(
    sizes, z_ref, k_ref, *refs,
):
    count, states, taps = sizes
    blocks = refs[:-7]
    select, step_w, decay, filters, filter_b, step_b, skip = refs[-7:]
    part = blocks[0].shape[1]
    zs = len(blocks) // 2
    rank = step_w.shape[0]
    for i, block in enumerate(blocks):
        core = k_ref[0] if i % 2 == 0 else 1 - k_ref[0]
        place = (z_block(z_ref, i // 2, zs) * 2 + core) * part
        at = pl.ds(pl.multiple_of(place, part), part)
        first = block[: states + 8, :].astype(F32)
        step_b[:, at] = first[0:1]
        skip[:, at] = first[1:2]
        decay[:, at] = first[8:]
        step_w[:, at] = block[states + 8 : states + 8 + rank, :].astype(F32)
        rest = block[states + 8 + rank :, :].astype(F32)
        filters[:, at] = rest[count : count + taps]
        filter_b[:, at] = rest[count + taps : count + taps + 1]
        chosen = jnp.concatenate([rest[:count], jnp.zeros((-count % LANES, part), F32)], 0)
        select[at, :] = chosen.T[:, :count]


def scan_kernel(
    layout, core_ref, pos_ref, act_ref, gate_ref, gg_ref, total_ref, rest_ref, sw_ref, par_ref,
    gated_ref, gateg_ref, sact_ref, small_ref, mine_ref, other_ref,
    bb, cb, hist, fac, ci_acc, co_acc, rate_s, reff_s, u_s, ds_s, y_s, s2_s, decb, sel_t, rate_low, rank_t,
):
    rank_width, states, bias_row, decay_row, skip_row = layout
    rows, lanes = act_ref.shape
    steps = rows // SUBLANES
    block = pl.program_id(0)
    wide = states * lanes
    first = core_ref[0] == 0
    spread = (
        lax.broadcasted_iota(jnp.int32, (states, wide), 1) // lanes
        == lax.broadcasted_iota(jnp.int32, (states, wide), 0)
    ).astype(F32).astype(BF16)

    @pl.when(block == 0)
    def _():
        total, rest = total_ref[...], rest_ref[...]
        sel_t[:, : rows // 2] = jnp.where(first, total, rest)
        sel_t[:, rows // 2 :] = jnp.where(first, rest, total)
        rate_low[...] = sel_t[:rank_width, :].T.astype(BF16)
        bb[...] = split_dot(sel_t[rank_width : rank_width + states, :], spread, TN)
        cb[...] = split_dot(sel_t[rank_width + states :, :], spread, TN)
        hist[0:SUBLANES, :] = jnp.zeros((SUBLANES, wide), F32)
        ci_acc[...] = jnp.zeros_like(ci_acc)
        co_acc[...] = jnp.zeros_like(co_acc)
        rank_t[...] = jnp.zeros_like(rank_t)

    decay = -jnp.exp(par_ref[decay_row : decay_row + states, :])
    for n in range(states):
        decb[8 * n : 8 * n + 8, :] = jnp.broadcast_to(decay[n : n + 1, :], (8, lanes))

    step_pre = dot(rate_low[...], sw_ref[...]) + par_ref[bias_row : bias_row + 1, :]
    step_slope = jax.nn.sigmoid(step_pre)
    rate = jnp.maximum(step_pre, 0.0) + jnp.log1p(jnp.exp(-jnp.abs(step_pre)))
    rate_s[...] = rate
    reff_s[...] = jnp.where(pos_ref[...] > 0.0, rate * LOG2E, RESET_RATE)
    u_s[...] = rate * act_ref[...]
    gate = gate_ref[...]
    ds_s[...] = gg_ref[...] * (gate * jax.nn.sigmoid(gate))

    def cols(n):
        return slice(n * lanes, (n + 1) * lanes)

    def forward(t, h):
        row = pl.ds(pl.multiple_of(t * 8, 8), 8)
        next_row = pl.ds(pl.multiple_of(t * 8 + 8, 8), 8)
        reff = reff_s[row, :]
        u = u_s[row, :]
        y = jnp.zeros((8, lanes), F32)
        fresh = []
        for n in range(states):
            a = jnp.exp2(reff * decb[8 * n : 8 * n + 8, :])
            hn = a * h[n] + bb[row, cols(n)] * u
            hist[next_row, cols(n)] = hn
            fac[row, cols(n)] = a
            y = y + cb[row, cols(n)] * hn
            fresh.append(hn)
        y_s[row, :] = y
        return tuple(fresh)

    zero = jnp.zeros((8, lanes), F32)
    lax.fori_loop(0, steps, forward, (zero,) * states)

    def backward(i, carried):
        g, dacc = carried
        t = steps - 1 - i
        row = pl.ds(pl.multiple_of(t * 8, 8), 8)
        next_row = pl.ds(pl.multiple_of(t * 8 + 8, 8), 8)
        ds = ds_s[row, :]
        u = u_s[row, :]
        rt = rate_s[row, :]
        s1 = jnp.zeros((8, lanes), F32)
        s2 = jnp.zeros((8, lanes), F32)
        g_new, d_new = [], []
        for n in range(states):
            lam = cb[row, cols(n)] * ds + g[n]
            q = lam * fac[row, cols(n)]
            hp = hist[row, cols(n)] * q
            s1 = s1 + hp * decb[8 * n : 8 * n + 8, :]
            s2 = s2 + lam * bb[row, cols(n)]
            ci_acc[row, cols(n)] += lam * u
            co_acc[row, cols(n)] += ds * hist[next_row, cols(n)]
            g_new.append(q)
            d_new.append(dacc[n] + hp * rt)
        s2_s[row, :] = s2
        reff_s[row, :] = s1
        return tuple(g_new), tuple(d_new)

    _, dacc = lax.fori_loop(0, steps, backward, ((zero,) * states, (zero,) * states))

    act = act_ref[...]
    skip = par_ref[skip_row : skip_row + 1, :]
    scanned = y_s[...] + skip * act
    sig = jax.nn.sigmoid(gate)
    gated_ref[...] = (scanned * (gate * sig)).astype(BF16)
    gateg_ref[...] = (gg_ref[...] * scanned * (sig * (1.0 + gate * (1.0 - sig)))).astype(BF16)
    s2_all = s2_s[...]
    dscan = ds_s[...]
    sact_ref[...] = rate_s[...] * s2_all + skip * dscan
    spre = (reff_s[...] + act * s2_all) * step_slope
    spre_low = spre.astype(BF16)
    sums = [jnp.sum(spre, axis=0, keepdims=True), jnp.sum(dscan * act, axis=0, keepdims=True)]
    sums.append(jnp.zeros((6, lanes), F32))
    for n in range(states):
        sums.append(jnp.sum(dacc[n], axis=0, keepdims=True) * decb[8 * n : 8 * n + 1, :])
    small_ref[: states + 8, :] = jnp.concatenate(sums, 0).astype(BF16)
    small_ref[states + 8 :, :] = dot(
        sel_t[:rank_width, :].astype(BF16), spre_low
    ).astype(BF16)
    rank_t[...] += dot(sw_ref[...], spre_low, NT)

    @pl.when(block == pl.num_programs(0) - 1)
    def _():
        high, low = slice(0, rows // 2), slice(rows // 2, rows)
        for acc, base in ((ci_acc, rank_width), (co_acc, rank_width + states)):
            sums_t = split_dot(acc[...], spread, NT).T
            sel_t[base : base + states, :] = sums_t
        sel_t[:rank_width, :] = rank_t[...]
        mine_ref[...] = jnp.where(first, sel_t[:, high], sel_t[:, low])
        other_ref[...] = jnp.where(first, sel_t[:, low], sel_t[:, high])


def mixer(layout, core, position, act, gate, gated_grad, total, rest, step_w, params):
    rows, channels = act.shape
    rank_width, states = layout[:2]
    lanes = LANES
    count = total.shape[0]

    def block(height):
        return pl.BlockSpec((height, lanes), lambda i: (0, i))

    def fixed(*dims):
        return pl.BlockSpec(dims, lambda i: (0, 0))

    tall = block(rows)
    wide = states * lanes
    return pl.pallas_call(
        partial(scan_kernel, layout),
        grid=(channels // lanes,),
        in_specs=[
            pl.BlockSpec(memory_space=pltpu.SMEM), fixed(rows, lanes), tall, tall, tall,
            fixed(count, rows // 2), fixed(count, rows // 2), block(rank_width),
            block(params.shape[0]),
        ],
        out_specs=[
            tall, tall, tall, block(rank_width + states + 8),
            fixed(count, rows // 2), fixed(count, rows // 2),
        ],
        out_shape=[
            shape((rows, channels), BF16), shape((rows, channels), BF16),
            shape((rows, channels), F32), shape((rank_width + states + 8, channels), BF16),
            shape((count, rows // 2), F32), shape((count, rows // 2), F32),
        ],
        scratch_shapes=[
            pltpu.VMEM((rows, wide), F32),
            pltpu.VMEM((rows, wide), F32),
            pltpu.VMEM((rows + 8, wide), F32),
            pltpu.VMEM((rows, wide), F32),
            pltpu.VMEM((rows, wide), F32),
            pltpu.VMEM((rows, wide), F32),
        ]
        + [pltpu.VMEM((rows, lanes), F32)] * 6
        + [
            pltpu.VMEM((8 * states, lanes), F32), pltpu.VMEM((count, rows), F32),
            pltpu.VMEM((rows, rank_width), BF16), pltpu.VMEM((rank_width, rows), F32),
        ],
        compiler_params=pltpu.CompilerParams(
            dimension_semantics=("arbitrary",), vmem_limit_bytes=48 << 20
        ),
        cost_estimate=pl.CostEstimate(
            flops=20 * rows * channels * states,
            bytes_accessed=30 * rows * channels,
            transcendentals=rows * channels * states,
        ),
        name="mixer",
    )(jnp.reshape(core, (1,)).astype(jnp.int32), position, act, gate, gated_grad, total, rest, step_w, params)


def after(value, *others):
    return lax.optimization_barrier((value, others))[0]


def swap(value, axis, name="swap"):
    with jax.named_scope(f"{name}_{axis}"):
        return lax.ppermute(value, axis, SWAP)


def sum_zk(mine, other, fillers=()):
    fillers = list(fillers) + [()] * 8
    total = mine + after(swap(other, "k", "select"), fillers.pop(0))
    first = None
    size = lax.axis_size("z")
    distance = 1
    while distance < size:
        sent = total.astype(BF16)
        got = lax.ppermute(sent, "z", [(i, i ^ distance) for i in range(size)])
        total = sent.astype(F32) + after(got, fillers.pop(0)).astype(F32)
        first = total if first is None else first
        distance *= 2
    return total, swap(total, "k", "select_rest"), first


def return_core(mine, other):
    return (mine.astype(F32) + swap(other, "k", "rows").astype(F32)).astype(BF16)


def return_rows(total):
    rows = lax.psum_scatter(total, "z", scatter_dimension=0, tiled=True)
    share = rows.shape[0] // 2
    near = jnp.concatenate([rows[:share], swap(rows[share:], "x", "rows")], 0)
    return near, swap(near, "t", "rows")


def exchange_halves(low, high):
    low_x, high_t = swap(low, "x", "gate_w"), swap(high, "t", "outer_w")
    low_t, high_x = swap(low, "t", "gate_w"), swap(high, "x", "outer_w")
    low_d, high_d = swap(low_x, "t", "gate_w_far"), swap(high_t, "x", "outer_w_far")
    return (low, low_x, low_t, low_d), (high, high_x, high_t, high_d)


def exchange_weight(own):
    half = own.shape[0] // 2
    by_x = swap(own, "x", "stream_w")
    by_t = swap(own, "t", "stream_w")
    low = swap(by_x[:half], "t", "stream_w_far")
    return own, by_x, by_t, low, swap(by_t[half:], "x", "stream_w_far")


def plus(value, *more):
    total = value.astype(F32)
    for v in more:
        total = total + v.astype(F32)
    return total.astype(BF16)


def diagonal_grads(low, high, name):
    return swap(low[3], "x", name + "_far"), swap(high[3], "t", name + "_far")


def first_grads(low, high, name):
    return swap(low[1], "x", name), swap(high[2], "t", name)


def second_grads(low, high, diagonal, name, ready=()):
    low_t = swap(plus(low[2], after(diagonal[0], ready)), "t", name + "_sum")
    high_x = swap(plus(high[1], after(diagonal[1], ready)), "x", name + "_sum")
    return low_t, high_x


def to_owners(value):
    return lax.all_to_all(value, ZK, 0, 0, tiled=True)


def rank_in_class(keys):
    count = keys.shape[1]
    earlier = jnp.arange(count)[:, None] > jnp.arange(count)[None, :]
    same = (keys[:, :, None] == keys[:, None, :]) & earlier[None]
    return jnp.sum(same.astype(jnp.int32), axis=2)


def body(
    tokens, cotangent, owner_slot, sequence_lengths, norm_gain, inner_weight, filter_weight,
    convolution_bias, select_weight, step_weight, step_bias, decay_log, skip_weight, output_weight,
):
    rings = lax.axis_size("r")
    zs = lax.axis_size("z")
    members = zs * 4
    ri, zi, xi, ki, ti = (lax.axis_index(a) for a in ("r", "z", "x", "k", "t"))
    local_rows, width = tokens.shape
    rank_width = step_weight.shape[0]
    states = decay_log.shape[0]
    taps = filter_weight.shape[0]
    half_channels = inner_weight.shape[2]
    part = half_channels // (2 * zs)
    channels = 2 * part
    block_rows = inner_weight.shape[0]
    ring_rows = rings * block_rows
    depth = width // 2
    batch_rows = local_rows // MB
    group_rows = zs * local_rows
    segments = group_rows // batch_rows
    share = local_rows // 4

    def to_blocks(value):
        if rings == 1:
            return value
        value = value.reshape(-1, rings, members, block_rows)
        return value.transpose(0, 2, 1, 3).reshape(-1, width)

    def from_blocks(value):
        if rings == 1:
            return value
        value = value.reshape(-1, members, rings, block_rows)
        return value.transpose(0, 2, 1, 3).reshape(-1, width)

    inner = inner_weight
    outer = output_weight.T
    gain = norm_gain[None, :]
    if rings > 1:
        inner = lax.all_gather(inner, "r", axis=0, tiled=True)
        outer = lax.all_gather(outer, "r", axis=0, tiled=True)
        gain = lax.all_gather(gain, "r", axis=1, tiled=True)

    blocks_w = 3 * zs
    kept, sent = whole(
        first_pack_kernel, "pack", [zi, ki], (inner[:, 0], inner[:, 1], outer),
        [shape((blocks_w, ring_rows, part), BF16)] * 2,
    )
    packed = whole(
        second_pack_kernel, "pack_cores", [ki], (kept, swap(sent, "k", "weights")),
        [shape((2 * ring_rows, part), BF16)] * blocks_w,
    )

    def from_z(blocks, name, ready=()):
        blocks = after(blocks, ready)
        got = [blocks[0]]
        for step in range(1, zs):
            with jax.named_scope(name):
                got.append(
                    lax.ppermute(blocks[step], "z", [(i, (i + step) % zs) for i in range(zs)])
                )
        return jnp.concatenate(got, 0)

    stream_own = from_z(packed[:zs], "stream_w_z")
    ws = exchange_weight(stream_own)
    gate_own = from_z(packed[zs : 2 * zs], "gate_w_z", stream_own)
    outer_own = from_z(packed[2 * zs :], "outer_w_z", gate_own)
    wg, wo = exchange_halves(gate_own, outer_own)

    slot_rows = owner_slot.reshape(rings, members, local_rows)
    tok, cot = tokens, cotangent
    ring_block = members * local_rows
    if rings > 1:
        per_ring = local_rows // rings
        flat = slot_rows.reshape(rings * members, local_rows)
        target = flat // ring_block
        place = target * per_ring + rank_in_class(target)
        chosen = jnp.arange(local_rows, dtype=jnp.int32)[None, :, None] == place[:, None, :]
        ordered = jnp.sum(jnp.where(chosen, flat[:, None, :], 0), axis=2)
        ordered = ordered.reshape(rings, members, rings, per_ring)
        ordered = lax.dynamic_index_in_dim(ordered, ri, 2, keepdims=False)
        slots = ordered.transpose(1, 0, 2).reshape(members, local_rows)
        own_place = lax.dynamic_index_in_dim(place, ri * members + zi * 4 + xi * 2 + ki, 0, False)
        ring_order = (
            jnp.arange(local_rows, dtype=jnp.int32)[:, None] == own_place[None, :]
        ).astype(BF16)

        def over_rings(value):
            value = value.reshape(rings, per_ring, width)
            return lax.all_to_all(value, "r", 0, 0, tiled=True).reshape(local_rows, width)

        tok, cot = (over_rings(dot(ring_order, v).astype(BF16)) for v in (tokens, cotangent))
    else:
        slots = slot_rows[0]
    local_slot = slots - ri * ring_block
    owner = local_slot // local_rows
    owner_z, owner_x, owner_k = owner // 4, (owner // 2) % 2, owner % 2
    rank = rank_in_class(owner_x * 2 + owner_k)
    in_owner = local_slot % local_rows
    scan_place = (in_owner % batch_rows) * segments + owner_z * MB + in_owner // batch_rows
    here = zi * 4 + xi * 2 + ki
    mine = [lax.dynamic_index_in_dim(v, here, 0, False) for v in (owner_x, owner_k, rank)]
    send_place = (mine[1] ^ ti) * (2 * share) + (mine[0] ^ xi) * share + mine[2]
    in_group = (owner_x == xi) & (owner_k == ti)
    ranked = (
        jnp.arange(share, dtype=jnp.int32)[None, :, None] == rank[:, None, :]
    ) & in_group[:, None, :]
    arrival = jnp.sum(jnp.where(ranked, scan_place[:, None, :], 0), axis=2)
    arrival = arrival.reshape(zs, 2, 2, share)
    arrival = jnp.where(xi == 0, arrival, arrival[:, ::-1]).transpose(0, 2, 1, 3)
    arrived = arrival.reshape(1, group_rows)
    returned = jnp.where(ki == 0, arrival, arrival[:, ::-1]).transpose(1, 0, 2, 3)
    returned = returned.reshape(group_rows, 1)

    blocks = [to_blocks(tok), to_blocks(cot)]
    lengths = sequence_lengths.reshape(1, -1).astype(BF16)
    lengths = jnp.concatenate([lengths, jnp.zeros((1, ring_rows - lengths.shape[1]), BF16)], 1)
    note = jnp.concatenate([gain, lengths, jnp.zeros((share - 2, ring_rows), BF16)], 0)
    noted, plain = shape((share, width + LANES), BF16), shape((share, width), BF16)
    rows_out = whole(
        prep_kernel, "prep", [xi], (send_place[None], *blocks, note), [noted, noted, plain, plain]
    )
    group_tokens = lax.all_gather(
        jnp.concatenate([rows_out[0], swap(rows_out[1], "x", "tokens")], 0), ZK, axis=0, tiled=True
    )

    first = (zi * 2 + ki) * part

    def own_channels(value):
        return lax.dynamic_slice_in_dim(value, first, part, 1)

    rows_f = taps + 3 + states
    floats = own_channels(
        jnp.concatenate(
            [
                filter_weight, convolution_bias[None], step_bias[None], decay_log,
                skip_weight[None], jnp.zeros((-rows_f % 8, half_channels), F32),
            ],
            axis=0,
        )
    )
    params = jnp.concatenate([floats, swap(floats, "t", "params")], axis=1)
    layout = (rank_width, states, taps + 1, taps + 2, taps + 2 + states)
    select_t = lax.dynamic_slice_in_dim(select_weight, first, part, 0).T
    lows = jnp.concatenate([own_channels(step_weight), select_t], 0)
    lows = jnp.concatenate([lows, swap(lows, "t", "params_low")], axis=1)
    step_w, select_w = lows[:rank_width], lows[rank_width:]

    count = select_w.shape[0]
    half_out = [shape((count, group_rows // 2), F32)] * 2
    full = shape((group_rows, channels), F32)
    wide_low = shape((group_rows, width), BF16)
    normed, stream, act, sel_mine, sel_other, position, gain_row = whole(
        partial(front_kernel, (taps, sequence_lengths.shape[1])), "front", [ki, ti, zi],
        (after(group_tokens, gate_own), arrived, *ws, params, select_w),
        [wide_low, full, full, *half_out, shape((group_rows, LANES), F32), shape((8, width), F32)],
        [pltpu.VMEM((group_rows, width), BF16), pltpu.VMEM((group_rows, channels), BF16)],
        flops=4 * group_rows * width * channels,
    )
    total, rest, _ = sum_zk(sel_mine, sel_other, ((), outer_own, (wg[1], wg[2])))
    cot_keep, cot_send = after((rows_out[2], rows_out[3]), gate_own)
    group_cot = lax.all_gather(
        jnp.concatenate([cot_keep, swap(cot_send, "x", "cot")], 0), ZK, axis=0, tiled=True
    )
    upstream, gate, gated_grad = whole(
        late_kernel, "late", [zi], (group_cot, arrived, normed, *wg, *wo), [wide_low, full, full],
        flops=6 * group_rows * width * channels,
    )
    gated, gate_grad, act_grad, small_a, sel_mine, sel_other = mixer(
        layout, ki, position, act, gate, gated_grad, total, rest, step_w, params
    )

    half_rows = [shape((group_rows // 2, width), BF16)] * 2
    out_mine, out_other = whole(
        out_kernel, "out_rows", [zi], (returned, gated, *wo), half_rows,
        flops=2 * group_rows * width * channels,
    )
    pieces = whole(
        late_grad_kernel, "late_grad", [zi], (normed, upstream, after(gate_grad, out_mine), gated),
        [shape((2 * zs, part, ring_rows), BF16)] * 8,
        flops=4 * group_rows * width * channels,
    )
    late_diagonal = diagonal_grads(pieces[:4], pieces[4:], "late_g")
    total, rest, first_sum = sum_zk(sel_mine, sel_other, (out_mine, pieces))
    out_total = return_core(out_mine, out_other)
    late_first = first_grads(
        *after((pieces[:4], pieces[4:]), first_sum), "late_g"
    )
    near, far = return_rows(out_total)
    total = after(total, late_diagonal, out_total)
    back_place = send_place[:, None]
    if rings > 1:
        zero = jnp.zeros_like(tokens)
        rows = whole(
            output_kernel, "output", [xi], (back_place, near, far, zero), [shape(tokens.shape, BF16)]
        )[0]
        rows = from_blocks(over_rings(rows))
        output = (tokens.astype(F32) + dot(ring_order, rows, TN)).astype(BF16)
    else:
        output = whole(
            output_kernel, "output", [xi], (back_place, near, far, tokens), [shape(tokens.shape, BF16)]
        )[0]
    low, small_b, *stream_pieces = whole(
        partial(back_kernel, taps), "back", [ki, zi],
        (total, rest, position, stream, act_grad, params, select_w, normed),
        [shape((group_rows, channels), BF16), shape((count + 8, channels), BF16)]
        + [shape((2 * zs, part // 2, ring_rows), BF16)] * 8,
        [pltpu.VMEM((group_rows, channels), BF16), pltpu.VMEM((channels, group_rows), BF16)],
        flops=4 * group_rows * width * channels,
    )
    in_mine, in_other = whole(
        in_kernel, "in_rows", [zi], (returned, low, gate_grad, *ws, *wg),
        half_rows, [pltpu.VMEM((group_rows, 2 * channels), BF16)],
        flops=4 * group_rows * width * channels,
    )
    in_total = return_core(in_mine, in_other)
    late_second = second_grads(pieces[:4], pieces[4:], late_diagonal, "late_g")
    sides = after((stream_pieces[::2], stream_pieces[1::2]), in_total)
    stream_diagonal = diagonal_grads(*sides, "stream_g")
    stream_first = first_grads(*sides, "stream_g")
    stream_second = second_grads(*sides, stream_diagonal, "stream_g")
    late_sum = jnp.concatenate(
        [
            plus(pieces[0], late_first[0], late_second[0]),
            plus(pieces[4], late_first[1], late_second[1]),
        ],
        axis=1,
    )
    late_home = to_owners(late_sum)
    gate_home, outer_home = late_home[:, :part], late_home[:, part:]
    outer_home = outer_home.reshape(half_channels, ring_rows).astype(F32)
    if rings > 1:
        outer_home = lax.psum_scatter(outer_home, "r", scatter_dimension=1, tiled=True)
    stream_sum = jnp.concatenate(
        [
            plus(sides[0][0], stream_first[0], stream_second[0]),
            plus(sides[1][0], stream_first[1], stream_second[1]),
        ],
        axis=1,
    )
    stream_home = to_owners(after(stream_sum, late_home))
    near, far = return_rows(in_total)
    if rings > 1:
        zero = jnp.zeros_like(tokens)
        rows = whole(
            output_kernel, "rows_back", [xi], (back_place, near, far, zero), [shape(tokens.shape, BF16)]
        )[0]
        rows = dot(ring_order, from_blocks(over_rings(rows)), TN)
        own_x = tokens.astype(F32)
        inverse = lax.rsqrt(jnp.mean(own_x * own_x, axis=1, keepdims=True) + EPSILON)
        hat = own_x * inverse
        gain_rel = gain_row[:1].reshape(2, zs, 2, ring_rows)
        gain_abs = jnp.where(xi == 0, gain_rel, gain_rel[::-1]).transpose(1, 0, 2, 3)
        grad = rows * from_blocks(gain_abs.reshape(1, width))
        input_grad = cotangent.astype(F32) + inverse * (
            grad - hat * jnp.mean(grad * hat, axis=1, keepdims=True)
        )
    else:
        input_grad = whole(
            input_kernel, "input_grad", [xi],
            (back_place, near, far, tokens, cotangent, gain_row), [shape(tokens.shape, F32)],
        )[0]
    inner_home = jnp.stack(
        [v.reshape(half_channels, ring_rows).T for v in (stream_home, gate_home)], axis=1
    ).astype(F32)
    if rings > 1:
        inner_home = lax.psum_scatter(inner_home, "r", scatter_dimension=0, tiled=True)
    gain_grad = jnp.sum(inner_home * inner_weight.astype(F32), axis=(1, 2))
    gain_grad = (gain_grad + swap(gain_grad, "t", "gain")) / norm_gain.astype(F32)

    small = after(jnp.concatenate([small_a, small_b], axis=0), stream_diagonal)
    small = plus(small[:, :part], swap(small[:, part:], "t", "small"))
    small = after(small, late_second)
    small = plus(small, swap(small, "x", "small"))
    if rings > 1:
        small = lax.psum(small.astype(F32), "r").astype(BF16)
    gathered = []
    for step in range(zs):
        with jax.named_scope("small_z"):
            block = small if step == 0 else lax.ppermute(
                small, "z", [(i, (i + step) % zs) for i in range(zs)]
            )
        gathered += [block, swap(block, "k", "small")]
    one_row = shape((1, half_channels), F32)
    select_grad, step_w_grad, decay_grad, filter_grad, filter_b_grad, step_b_grad, skip_grad = whole(
        partial(small_kernel, (count, states, taps)), "small", [zi, ki], gathered,
        [
            shape((half_channels, count), F32), shape((rank_width, half_channels), F32),
            shape((states, half_channels), F32), shape((taps, half_channels), F32),
            one_row, one_row, one_row,
        ],
    )
    return (
        output,
        input_grad,
        gain_grad,
        inner_home,
        filter_grad,
        filter_b_grad[0],
        select_grad,
        step_w_grad,
        step_b_grad[0],
        decay_grad,
        skip_grad[0],
        outer_home,
    )


def solution(mesh):
    devices = mesh.devices
    split = Mesh(
        devices.reshape(devices.shape[0] // 16, 4, 2, 2, devices.shape[1]), DP + ("t",)
    )
    in_specs = (
        P(DP, None), P(DP, None), P(), P(DP, None), P(DP), P(DP, None, "t"), P(None, "t"), P("t"),
        P("t", None), P(None, "t"), P("t"), P(None, "t"), P("t"), P("t", DP),
    )
    out_specs = (
        P(DP, None), P(DP, None), P(DP), P(DP, None, "t"), P(None, "t"), P("t"), P("t", None),
        P(None, "t"), P("t"), P(None, "t"), P("t"), P("t", DP),
    )
    return jax.shard_map(body, mesh=split, in_specs=in_specs, out_specs=out_specs, check_vma=False)
```

time: 1730 us -> 386 us (0.22)
  waiting for transfers between devices: 869 us -> 136 us
  other arithmetic: 431 us -> 21.1 us
  local copies, waits for them, and re-layouts: 215 us -> 53.9 us
  matrix products: 114 us -> 0 us
  Pallas kernels: 0 us -> 64.8 us
  starting transfers between devices: 26.8 us -> 88.8 us
  blocking collectives: 39.1 us -> 0 us
    reduce_scatter x2, waiting for transfers between devices: 515 us -> 0.04 us  [return_rows(): rows = lax.psum_scatter(total, 'z', scatter_dimension=0, tiled=True)]
    psum x3 -> x0, waiting for transfers between devices: 167 us -> none  [the longest x1 100 us: body(): lax.psum((filter_acc, fbias_acc, select_acc, stepw_acc, stepb_acc, decay_...]
    all_gather x2, waiting for transfers between devices: 139 us -> 0.01 us  [the longest x1 0.01 us: body(): lax.all_gather(jnp.concatenate([rows_out[0], swap(rows_out[1], 'x', 'toke...]
    ppermute x0 -> x60, waiting for transfers between devices: none -> 136 us  [the longest x44 80.1 us: swap(): return lax.ppermute(value, axis, SWAP)]
    reduce_sum x70 -> x3, other arithmetic: 126 us -> 1.62 us  [the longest x1 0.64 us: body(): gain_grad = jnp.sum(inner_home * inner_weight.astype(F32), axis=(1, 2))]
    dot_general x24 -> x0, matrix products: 114 us -> none  [the longest x2 35.2 us: inner_term(): jnp.einsum('rd,rce->dce', normed, projected_grad, preferred_element_type=...]
    dot_general x32 -> x0, other arithmetic: 83.9 us -> none  [advance(): hidden_states = jnp.einsum('lhyj,hyj->lyj', weight_table, incoming_rows)]
    ppermute x0 -> x60, starting transfers between devices: none -> 79.4 us  [the longest x44 39.6 us: swap(): return lax.ppermute(value, axis, SWAP)]
  transfers between devices with their start and end apart: 12 -> 66, of which waited for: 10 -> 30; matrix products, arithmetic and copies ran while one was open for 6% -> 8% of each run, Pallas kernels for 0% -> 9%
where the time goes in v1:
time: 386 us; the launch traced here: 380 us
  waiting for transfers between devices  136 us (35%)
  starting transfers between devices  88.8 us (23%)
  Pallas kernels  64.8 us (17%)
  local copies, waits for them, and re-layouts  53.9 us (14%)
  other arithmetic  21.1 us (5%)
  between operations  15.3 us (4%)
    ppermute x44, waiting for transfers between devices, swap(): return lax.ppermute(value, axis, SWAP)  80.1 us
    unnamed x205, local copies, waits for them, and re-layouts  45 us
    ppermute x44, starting transfers between devices, swap(): return lax.ppermute(value, axis, SWAP)  39.6 us
    pallas_call x12, Pallas kernels, whole(): pl.pallas_call(copied, in_specs=[pl.BlockSpec(memory_space=pltpu.SMEM)] *...  36.1 us
    ppermute x9, starting transfers between devices, from_z(): lax.ppermute(blocks[step], 'z', [(i, (i + step) % zs) for i in range(zs)])  28.9 us
    pallas_call x1, Pallas kernels, mixer(): pl.pallas_call(partial(scan_kernel, layout), grid=(channels // lanes,), i...  28.6 us
    ppermute x9, waiting for transfers between devices, from_z(): lax.ppermute(blocks[step], 'z', [(i, (i + step) % zs) for i in range(zs)])  28.2 us
    ppermute x3, waiting for transfers between devices, body(): lax.ppermute(small, 'z', [(i, (i + step) % zs) for i in range(zs)])  22.3 us
  transfers between devices with their start and end apart: 66, of which 30 were waited for; matrix products, arithmetic and copies ran while one was open for 8% of the time, Pallas kernels for 9%

profile of v1, /device:TPU:0, one launch (start us, length us, event | category | flops | bytes accessed | tf_op | source)
XLA Modules:
  0.0 380.0 jit_solution(12532806339456491401)
XLA Ops:
  33.6 10.9 %collective-permute-done.3 = bf16[256,256]{1,0:T(8,128)(2,1)S(1)} collective-permute-done((bf16[256,256]{1,0:T(8,128)(2,1)S(1)}, bf16[256,256]{1,0:T(8,128)(2,1)S(1)}, u32[]{:S(2)}, u32[]{:S(2)}) %collective-permute-start.3) | collective-permute-done | bytes 131104 | tf_op jit(solution)/shard_map/stream_w_z/ppermute | solution.py:771
  44.5 11.5 %collective-permute-start.5 = (bf16[256,256]{1,0:T(8,128)(2,1)S(1)}, bf16[256,256]{1,0:T(8,128)(2,1)S(1)}, u32[]{:S(2)}, u32[]{:S(2)}) collective-permute-start(bf16[256,256]{1,0:T(8,128)(2,1)S(1)} %get-tuple-element.126), channel_id=1, source_target_pairs={{0,8},{8,16},{16,24},{24,0},{1,9},{9,17},{17,25},{25,1},{2,10},{10... | collective-permute-start | bytes 393224 | tf_op jit(solution)/shard_map/gate_w_z/ppermute | solution.py:771
  60.4 7.5 %collective-permute-done.6 = bf16[256,256]{1,0:T(8,128)(2,1)S(1)} collective-permute-done((bf16[256,256]{1,0:T(8,128)(2,1)S(1)}, bf16[256,256]{1,0:T(8,128)(2,1)S(1)}, u32[]{:S(2)}, u32[]{:S(2)}) %collective-permute-start.6) | collective-permute-done | bytes 131104 | tf_op jit(solution)/shard_map/gate_w_z/ppermute | solution.py:771
  91.6 4.3 %collective-permute-start.20 = (bf16[256,256]{1,0:T(8,128)(2,1)S(1)}, bf16[256,256]{1,0:T(8,128)(2,1)S(1)}, u32[]{:S(2)}, u32[]{:S(2)}) collective-permute-start(bf16[256,256]{1,0:T(8,128)(2,1)S(1)} %get-tuple-element.144), channel_id=1, source_target_pairs={{0,24},{8,0},{16,8},{24,16},{1,25},{9,1},{17,9},{25,17},{2,26},{10... | collective-permute-start | bytes 393224 | tf_op jit(solution)/shard_map/outer_w_z/ppermute | solution.py:771
  102.2 3.7 collective-permute-done.20
  109.9 6.1 %front.1 = (bf16[512,2048]{1,0:T(8,128)(2,1)S(1)}, f32[512,512]{1,0:T(8,128)S(1)}, f32[512,512]{1,0:T(8,128)S(1)}, f32[160,256]{1,0:T(8,128)S(1)}, f32[160,256]{...) custom-call(s32[1]{0:T(128)} %bitcast.7.refs_1_.refs_0_.core_ref, s32[1]{0:T(128)} %bitcast.8.refs_1_, ...), custom_call_target="tpu_custom_call" | custom-call | flops 2147483648 | bytes 9390080 | tf_op jit(solution)/shard_map/front/pallas_call | solution.py:57
  120.7 4.9 %collective-permute-start.25 = (bf16[160,256]{1,0:T(8,128)(2,1)S(1)}, bf16[160,256]{1,0:T(8,128)(2,1)S(1)}, u32[]{:S(2)}, u32[]{:S(2)}) collective-permute-start(bf16[160,256]{1,0:T(8,128)(2,1)S(1)} %add_convert_fusion.14), channel_id=1, source_target_pairs={{0,8},{8,0},{16,24},{24,16},{1,9},{9,1},{17,25},{25,17},{2,10},{10... | collective-permute-start | bytes 245768 | tf_op jit(solution)/shard_map/ppermute | solution.py:647
  130.0 4.1 %collective-permute-done.16.refs_6_.refs_11_ = bf16[1024,256]{1,0:T(8,128)(2,1)S(1)} collective-permute-done((bf16[1024,256]{1,0:T(8,128)(2,1)S(1)}, bf16[1024,256]{1,0:T(8,128)(2,1)S(1)}, u32[]{:S(2)}, u32[]{:S(2)}) %collective-permute-start.16) | collective-permute-done | bytes 524320 | tf_op jit(solution)/shard_map/gate_w_t/ppermute | solution.py:636
  135.1 5.3 %collective-permute-done.21.refs_9_.refs_4_ = bf16[1024,256]{1,0:T(8,128)(2,1)S(1)} collective-permute-done((bf16[1024,256]{1,0:T(8,128)(2,1)S(1)}, bf16[1024,256]{1,0:T(8,128)(2,1)S(1)}, u32[]{:S(2)}, u32[]{:S(2)}) %collective-permute-start.21) | collective-permute-done | bytes 524320 | tf_op jit(solution)/shard_map/outer_w_x/ppermute | solution.py:636
  144.8 5.8 %collective-permute-done.23.refs_11_.refs_6_ = bf16[1024,256]{1,0:T(8,128)(2,1)S(1)} collective-permute-done((bf16[1024,256]{1,0:T(8,128)(2,1)}, bf16[1024,256]{1,0:T(8,128)(2,1)S(1)}, u32[]{:S(2)}, u32[]{:S(2)}) %collective-permute-start.23) | collective-permute-done | bytes 524320 | tf_op jit(solution)/shard_map/outer_w_far_x/ppermute | solution.py:636
  156.7 5.2 %late.1 = (bf16[512,2048]{1,0:T(8,128)(2,1)S(1)}, f32[512,512]{1,0:T(8,128)S(1)}, f32[512,512]{1,0:T(8,128)S(1)}) custom-call(s32[1]{0:T(128)} %bitcast.3.refs_0_.refs_2_.refs_1_, bf16[512,2048]{1,0:T(8,128)(2,1)S(1)} %copy-done.29, s32[1,512]{1,0:T(1,128)S(1)} %reshape.365.refs_4_.refs_2_, bf16[512,2048]{1,0:T(8,128)(2,1)S(1)} %copy-done.56, ...), custom_call_target="tpu_custom_call" | custom-call | flops 3221225472 | bytes 12584960 | tf_op jit(solution)/shard_map/late/pallas_call | solution.py:57
  164.2 28.6 %mixer.1 = (bf16[512,512]{1,0:T(8,128)(2,1)S(1)}, bf16[512,512]{1,0:T(8,128)(2,1)S(1)}, f32[512,512]{1,0:T(8,128)S(1)}, bf16[152,512]{1,0:T(8,128)(2,1)S(1)}, f3...) custom-call(s32[1]{0:T(128)} %bitcast.7.refs_1_.refs_0_.core_ref, f32[512,128]{1,0:T(8,128)S(1)} %copy-done.72, ...), custom_call_target="tpu_custom_call" | custom-call | flops 83886080 | bytes 7864320 | tf_op jit(solution)/shard_map/mixer/pallas_call | solution.py:588
  209.3 4.3 %collective-permute-done.33 = bf16[160,256]{1,0:T(8,128)(2,1)S(1)} collective-permute-done((bf16[160,256]{1,0:T(8,128)(2,1)S(1)}, bf16[160,256]{1,0:T(8,128)(2,1)S(1)}, u32[]{:S(2)}, u32[]{:S(2)}) %collective-permute-start.33) | collective-permute-done | bytes 81952 | tf_op jit(solution)/shard_map/ppermute | solution.py:647
  214.4 6.3 %collective-permute-done.34 = bf16[8,256,128]{2,1,0:T(8,128)(2,1)S(1)} collective-permute-done((bf16[8,256,128]{2,1,0:T(8,128)(2,1)S(1)}, bf16[8,256,128]{2,1,0:T(8,128)(2,1)S(1)}, u32[]{:S(2)}, u32[]{:S(2)}) %collective-permute-start.34) | collective-permute-done | bytes 524320 | tf_op jit(solution)/shard_map/late_g_far_x/ppermute | solution.py:636
  232.1 4.2 %back.1 = (bf16[512,512]{1,0:T(8,128)(2,1)S(1)}, bf16[168,512]{1,0:T(8,128)(2,1)S(1)}, bf16[8,128,128]{2,1,0:T(8,128)(2,1)S(1)}, bf16[8,128,128]{2,1,0:T(8,128)(...) custom-call(s32[1]{0:T(128)} %bitcast.7.refs_1_.refs_0_.core_ref, ...), custom_call_target="tpu_custom_call" | custom-call | flops 2147483648 | bytes 7790592 | tf_op jit(solution)/shard_map/back/pallas_call | solution.py:57
  239.2 4.4 %in_rows.1 = (bf16[256,2048]{1,0:T(8,128)(2,1)S(1)}, bf16[256,2048]{1,0:T(8,128)(2,1)S(1)}) custom-call(s32[1]{0:T(128)} %bitcast.3.refs_0_.refs_2_.refs_1_, s32[512,1]{1,0:T(8,128)S(1)} %reshape.369.refs_1_, bf16[512,512]{1,0:T(8,128)(2,1)S(1)} %get-tuple-element.172.refs_2_, bf16[512,512]{1,0:T(8,128)(2,1)S(1)} %copy-done.69, ...), custom_call_target="tpu_custom_call" | custom-call | flops 2147483648 | bytes 7342080 | tf_op jit(solution)/shard_map/in_rows/pallas_call | solution.py:57
  247.2 11.0 %collective-permute-done.49 = bf16[8,256,128]{2,1,0:T(8,128)(2,1)S(1)} collective-permute-done((bf16[8,256,128]{2,1,0:T(8,128)(2,1)S(1)}, bf16[8,256,128]{2,1,0:T(8,128)(2,1)S(1)}, u32[]{:S(2)}, u32[]{:S(2)}) %collective-permute-start.49) | collective-permute-done | bytes 524320 | tf_op jit(solution)/shard_map/late_g_sum_x/ppermute | solution.py:636
  264.8 4.9 %all-to-all-start = ((bf16[8,512,128]{2,1,0:T(8,128)(2,1)}), bf16[8,512,128]{2,1,0:T(8,128)(2,1)}, u32[]{:S(2)}, u32[]{:S(2)}) async-start(bf16[8,512,128]{2,1,0:T(8,128)(2,1)} %pad_maximum_fusion), calls=%async_computation.2 | async-start | bytes 2097152 | tf_op jit(solution)/shard_map/all_to_all | solution.py:702
  274.6 4.8 %collective-permute-done.44 = bf16[8,128,128]{2,1,0:T(8,128)(2,1)} collective-permute-done((bf16[8,128,128]{2,1,0:T(8,128)(2,1)S(1)}, bf16[8,128,128]{2,1,0:T(8,128)(2,1)}, u32[]{:S(2)}, u32[]{:S(2)}) %collective-permute-start.44) | collective-permute-done | bytes 262176 | tf_op jit(solution)/shard_map/stream_g_far_t/ppermute | solution.py:636
  282.7 10.9 %collective-permute-done.51 = bf16[320,256]{1,0:T(8,128)(2,1)S(1)} collective-permute-done((bf16[320,256]{1,0:T(8,128)(2,1)S(1)}, bf16[320,256]{1,0:T(8,128)(2,1)S(1)}, u32[]{:S(2)}, u32[]{:S(2)}) %collective-permute-start.51) | collective-permute-done | bytes 163872 | tf_op jit(solution)/shard_map/small_t/ppermute | solution.py:636
  294.7 4.8 %collective-permute-done.52 = bf16[320,256]{1,0:T(8,128)(2,1)S(1)} collective-permute-done((bf16[320,256]{1,0:T(8,128)(2,1)S(1)}, bf16[320,256]{1,0:T(8,128)(2,1)S(1)}, u32[]{:S(2)}, u32[]{:S(2)}) %collective-permute-start.52) | collective-permute-done | bytes 163872 | tf_op jit(solution)/shard_map/small_x/ppermute | solution.py:636
  304.8 10.1 %collective-permute-done.58.refs_8_ = bf16[320,256]{1,0:T(8,128)(2,1)S(1)} collective-permute-done((bf16[320,256]{1,0:T(8,128)(2,1)S(1)}, bf16[320,256]{1,0:T(8,128)(2,1)S(1)}, u32[]{:S(2)}, u32[]{:S(2)}) %collective-permute-start.58) | collective-permute-done | bytes 163872 | tf_op jit(solution)/shard_map/small_z/ppermute | solution.py:991
  314.9 12.2 %collective-permute-done.56.refs_6_ = bf16[320,256]{1,0:T(8,128)(2,1)S(1)} collective-permute-done((bf16[320,256]{1,0:T(8,128)(2,1)S(1)}, bf16[320,256]{1,0:T(8,128)(2,1)S(1)}, u32[]{:S(2)}, u32[]{:S(2)}) %collective-permute-start.56) | collective-permute-done | bytes 163872 | tf_op jit(solution)/shard_map/small_z/ppermute | solution.py:991
  327.7 4.1 %all-to-all-start.1 = ((bf16[8,256,128]{2,1,0:T(8,128)(2,1)}), bf16[8,256,128]{2,1,0:T(8,128)(2,1)}, u32[]{:S(2)}, u32[]{:S(2)}) async-start(bf16[8,256,128]{2,1,0:T(8,128)(2,1)} %pad_maximum_fusion.1), calls=%async_computation.3 | async-start | bytes 1048576 | tf_op jit(solution)/shard_map/all_to_all | solution.py:702
  (400 shorter events, 184.9 us)
Async XLA Ops:
  7.2 99.9 %all-gather.3.cloned.1.call-start = ((), (), s32[]{:S(2)}) async-start(), calls=%async_computation.4 | async-start | bytes 2506752 | tf_op jit(solution)/shard_map/all_gather | solution.py:834
  20.9 130.5 %all-gather.5.cloned.1.call-start = ((), (), s32[]{:S(2)}) async-start(), calls=%async_computation.5 | async-start | bytes 2359296 | tf_op jit(solution)/shard_map/all_gather | solution.py:873
  27.1 17.3 %collective-permute-start.3 = (bf16[256,256]{1,0:T(8,128)(2,1)S(1)}, bf16[256,256]{1,0:T(8,128)(2,1)S(1)}, u32[]{:S(2)}, u32[]{:S(2)}) collective-permute-start(bf16[256,256]{1,0:T(8,128)(2,1)S(1)} %get-tuple-element.123), channel_id=1, source_target_pairs={{0,16},{8,24},{16,0},{24,8},{1,17},{9,25},{17,1},{25,9},{2,18},{10... | collective-permute-start | bytes 393224 | tf_op jit(solution)/shard_map/stream_w_z/ppermute | solution.py:771
  74.0 257.9 %reduce-scatter.3.cloned.1.call-start = ((), (), s32[]{:S(2)}) async-start(), calls=%async_computation.6 | async-start | bytes 1310720 | tf_op jit(solution)/shard_map/reduce_scatter | solution.py:659
  85.9 40.7 %collective-permute-start.15 = (bf16[1024,256]{1,0:T(8,128)(2,1)S(1)}, bf16[1024,256]{1,0:T(8,128)(2,1)}, u32[]{:S(2)}, u32[]{:S(2)}) collective-permute-start(bf16[1024,256]{1,0:T(8,128)(2,1)S(1)} %constant_dynamic-update-slice_fusion.4.refs_4_.refs_9_), channel_id=1, source_target_pairs={{0,4},{4,0},{1,5},{5,1},{2,6},{6,2},{3,7},{7,3},{8,12},{12,8},{9,1... | collective-permute-start | bytes 1572872 | tf_op jit(solution)/shard_map/gate_w_x/ppermute | solution.py:636
  105.9 21.5 %collective-permute-start.22 = (bf16[1024,256]{1,0:T(8,128)(2,1)S(1)}, bf16[1024,256]{1,0:T(8,128)(2,1)}, u32[]{:S(2)}, u32[]{:S(2)}) collective-permute-start(bf16[1024,256]{1,0:T(8,128)(2,1)S(1)} %constant_dynamic-update-slice_fusion.8.refs_8_.refs_3_), channel_id=1, source_target_pairs={{0,1},{1,0},{2,3},{3,2},{4,5},{5,4},{6,7},{7,6},{8,9},{9,8},{10,11... | collective-permute-start | bytes 1572872 | tf_op jit(solution)/shard_map/outer_w_t/ppermute | solution.py:636
  126.6 18.2 %collective-permute-start.17 = (bf16[1024,256]{1,0:T(8,128)(2,1)}, bf16[1024,256]{1,0:T(8,128)(2,1)S(1)}, u32[]{:S(2)}, u32[]{:S(2)}) collective-permute-start(bf16[1024,256]{1,0:T(8,128)(2,1)} %collective-permute-done.15.refs_5_.refs_10_), channel_id=1, source_target_pairs={{0,1},{1,0},{2,3},{3,2},{4,5},{5,4},{6,7},{7,6},{8,9},{9,8},{10,11... | collective-permute-start | bytes 1572872 | tf_op jit(solution)/shard_map/gate_w_far_t/ppermute | solution.py:636
  127.3 23.2 %collective-permute-start.23 = (bf16[1024,256]{1,0:T(8,128)(2,1)}, bf16[1024,256]{1,0:T(8,128)(2,1)S(1)}, u32[]{:S(2)}, u32[]{:S(2)}) collective-permute-start(bf16[1024,256]{1,0:T(8,128)(2,1)} %collective-permute-done.22.refs_10_.refs_5_), channel_id=1, source_target_pairs={{0,4},{4,0},{1,5},{5,1},{2,6},{6,2},{3,7},{7,3},{8,12},{12,8},{9,1... | collective-permute-start | bytes 1572872 | tf_op jit(solution)/shard_map/outer_w_far_x/ppermute | solution.py:636
  135.1 29.1 %collective-permute-start.27 = (f32[160,256]{1,0:T(8,128)S(1)}, f32[160,256]{1,0:T(8,128)S(1)}, u32[]{:S(2)}, u32[]{:S(2)}) collective-permute-start(f32[160,256]{1,0:T(8,128)S(1)} %convert_add_fusion.2.total_ref), channel_id=1, source_target_pairs={{0,2},{2,0},{1,3},{3,1},{4,6},{6,4},{5,7},{7,5},{8,10},{10,8},{9,1... | collective-permute-start | bytes 491528 | tf_op jit(solution)/shard_map/select_rest_k/ppermute | solution.py:636
  199.7 23.4 %collective-permute-start.28 = (bf16[256,2048]{1,0:T(8,128)(2,1)S(1)}, bf16[256,2048]{1,0:T(8,128)(2,1)S(1)}, u32[]{:S(2)}, u32[]{:S(2)}) collective-permute-start(bf16[256,2048]{1,0:T(8,128)(2,1)S(1)} %get-tuple-element.153), channel_id=1, source_target_pairs={{0,2},{2,0},{1,3},{3,1},{4,6},{6,4},{5,7},{7,5},{8,10},{10,8},{9,1... | collective-permute-start | bytes 3145736 | tf_op jit(solution)/shard_map/rows_k/ppermute | solution.py:636
  208.3 36.7 %collective-permute-start.46 = (bf16[8,256,128]{2,1,0:T(8,128)(2,1)}, bf16[8,256,128]{2,1,0:T(8,128)(2,1)}, u32[]{:S(2)}, u32[]{:S(2)}) collective-permute-start(bf16[8,256,128]{2,1,0:T(8,128)(2,1)} %get-tuple-element.192), channel_id=1, source_target_pairs={{0,4},{4,0},{1,5},{5,1},{2,6},{6,2},{3,7},{7,3},{8,12},{12,8},{9,1... | collective-permute-start | bytes 1572872 | tf_op jit(solution)/shard_map/late_g_x/ppermute | solution.py:636
  213.7 33.5 %collective-permute-start.48 = (bf16[8,256,128]{2,1,0:T(8,128)(2,1)}, bf16[8,256,128]{2,1,0:T(8,128)(2,1)}, u32[]{:S(2)}, u32[]{:S(2)}) collective-permute-start(bf16[8,256,128]{2,1,0:T(8,128)(2,1)} %get-tuple-element.193), channel_id=1, source_target_pairs={{0,1},{1,0},{2,3},{3,2},{4,5},{5,4},{6,7},{7,6},{8,9},{9,8},{10,11... | collective-permute-start | bytes 1572872 | tf_op jit(solution)/shard_map/late_g_t/ppermute | solution.py:636
  222.4 22.6 %collective-permute-start.47 = (bf16[8,256,128]{2,1,0:T(8,128)(2,1)}, bf16[8,256,128]{2,1,0:T(8,128)(2,1)}, u32[]{:S(2)}, u32[]{:S(2)}) collective-permute-start(bf16[8,256,128]{2,1,0:T(8,128)(2,1)} %add_convert_fusion.5), channel_id=1, source_target_pairs={{0,1},{1,0},{2,3},{3,2},{4,5},{5,4},{6,7},{7,6},{8,9},{9,8},{10,11... | collective-permute-start | bytes 1572872 | tf_op jit(solution)/shard_map/late_g_sum_t/ppermute | solution.py:636
  264.8 62.9 %all-to-all-start = ((bf16[8,512,128]{2,1,0:T(8,128)(2,1)}), bf16[8,512,128]{2,1,0:T(8,128)(2,1)}, u32[]{:S(2)}, u32[]{:S(2)}) async-start(bf16[8,512,128]{2,1,0:T(8,128)(2,1)} %pad_maximum_fusion), calls=%async_computation.2 | async-start | bytes 2097152 | tf_op jit(solution)/shard_map/all_to_all | solution.py:702
  269.6 88.4 %reduce-scatter.5.cloned.1.call-start = ((), (), s32[]{:S(2)}) async-start(), calls=%async_computation.7 | async-start | bytes 1310720 | tf_op jit(solution)/shard_map/reduce_scatter | solution.py:659
  271.4 23.2 %collective-permute-start.40 = (bf16[8,128,128]{2,1,0:T(8,128)(2,1)S(1)}, bf16[8,128,128]{2,1,0:T(8,128)(2,1)S(1)}, u32[]{:S(2)}, u32[]{:S(2)}) collective-permute-start(bf16[8,128,128]{2,1,0:T(8,128)(2,1)S(1)} %copy-done.45), channel_id=1, source_target_pairs={{0,4},{4,0},{1,5},{5,1},{2,6},{6,2},{3,7},{7,3},{8,12},{12,8},{9,1... | collective-permute-start | bytes 786440 | tf_op jit(solution)/shard_map/stream_g_x/ppermute | solution.py:636
  272.4 31.5 %collective-permute-start.43 = (bf16[8,128,128]{2,1,0:T(8,128)(2,1)S(1)}, bf16[8,128,128]{2,1,0:T(8,128)(2,1)S(1)}, u32[]{:S(2)}, u32[]{:S(2)}) collective-permute-start(bf16[8,128,128]{2,1,0:T(8,128)(2,1)S(1)} %copy-done.43), channel_id=1, source_target_pairs={{0,1},{1,0},{2,3},{3,2},{4,5},{5,4},{6,7},{7,6},{8,9},{9,8},{10,11... | collective-permute-start | bytes 786440 | tf_op jit(solution)/shard_map/stream_g_t/ppermute | solution.py:636
  273.3 21.3 %collective-permute-start.42 = (bf16[8,128,128]{2,1,0:T(8,128)(2,1)S(1)}, bf16[8,128,128]{2,1,0:T(8,128)(2,1)S(1)}, u32[]{:S(2)}, u32[]{:S(2)}) collective-permute-start(bf16[8,128,128]{2,1,0:T(8,128)(2,1)S(1)} %add_convert_fusion.9), channel_id=1, source_target_pairs={{0,1},{1,0},{2,3},{3,2},{4,5},{5,4},{6,7},{7,6},{8,9},{9,8},{10,11... | collective-permute-start | bytes 786440 | tf_op jit(solution)/shard_map/stream_g_sum_t/ppermute | solution.py:636
  281.6 22.3 %collective-permute-start.45 = (bf16[8,128,128]{2,1,0:T(8,128)(2,1)S(1)}, bf16[8,128,128]{2,1,0:T(8,128)(2,1)S(1)}, u32[]{:S(2)}, u32[]{:S(2)}) collective-permute-start(bf16[8,128,128]{2,1,0:T(8,128)(2,1)S(1)} %add_convert_fusion.7), channel_id=1, source_target_pairs={{0,4},{4,0},{1,5},{5,1},{2,6},{6,2},{3,7},{7,3},{8,12},{12,8},{9,1... | collective-permute-start | bytes 786440 | tf_op jit(solution)/shard_map/stream_g_sum_x/ppermute | solution.py:636
  302.8 24.4 %collective-permute-start.56 = (bf16[320,256]{1,0:T(8,128)(2,1)S(1)}, bf16[320,256]{1,0:T(8,128)(2,1)S(1)}, u32[]{:S(2)}, u32[]{:S(2)}) collective-permute-start(bf16[320,256]{1,0:T(8,128)(2,1)S(1)} %add_convert_fusion.10.refs_2_), channel_id=1, source_target_pairs={{0,16},{8,24},{16,0},{24,8},{1,17},{9,25},{17,1},{25,9},{2,18},{10... | collective-permute-start | bytes 491528 | tf_op jit(solution)/shard_map/small_z/ppermute | solution.py:991
  302.8 24.4 %collective-permute-start.54 = (bf16[320,256]{1,0:T(8,128)(2,1)S(1)}, bf16[320,256]{1,0:T(8,128)(2,1)S(1)}, u32[]{:S(2)}, u32[]{:S(2)}) collective-permute-start(bf16[320,256]{1,0:T(8,128)(2,1)S(1)} %add_convert_fusion.10.refs_2_), channel_id=1, source_target_pairs={{0,8},{8,16},{16,24},{24,0},{1,9},{9,17},{17,25},{25,1},{2,10},{10... | collective-permute-start | bytes 491528 | tf_op jit(solution)/shard_map/small_z/ppermute | solution.py:991
  304.8 37.2 %collective-permute-start.53 = (bf16[320,256]{1,0:T(8,128)(2,1)S(1)}, bf16[320,256]{1,0:T(8,128)(2,1)S(1)}, u32[]{:S(2)}, u32[]{:S(2)}) collective-permute-start(bf16[320,256]{1,0:T(8,128)(2,1)S(1)} %add_convert_fusion.10.refs_2_), channel_id=1, source_target_pairs={{0,2},{2,0},{1,3},{3,1},{4,6},{6,4},{5,7},{7,5},{8,10},{10,8},{9,1... | collective-permute-start | bytes 491528 | tf_op jit(solution)/shard_map/small_k/ppermute | solution.py:636
  314.9 27.8 %collective-permute-start.59 = (bf16[320,256]{1,0:T(8,128)(2,1)S(1)}, bf16[320,256]{1,0:T(8,128)(2,1)S(1)}, u32[]{:S(2)}, u32[]{:S(2)}) collective-permute-start(bf16[320,256]{1,0:T(8,128)(2,1)S(1)} %collective-permute-done.58.refs_8_), channel_id=1, source_target_pairs={{0,2},{2,0},{1,3},{3,1},{4,6},{6,4},{5,7},{7,5},{8,10},{10,8},{9,1... | collective-permute-start | bytes 491528 | tf_op jit(solution)/shard_map/small_k/ppermute | solution.py:636
  327.7 29.1 %all-to-all-start.1 = ((bf16[8,256,128]{2,1,0:T(8,128)(2,1)}), bf16[8,256,128]{2,1,0:T(8,128)(2,1)}, u32[]{:S(2)}, u32[]{:S(2)}) async-start(bf16[8,256,128]{2,1,0:T(8,128)(2,1)} %pad_maximum_fusion.1), calls=%async_computation.3 | async-start | bytes 1048576 | tf_op jit(solution)/shard_map/all_to_all | solution.py:702
  (138 other events, 1647.3 us)
Sparse Core Ops, SparseCore 0:
  21.0 47.3 all-gather.2
  74.1 41.3 all-gather.4
  224.7 27.4 reduce-scatter.2
  273.1 42.9 reduce-scatter.4

commit v2 on v1

--- a/solution.py
+++ b/solution.py
@@ -16,6 +16,8 @@
 RESET_RATE = 1e30
 LANES = 128
 SUBLANES = 8
+SIDE = 2
+GROUP = 8
 F32 = jnp.float32
 BF16 = jnp.bfloat16
 NT = ((1,), (1,))
@@ -39,33 +41,43 @@
 def whole(kernel, name, scalars, arrays, outs, scratch=(), flops=0):
     scalars = [jnp.reshape(v, (1,)).astype(jnp.int32) for v in scalars]
     size = sum(v.size * v.dtype.itemsize for v in (*arrays, *outs))
-    few, many = len(scalars), len(arrays)
+    few, many, made = len(scalars), len(arrays), len(outs)
 
     def copied(*refs):
-        inputs, rest = refs[few : few + many], refs[few + many : -many - 1]
-        held, semaphores = refs[-many - 1 : -1], refs[-1]
-        copies = [
+        inputs, refs_rest = refs[few : few + many], refs[few + many :]
+        outputs, refs_rest = refs_rest[:made], refs_rest[made:]
+        held, results = refs_rest[:many], refs_rest[many : many + made]
+        *rest, semaphores = refs_rest[many + made :]
+        loads = [
             pltpu.make_async_copy(source, target, semaphores.at[i])
             for i, (source, target) in enumerate(zip(inputs, held))
         ]
-        for copy in copies:
+        stores = [
+            pltpu.make_async_copy(source, target, semaphores.at[many + i])
+            for i, (source, target) in enumerate(zip(results, outputs))
+        ]
+        for copy in loads:
             copy.start()
-        for copy in copies:
+        for copy in loads:
             copy.wait()
-        kernel(*refs[:few], *held, *rest)
+        kernel(*refs[:few], *held, *results, *rest)
+        for copy in stores:
+            copy.start()
+        for copy in stores:
+            copy.wait()
 
     return pl.pallas_call(
         copied,
         in_specs=[pl.BlockSpec(memory_space=pltpu.SMEM)] * few
-        + [pl.BlockSpec(memory_space=pl.ANY)] * many,
-        out_specs=[pl.BlockSpec(memory_space=pltpu.VMEM)] * len(outs),
+        + [pl.BlockSpec(memory_space=pltpu.HBM)] * many,
+        out_specs=[pl.BlockSpec(memory_space=pltpu.HBM)] * made,
         out_shape=list(outs),
         scratch_shapes=[
+            *(pltpu.VMEM(v.shape, v.dtype) for v in (*arrays, *outs)),
             *scratch,
-            *(pltpu.VMEM(v.shape, v.dtype) for v in arrays),
-            pltpu.SemaphoreType.DMA((many,)),
+            pltpu.SemaphoreType.DMA((many + made,)),
         ],
-        compiler_params=pltpu.CompilerParams(vmem_limit_bytes=40 << 20),
+        compiler_params=pltpu.CompilerParams(vmem_limit_bytes=60 << 20),
         cost_estimate=pl.CostEstimate(flops=flops, bytes_accessed=size, transcendentals=0),
         name=name,
     )(*scalars, *arrays)
@@ -408,7 +420,14 @@
         low_ref[:, at] = stream_grad.astype(BF16)
         grad_t[at, :] = stream_grad.T.astype(BF16)
     small_ref[:count, :] = dot(selected_low, act_low[...]).astype(BF16)
-    grad_pieces(z_ref, grad_t[...], n_ref, [outs[2 * i : 2 * i + 2] for i in range(4)])
+    own_low, own_high, by_x_high, by_t_low, x_way, t_way = outs
+    grad_pieces(
+        z_ref, grad_t[...], n_ref,
+        [
+            (own_low, own_high), (x_way.at[1], by_x_high),
+            (by_t_low, t_way.at[1]), (x_way.at[0], t_way.at[0]),
+        ],
+    )
 
 
 def in_kernel(z_ref, place_ref, low_ref, gate_grad_ref, *refs):
@@ -450,185 +469,191 @@
 def scan_kernel(
     layout, core_ref, pos_ref, act_ref, gate_ref, gg_ref, total_ref, rest_ref, sw_ref, par_ref,
     gated_ref, gateg_ref, sact_ref, small_ref, mine_ref, other_ref,
-    bb, cb, hist, fac, ci_acc, co_acc, rate_s, reff_s, u_s, ds_s, y_s, s2_s, decb, sel_t, rate_low, rank_t,
+    bb, cb, hist, fac, ci_acc, co_acc, rate_s, reff_s, u_s, ds_s, y_s, s2_s, slope_s, decb, sel_t, rate_low, rank_t,
 ):
     rank_width, states, bias_row, decay_row, skip_row = layout
-    rows, lanes = act_ref.shape
+    rows, channels = act_ref.shape
+    lanes = LANES
     steps = rows // SUBLANES
-    block = pl.program_id(0)
     wide = states * lanes
     first = core_ref[0] == 0
     spread = (
         lax.broadcasted_iota(jnp.int32, (states, wide), 1) // lanes
         == lax.broadcasted_iota(jnp.int32, (states, wide), 0)
     ).astype(F32).astype(BF16)
-
-    @pl.when(block == 0)
-    def _():
-        total, rest = total_ref[...], rest_ref[...]
-        sel_t[:, : rows // 2] = jnp.where(first, total, rest)
-        sel_t[:, rows // 2 :] = jnp.where(first, rest, total)
-        rate_low[...] = sel_t[:rank_width, :].T.astype(BF16)
-        bb[...] = split_dot(sel_t[rank_width : rank_width + states, :], spread, TN)
-        cb[...] = split_dot(sel_t[rank_width + states :, :], spread, TN)
-        hist[0:SUBLANES, :] = jnp.zeros((SUBLANES, wide), F32)
-        ci_acc[...] = jnp.zeros_like(ci_acc)
-        co_acc[...] = jnp.zeros_like(co_acc)
-        rank_t[...] = jnp.zeros_like(rank_t)
-
-    decay = -jnp.exp(par_ref[decay_row : decay_row + states, :])
-    for n in range(states):
-        decb[8 * n : 8 * n + 8, :] = jnp.broadcast_to(decay[n : n + 1, :], (8, lanes))
-
-    step_pre = dot(rate_low[...], sw_ref[...]) + par_ref[bias_row : bias_row + 1, :]
-    step_slope = jax.nn.sigmoid(step_pre)
-    rate = jnp.maximum(step_pre, 0.0) + jnp.log1p(jnp.exp(-jnp.abs(step_pre)))
-    rate_s[...] = rate
-    reff_s[...] = jnp.where(pos_ref[...] > 0.0, rate * LOG2E, RESET_RATE)
-    u_s[...] = rate * act_ref[...]
-    gate = gate_ref[...]
-    ds_s[...] = gg_ref[...] * (gate * jax.nn.sigmoid(gate))
+    total, rest = total_ref[...], rest_ref[...]
+    sel_t[:, : rows // 2] = jnp.where(first, total, rest)
+    sel_t[:, rows // 2 :] = jnp.where(first, rest, total)
+    rate_low[...] = sel_t[:rank_width, :].T.astype(BF16)
+    bb[...] = split_dot(sel_t[rank_width : rank_width + states, :], spread, TN)
+    cb[...] = split_dot(sel_t[rank_width + states :, :], spread, TN)
+    hist[0:SUBLANES, :] = jnp.zeros((SUBLANES, SIDE * wide), F32)
+    ci_acc[...] = jnp.zeros_like(ci_acc)
+    co_acc[...] = jnp.zeros_like(co_acc)
+    rank_t[...] = jnp.zeros_like(rank_t)
+    zero = jnp.zeros((8, lanes), F32)
+    sides = range(SIDE)
+    both = SIDE * lanes
 
     def cols(n):
         return slice(n * lanes, (n + 1) * lanes)
 
-    def forward(t, h):
-        row = pl.ds(pl.multiple_of(t * 8, 8), 8)
-        next_row = pl.ds(pl.multiple_of(t * 8 + 8, 8), 8)
-        reff = reff_s[row, :]
-        u = u_s[row, :]
-        y = jnp.zeros((8, lanes), F32)
-        fresh = []
+    def wide_cols(n, side):
+        return slice((n * SIDE + side) * lanes, (n * SIDE + side + 1) * lanes)
+
+    def side_cols(side):
+        return slice(side * lanes, (side + 1) * lanes)
+
+    def one_block(block, _):
+        at = pl.ds(pl.multiple_of(block * both, both), both)
+        decay = -jnp.exp(par_ref[decay_row : decay_row + states, at])
         for n in range(states):
-            a = jnp.exp2(reff * decb[8 * n : 8 * n + 8, :])
-            hn = a * h[n] + bb[row, cols(n)] * u
-            hist[next_row, cols(n)] = hn
-            fac[row, cols(n)] = a
-            y = y + cb[row, cols(n)] * hn
-            fresh.append(hn)
-        y_s[row, :] = y
-        return tuple(fresh)
-
-    zero = jnp.zeros((8, lanes), F32)
-    lax.fori_loop(0, steps, forward, (zero,) * states)
-
-    def backward(i, carried):
-        g, dacc = carried
-        t = steps - 1 - i
-        row = pl.ds(pl.multiple_of(t * 8, 8), 8)
-        next_row = pl.ds(pl.multiple_of(t * 8 + 8, 8), 8)
-        ds = ds_s[row, :]
-        u = u_s[row, :]
-        rt = rate_s[row, :]
-        s1 = jnp.zeros((8, lanes), F32)
-        s2 = jnp.zeros((8, lanes), F32)
-        g_new, d_new = [], []
-        for n in range(states):
-            lam = cb[row, cols(n)] * ds + g[n]
-            q = lam * fac[row, cols(n)]
-            hp = hist[row, cols(n)] * q
-            s1 = s1 + hp * decb[8 * n : 8 * n + 8, :]
-            s2 = s2 + lam * bb[row, cols(n)]
-            ci_acc[row, cols(n)] += lam * u
-            co_acc[row, cols(n)] += ds * hist[next_row, cols(n)]
-            g_new.append(q)
-            d_new.append(dacc[n] + hp * rt)
-        s2_s[row, :] = s2
-        reff_s[row, :] = s1
-        return tuple(g_new), tuple(d_new)
-
-    _, dacc = lax.fori_loop(0, steps, backward, ((zero,) * states, (zero,) * states))
-
-    act = act_ref[...]
-    skip = par_ref[skip_row : skip_row + 1, :]
-    scanned = y_s[...] + skip * act
-    sig = jax.nn.sigmoid(gate)
-    gated_ref[...] = (scanned * (gate * sig)).astype(BF16)
-    gateg_ref[...] = (gg_ref[...] * scanned * (sig * (1.0 + gate * (1.0 - sig)))).astype(BF16)
-    s2_all = s2_s[...]
-    dscan = ds_s[...]
-    sact_ref[...] = rate_s[...] * s2_all + skip * dscan
-    spre = (reff_s[...] + act * s2_all) * step_slope
-    spre_low = spre.astype(BF16)
-    sums = [jnp.sum(spre, axis=0, keepdims=True), jnp.sum(dscan * act, axis=0, keepdims=True)]
-    sums.append(jnp.zeros((6, lanes), F32))
-    for n in range(states):
-        sums.append(jnp.sum(dacc[n], axis=0, keepdims=True) * decb[8 * n : 8 * n + 1, :])
-    small_ref[: states + 8, :] = jnp.concatenate(sums, 0).astype(BF16)
-    small_ref[states + 8 :, :] = dot(
-        sel_t[:rank_width, :].astype(BF16), spre_low
-    ).astype(BF16)
-    rank_t[...] += dot(sw_ref[...], spre_low, NT)
-
-    @pl.when(block == pl.num_programs(0) - 1)
-    def _():
-        high, low = slice(0, rows // 2), slice(rows // 2, rows)
-        for acc, base in ((ci_acc, rank_width), (co_acc, rank_width + states)):
-            sums_t = split_dot(acc[...], spread, NT).T
-            sel_t[base : base + states, :] = sums_t
-        sel_t[:rank_width, :] = rank_t[...]
-        mine_ref[...] = jnp.where(first, sel_t[:, high], sel_t[:, low])
-        other_ref[...] = jnp.where(first, sel_t[:, low], sel_t[:, high])
+            decb[8 * n : 8 * n + 8, :] = jnp.broadcast_to(decay[n : n + 1, :], (8, both))
+        step_pre = dot(rate_low[...], sw_ref[:, at]) + par_ref[bias_row : bias_row + 1, at]
+        rate = jnp.maximum(step_pre, 0.0) + jnp.log1p(jnp.exp(-jnp.abs(step_pre)))
+        rate_s[...] = rate
+        for side in sides:
+            reff_s[:, side_cols(side)] = jnp.where(
+                pos_ref[...] > 0.0, rate[:, side_cols(side)] * LOG2E, RESET_RATE
+            )
+        u_s[...] = rate * act_ref[:, at]
+        slope_s[...] = jax.nn.sigmoid(step_pre)
+        gate = gate_ref[:, at]
+        ds_s[...] = gg_ref[:, at] * (gate * jax.nn.sigmoid(gate))
+
+        for group in range(states // GROUP):
+            names = range(group * GROUP, (group + 1) * GROUP)
+
+            def forward(t, h, names=names, group=group):
+                row = pl.ds(pl.multiple_of(t * 8, 8), 8)
+                next_row = pl.ds(pl.multiple_of(t * 8 + 8, 8), 8)
+                reff = [reff_s[row, side_cols(i)] for i in sides]
+                u = [u_s[row, side_cols(i)] for i in sides]
+                ds = [ds_s[row, side_cols(i)] for i in sides]
+                y = [zero if group == 0 else y_s[row, side_cols(i)] for i in sides]
+                fresh = []
+                for n in names:
+                    b, c = bb[row, cols(n)], cb[row, cols(n)]
+                    out = co_acc[row, cols(n)]
+                    for i in sides:
+                        a = jnp.exp2(reff[i] * decb[8 * n : 8 * n + 8, side_cols(i)])
+                        hn = a * h[len(fresh)] + b * u[i]
+                        hist[next_row, wide_cols(n, i)] = hn
+                        fac[row, wide_cols(n, i)] = a
+                        y[i] = y[i] + c * hn
+                        out = out + ds[i] * hn
+                        fresh.append(hn)
+                    co_acc[row, cols(n)] = out
+                for i in sides:
+                    y_s[row, side_cols(i)] = y[i]
+                return tuple(fresh)
+
+            lax.fori_loop(0, steps, forward, (zero,) * (GROUP * SIDE))
+
+        act = act_ref[:, at]
+        skip = par_ref[skip_row : skip_row + 1, at]
+        scanned = y_s[...] + skip * act
+        sig = jax.nn.sigmoid(gate)
+        gated_ref[:, at] = (scanned * (gate * sig)).astype(BF16)
+        gateg_ref[:, at] = (
+            gg_ref[:, at] * scanned * (sig * (1.0 + gate * (1.0 - sig)))
+        ).astype(BF16)
+
+        sums = []
+        for group in range(states // GROUP):
+            names = range(group * GROUP, (group + 1) * GROUP)
+
+            def backward(i, carried, names=names, group=group):
+                g, dacc = carried
+                t = steps - 1 - i
+                row = pl.ds(pl.multiple_of(t * 8, 8), 8)
+                ds = [ds_s[row, side_cols(k)] for k in sides]
+                u = [u_s[row, side_cols(k)] for k in sides]
+                rt = [rate_s[row, side_cols(k)] for k in sides]
+                s1 = [zero if group == 0 else reff_s[row, side_cols(k)] for k in sides]
+                s2 = [zero if group == 0 else s2_s[row, side_cols(k)] for k in sides]
+                g_new, d_new = [], []
+                for n in names:
+                    b, c = bb[row, cols(n)], cb[row, cols(n)]
+                    out = ci_acc[row, cols(n)]
+                    for k in sides:
+                        lam = c * ds[k] + g[len(g_new)]
+                        q = lam * fac[row, wide_cols(n, k)]
+                        hp = hist[row, wide_cols(n, k)] * q
+                        s1[k] = s1[k] + hp * decb[8 * n : 8 * n + 8, side_cols(k)]
+                        s2[k] = s2[k] + lam * b
+                        out = out + lam * u[k]
+                        d_new.append(dacc[len(g_new)] + hp * rt[k])
+                        g_new.append(q)
+                    ci_acc[row, cols(n)] = out
+                for k in sides:
+                    s2_s[row, side_cols(k)] = s2[k]
+                    reff_s[row, side_cols(k)] = s1[k]
+                return tuple(g_new), tuple(d_new)
+
+            none = (zero,) * (GROUP * SIDE)
+            _, dacc = lax.fori_loop(0, steps, backward, (none, none))
+            for n in range(GROUP):
+                row = jnp.concatenate(
+                    [jnp.sum(dacc[n * SIDE + k], axis=0, keepdims=True) for k in sides], 1
+                )
+                name = group * GROUP + n
+                sums.append(row * decb[8 * name : 8 * name + 1, :])
+
+        act = act_ref[:, at]
+        skip = par_ref[skip_row : skip_row + 1, at]
+        s2_all = s2_s[...]
+        dscan = ds_s[...]
+        sact_ref[:, at] = rate_s[...] * s2_all + skip * dscan
+        spre = (reff_s[...] + act * s2_all) * slope_s[...]
+        spre_low = spre.astype(BF16)
+        head = [jnp.sum(spre, axis=0, keepdims=True), jnp.sum(dscan * act, axis=0, keepdims=True)]
+        head.append(jnp.zeros((6, both), F32))
+        small_ref[: states + 8, at] = jnp.concatenate(head + sums, 0).astype(BF16)
+        small_ref[states + 8 :, at] = dot(
+            sel_t[:rank_width, :].astype(BF16), spre_low
+        ).astype(BF16)
+        rank_t[...] += dot(sw_ref[:, at], spre_low, NT)
+        return 0
+
+    lax.fori_loop(0, channels // both, one_block, 0)
+    high, low = slice(0, rows // 2), slice(rows // 2, rows)
+    for acc, base in ((ci_acc, rank_width), (co_acc, rank_width + states)):
+        sel_t[base : base + states, :] = split_dot(acc[...], spread, NT).T
+    sel_t[:rank_width, :] = rank_t[...]
+    mine_ref[...] = jnp.where(first, sel_t[:, high], sel_t[:, low])
+    other_ref[...] = jnp.where(first, sel_t[:, low], sel_t[:, high])
 
 
 def mixer(layout, core, position, act, gate, gated_grad, total, rest, step_w, params):
     rows, channels = act.shape
     rank_width, states = layout[:2]
-    lanes = LANES
     count = total.shape[0]
-
-    def block(height):
-        return pl.BlockSpec((height, lanes), lambda i: (0, i))
-
-    def fixed(*dims):
-        return pl.BlockSpec(dims, lambda i: (0, 0))
-
-    tall = block(rows)
-    wide = states * lanes
-    return pl.pallas_call(
-        partial(scan_kernel, layout),
-        grid=(channels // lanes,),
-        in_specs=[
-            pl.BlockSpec(memory_space=pltpu.SMEM), fixed(rows, lanes), tall, tall, tall,
-            fixed(count, rows // 2), fixed(count, rows // 2), block(rank_width),
-            block(params.shape[0]),
-        ],
-        out_specs=[
-            tall, tall, tall, block(rank_width + states + 8),
-            fixed(count, rows // 2), fixed(count, rows // 2),
-        ],
-        out_shape=[
+    wide = states * LANES
+    return whole(
+        partial(scan_kernel, layout), "mixer", [core],
+        (position, act, gate, gated_grad, total, rest, step_w, params),
+        [
             shape((rows, channels), BF16), shape((rows, channels), BF16),
             shape((rows, channels), F32), shape((rank_width + states + 8, channels), BF16),
             shape((count, rows // 2), F32), shape((count, rows // 2), F32),
         ],
-        scratch_shapes=[
-            pltpu.VMEM((rows, wide), F32),
-            pltpu.VMEM((rows, wide), F32),
-            pltpu.VMEM((rows + 8, wide), F32),
-            pltpu.VMEM((rows, wide), F32),
-            pltpu.VMEM((rows, wide), F32),
-            pltpu.VMEM((rows, wide), F32),
+        [
+            pltpu.VMEM((rows, wide), F32), pltpu.VMEM((rows, wide), F32),
+            pltpu.VMEM((rows + 8, SIDE * wide), F32), pltpu.VMEM((rows, SIDE * wide), F32),
+            pltpu.VMEM((rows, wide), F32), pltpu.VMEM((rows, wide), F32),
         ]
-        + [pltpu.VMEM((rows, lanes), F32)] * 6
+        + [pltpu.VMEM((rows, SIDE * LANES), F32)] * 7
         + [
-            pltpu.VMEM((8 * states, lanes), F32), pltpu.VMEM((count, rows), F32),
+            pltpu.VMEM((8 * states, SIDE * LANES), F32), pltpu.VMEM((count, rows), F32),
             pltpu.VMEM((rows, rank_width), BF16), pltpu.VMEM((rank_width, rows), F32),
         ],
-        compiler_params=pltpu.CompilerParams(
-            dimension_semantics=("arbitrary",), vmem_limit_bytes=48 << 20
-        ),
-        cost_estimate=pl.CostEstimate(
-            flops=20 * rows * channels * states,
-            bytes_accessed=30 * rows * channels,
-            transcendentals=rows * channels * states,
-        ),
-        name="mixer",
-    )(jnp.reshape(core, (1,)).astype(jnp.int32), position, act, gate, gated_grad, total, rest, step_w, params)
-
-
-def after(value, *others):
-    return lax.optimization_barrier((value, others))[0]
+        flops=20 * rows * channels * states,
+    )
+
+
+def step(*values):
+    return lax.optimization_barrier(values)
 
 
 def swap(value, axis, name="swap"):
@@ -636,45 +661,21 @@
         return lax.ppermute(value, axis, SWAP)
 
 
-def sum_zk(mine, other, fillers=()):
-    fillers = list(fillers) + [()] * 8
-    total = mine + after(swap(other, "k", "select"), fillers.pop(0))
-    first = None
+def exchange_z(value, distance, name):
     size = lax.axis_size("z")
-    distance = 1
-    while distance < size:
-        sent = total.astype(BF16)
-        got = lax.ppermute(sent, "z", [(i, i ^ distance) for i in range(size)])
-        total = sent.astype(F32) + after(got, fillers.pop(0)).astype(F32)
-        first = total if first is None else first
-        distance *= 2
-    return total, swap(total, "k", "select_rest"), first
-
-
-def return_core(mine, other):
-    return (mine.astype(F32) + swap(other, "k", "rows").astype(F32)).astype(BF16)
-
-
-def return_rows(total):
-    rows = lax.psum_scatter(total, "z", scatter_dimension=0, tiled=True)
-    share = rows.shape[0] // 2
-    near = jnp.concatenate([rows[:share], swap(rows[share:], "x", "rows")], 0)
-    return near, swap(near, "t", "rows")
-
-
-def exchange_halves(low, high):
-    low_x, high_t = swap(low, "x", "gate_w"), swap(high, "t", "outer_w")
-    low_t, high_x = swap(low, "t", "gate_w"), swap(high, "x", "outer_w")
-    low_d, high_d = swap(low_x, "t", "gate_w_far"), swap(high_t, "x", "outer_w_far")
-    return (low, low_x, low_t, low_d), (high, high_x, high_t, high_d)
-
-
-def exchange_weight(own):
-    half = own.shape[0] // 2
-    by_x = swap(own, "x", "stream_w")
-    by_t = swap(own, "t", "stream_w")
-    low = swap(by_x[:half], "t", "stream_w_far")
-    return own, by_x, by_t, low, swap(by_t[half:], "x", "stream_w_far")
+    with jax.named_scope(f"{name}_z"):
+        return lax.ppermute(value, "z", [(i, i ^ distance) for i in range(size)])
+
+
+def from_z(blocks, name):
+    size = lax.axis_size("z")
+    got = [blocks[0]]
+    for shift in range(1, size):
+        with jax.named_scope(f"{name}_z"):
+            got.append(
+                lax.ppermute(blocks[shift], "z", [(i, (i + shift) % size) for i in range(size)])
+            )
+    return got
 
 
 def plus(value, *more):
@@ -682,20 +683,6 @@
     for v in more:
         total = total + v.astype(F32)
     return total.astype(BF16)
-
-
-def diagonal_grads(low, high, name):
-    return swap(low[3], "x", name + "_far"), swap(high[3], "t", name + "_far")
-
-
-def first_grads(low, high, name):
-    return swap(low[1], "x", name), swap(high[2], "t", name)
-
-
-def second_grads(low, high, diagonal, name, ready=()):
-    low_t = swap(plus(low[2], after(diagonal[0], ready)), "t", name + "_sum")
-    high_x = swap(plus(high[1], after(diagonal[1], ready)), "x", name + "_sum")
-    return low_t, high_x
 
 
 def to_owners(value):
@@ -757,26 +744,6 @@
         first_pack_kernel, "pack", [zi, ki], (inner[:, 0], inner[:, 1], outer),
         [shape((blocks_w, ring_rows, part), BF16)] * 2,
     )
-    packed = whole(
-        second_pack_kernel, "pack_cores", [ki], (kept, swap(sent, "k", "weights")),
-        [shape((2 * ring_rows, part), BF16)] * blocks_w,
-    )
-
-    def from_z(blocks, name, ready=()):
-        blocks = after(blocks, ready)
-        got = [blocks[0]]
-        for step in range(1, zs):
-            with jax.named_scope(name):
-                got.append(
-                    lax.ppermute(blocks[step], "z", [(i, (i + step) % zs) for i in range(zs)])
-                )
-        return jnp.concatenate(got, 0)
-
-    stream_own = from_z(packed[:zs], "stream_w_z")
-    ws = exchange_weight(stream_own)
-    gate_own = from_z(packed[zs : 2 * zs], "gate_w_z", stream_own)
-    outer_own = from_z(packed[2 * zs :], "outer_w_z", gate_own)
-    wg, wo = exchange_halves(gate_own, outer_own)
 
     slot_rows = owner_slot.reshape(rings, members, local_rows)
     tok, cot = tokens, cotangent
@@ -828,13 +795,10 @@
     lengths = jnp.concatenate([lengths, jnp.zeros((1, ring_rows - lengths.shape[1]), BF16)], 1)
     note = jnp.concatenate([gain, lengths, jnp.zeros((share - 2, ring_rows), BF16)], 0)
     noted, plain = shape((share, width + LANES), BF16), shape((share, width), BF16)
+    blocks = step(kept, *blocks)[1:]
     rows_out = whole(
         prep_kernel, "prep", [xi], (send_place[None], *blocks, note), [noted, noted, plain, plain]
     )
-    group_tokens = lax.all_gather(
-        jnp.concatenate([rows_out[0], swap(rows_out[1], "x", "tokens")], 0), ZK, axis=0, tiled=True
-    )
-
     first = (zi * 2 + ki) * part
 
     def own_channels(value):
@@ -850,113 +814,169 @@
             axis=0,
         )
     )
-    params = jnp.concatenate([floats, swap(floats, "t", "params")], axis=1)
     layout = (rank_width, states, taps + 1, taps + 2, taps + 2 + states)
     select_t = lax.dynamic_slice_in_dim(select_weight, first, part, 0).T
     lows = jnp.concatenate([own_channels(step_weight), select_t], 0)
-    lows = jnp.concatenate([lows, swap(lows, "t", "params_low")], axis=1)
-    step_w, select_w = lows[:rank_width], lows[rank_width:]
-
-    count = select_w.shape[0]
+    count = select_t.shape[0]
     half_out = [shape((count, group_rows // 2), F32)] * 2
+    half_rows = [shape((group_rows // 2, width), BF16)] * 2
     full = shape((group_rows, channels), F32)
     wide_low = shape((group_rows, width), BF16)
+    half = depth // 2
+
+    def gathered(keep, send):
+        return lax.all_gather(jnp.concatenate([keep, send], 0), ZK, axis=0, tiled=True)
+
+    tok_keep, tok_send, cot_keep, cot_send = rows_out
+    (other_core,) = step(swap(sent, "k", "weights"))
+    packed = whole(
+        second_pack_kernel, "pack_cores", [ki], (kept, other_core),
+        [shape((2 * ring_rows, part), BF16)] * blocks_w,
+    )
+    tok_got = swap(tok_send, "x", "tokens")
+    group_tokens = gathered(tok_keep, tok_got)
+    stream_own, floats_t, lows_t, *packed = step(
+        jnp.concatenate(from_z(packed[:zs], "stream_w"), 0),
+        swap(floats, "t", "params"), swap(lows, "t", "params_low"), *packed[zs:],
+    )
+    stream_x, stream_t, gate_own, *packed = step(
+        swap(stream_own, "x", "stream_w"), swap(stream_own, "t", "stream_w"),
+        jnp.concatenate(from_z(packed[:zs], "gate_w"), 0), *packed[zs:],
+    )
+    params = jnp.concatenate([floats, floats_t], axis=1)
+    lows = jnp.concatenate([lows, lows_t], axis=1)
+    step_w, select_w = lows[:rank_width], lows[rank_width:]
+    stream_low, stream_high, outer_own, cot_got, gate_own, group_tokens = step(
+        swap(stream_x[:half], "t", "stream_w_far"), swap(stream_t[half:], "x", "stream_w_far"),
+        jnp.concatenate(from_z(packed, "outer_w"), 0), swap(cot_send, "x", "cot"),
+        gate_own, group_tokens,
+    )
+    ws = (stream_own, stream_x, stream_t, stream_low, stream_high)
+    group_cot = gathered(cot_keep, cot_got)
     normed, stream, act, sel_mine, sel_other, position, gain_row = whole(
         partial(front_kernel, (taps, sequence_lengths.shape[1])), "front", [ki, ti, zi],
-        (after(group_tokens, gate_own), arrived, *ws, params, select_w),
+        (group_tokens, arrived, *ws, params, select_w),
         [wide_low, full, full, *half_out, shape((group_rows, LANES), F32), shape((8, width), F32)],
         [pltpu.VMEM((group_rows, width), BF16), pltpu.VMEM((group_rows, channels), BF16)],
         flops=4 * group_rows * width * channels,
     )
-    total, rest, _ = sum_zk(sel_mine, sel_other, ((), outer_own, (wg[1], wg[2])))
-    cot_keep, cot_send = after((rows_out[2], rows_out[3]), gate_own)
-    group_cot = lax.all_gather(
-        jnp.concatenate([cot_keep, swap(cot_send, "x", "cot")], 0), ZK, axis=0, tiled=True
-    )
+    normed, stream, act, sel_mine, sel_other, gate_x, outer_t = step(
+        normed, stream, act, sel_mine, sel_other,
+        swap(gate_own, "x", "gate_w"), swap(outer_own, "t", "outer_w"),
+    )
+    sent = (sel_mine + swap(sel_other, "k", "select")).astype(BF16)
+    got, gate_t, outer_x, sent = step(
+        exchange_z(sent, 1, "select"), swap(gate_own, "t", "gate_w"),
+        swap(outer_own, "x", "outer_w"), sent,
+    )
+    sent = plus(sent, got)
+    got, gate_d, outer_d, sent = step(
+        exchange_z(sent, 2, "select"), swap(gate_x, "t", "gate_w_far"),
+        swap(outer_t, "x", "outer_w_far"), sent,
+    )
+    total = sent.astype(F32) + got.astype(F32)
+    wg, wo = (gate_own, gate_x, gate_t, gate_d), (outer_own, outer_x, outer_t, outer_d)
     upstream, gate, gated_grad = whole(
         late_kernel, "late", [zi], (group_cot, arrived, normed, *wg, *wo), [wide_low, full, full],
         flops=6 * group_rows * width * channels,
     )
+    rest = swap(total, "k", "select_rest")
     gated, gate_grad, act_grad, small_a, sel_mine, sel_other = mixer(
         layout, ki, position, act, gate, gated_grad, total, rest, step_w, params
     )
 
-    half_rows = [shape((group_rows // 2, width), BF16)] * 2
     out_mine, out_other = whole(
         out_kernel, "out_rows", [zi], (returned, gated, *wo), half_rows,
         flops=2 * group_rows * width * channels,
     )
+    got, out_mine, out_other, gated, gate_grad = step(
+        swap(sel_other, "k", "select"), out_mine, out_other, gated, gate_grad
+    )
+    sent = (sel_mine + got).astype(BF16)
     pieces = whole(
-        late_grad_kernel, "late_grad", [zi], (normed, upstream, after(gate_grad, out_mine), gated),
+        late_grad_kernel, "late_grad", [zi], (normed, upstream, gate_grad, gated),
         [shape((2 * zs, part, ring_rows), BF16)] * 8,
         flops=4 * group_rows * width * channels,
     )
-    late_diagonal = diagonal_grads(pieces[:4], pieces[4:], "late_g")
-    total, rest, first_sum = sum_zk(sel_mine, sel_other, (out_mine, pieces))
-    out_total = return_core(out_mine, out_other)
-    late_first = first_grads(
-        *after((pieces[:4], pieces[4:]), first_sum), "late_g"
-    )
-    near, far = return_rows(out_total)
-    total = after(total, late_diagonal, out_total)
-    back_place = send_place[:, None]
-    if rings > 1:
-        zero = jnp.zeros_like(tokens)
-        rows = whole(
-            output_kernel, "output", [xi], (back_place, near, far, zero), [shape(tokens.shape, BF16)]
-        )[0]
-        rows = from_blocks(over_rings(rows))
-        output = (tokens.astype(F32) + dot(ring_order, rows, TN)).astype(BF16)
-    else:
-        output = whole(
-            output_kernel, "output", [xi], (back_place, near, far, tokens), [shape(tokens.shape, BF16)]
-        )[0]
-    low, small_b, *stream_pieces = whole(
+    got, out_got, sent, *pieces = step(
+        exchange_z(sent, 1, "select"), swap(out_other, "k", "rows"), sent, *pieces
+    )
+    out_total = plus(out_mine, out_got)
+    gate_g, outer_g = pieces[:4], pieces[4:]
+    sent = plus(sent, got)
+    got, gate_far, outer_far, sent, out_total, *pieces = step(
+        exchange_z(sent, 2, "select"), swap(gate_g[3], "x", "gate_g_far"),
+        swap(outer_g[3], "t", "outer_g_far"), sent, out_total, *pieces,
+    )
+    gate_g, outer_g = pieces[:4], pieces[4:]
+    out_back = lax.psum_scatter(out_total, "z", scatter_dimension=0, tiled=True)
+    total = sent.astype(F32) + got.astype(F32)
+    rest = swap(total, "k", "select_rest")
+    low, small_b, *stream_g = whole(
         partial(back_kernel, taps), "back", [ki, zi],
         (total, rest, position, stream, act_grad, params, select_w, normed),
         [shape((group_rows, channels), BF16), shape((count + 8, channels), BF16)]
-        + [shape((2 * zs, part // 2, ring_rows), BF16)] * 8,
+        + [shape((2 * zs, part // 2, ring_rows), BF16)] * 4
+        + [shape((2, 2 * zs, part // 2, ring_rows), BF16)] * 2,
         [pltpu.VMEM((group_rows, channels), BF16), pltpu.VMEM((channels, group_rows), BF16)],
         flops=4 * group_rows * width * channels,
     )
+    small = jnp.concatenate([small_a, small_b], axis=0)
+    gate_first, outer_first, low, small_got, small, *stream_g = step(
+        swap(gate_g[1], "x", "gate_g"), swap(outer_g[2], "t", "outer_g"), low,
+        swap(small[:, part:], "t", "small"), small, *stream_g,
+    )
+    small = plus(small[:, :part], small_got)
     in_mine, in_other = whole(
         in_kernel, "in_rows", [zi], (returned, low, gate_grad, *ws, *wg),
         half_rows, [pltpu.VMEM((group_rows, 2 * channels), BF16)],
         flops=4 * group_rows * width * channels,
     )
-    in_total = return_core(in_mine, in_other)
-    late_second = second_grads(pieces[:4], pieces[4:], late_diagonal, "late_g")
-    sides = after((stream_pieces[::2], stream_pieces[1::2]), in_total)
-    stream_diagonal = diagonal_grads(*sides, "stream_g")
-    stream_first = first_grads(*sides, "stream_g")
-    stream_second = second_grads(*sides, stream_diagonal, "stream_g")
+    in_total = plus(in_mine, swap(in_other, "k", "rows"))
+    in_back = lax.psum_scatter(in_total, "z", scatter_dimension=0, tiled=True)
+    gate_second, outer_second, small_got, small, _ = step(
+        swap(plus(gate_g[2], gate_far), "t", "gate_g_sum"),
+        swap(plus(outer_g[1], outer_far), "x", "outer_g_sum"),
+        swap(small, "x", "small"), small, in_total,
+    )
+    small = plus(small, small_got)
     late_sum = jnp.concatenate(
-        [
-            plus(pieces[0], late_first[0], late_second[0]),
-            plus(pieces[4], late_first[1], late_second[1]),
-        ],
+        [plus(gate_g[0], gate_first, gate_second), plus(outer_g[0], outer_first, outer_second)],
         axis=1,
     )
     late_home = to_owners(late_sum)
-    gate_home, outer_home = late_home[:, :part], late_home[:, part:]
-    outer_home = outer_home.reshape(half_channels, ring_rows).astype(F32)
+    own_low, own_high, by_x_high, by_t_low, x_way, t_way = stream_g
+    def near_rows(rows):
+        return jnp.concatenate([rows[:share], swap(rows[share:], "x", "rows")], 0)
+
+    x_way, t_way, small, out_near = step(
+        swap(x_way, "x", "stream_g"), swap(t_way, "t", "stream_g"), small, near_rows(out_back),
+    )
     if rings > 1:
-        outer_home = lax.psum_scatter(outer_home, "r", scatter_dimension=1, tiled=True)
+        small = lax.psum(small.astype(F32), "r").astype(BF16)
+    low_second, high_second, out_far, out_near, in_back, late_home, *gathered_small = step(
+        swap(plus(by_t_low, x_way[0]), "t", "stream_g_sum"),
+        swap(plus(by_x_high, t_way[0]), "x", "stream_g_sum"),
+        swap(out_near, "t", "rows"), out_near, in_back, late_home, *from_z([small] * zs, "small"),
+    )
     stream_sum = jnp.concatenate(
-        [
-            plus(sides[0][0], stream_first[0], stream_second[0]),
-            plus(sides[1][0], stream_first[1], stream_second[1]),
-        ],
-        axis=1,
-    )
-    stream_home = to_owners(after(stream_sum, late_home))
-    near, far = return_rows(in_total)
+        [plus(own_low, x_way[1], low_second), plus(own_high, t_way[1], high_second)], axis=1
+    )
+    stream_home, in_near = step(to_owners(stream_sum), near_rows(in_back))
+    in_far = swap(in_near, "t", "rows")
+    small_blocks = [v for block in gathered_small for v in (block, swap(block, "k", "small"))]
+
+    back_place = send_place[:, None]
     if rings > 1:
-        zero = jnp.zeros_like(tokens)
-        rows = whole(
-            output_kernel, "rows_back", [xi], (back_place, near, far, zero), [shape(tokens.shape, BF16)]
-        )[0]
-        rows = dot(ring_order, from_blocks(over_rings(rows)), TN)
+        def own_rows(near, far, name):
+            rows = whole(
+                output_kernel, name, [xi], (back_place, near, far, jnp.zeros_like(tokens)),
+                [shape(tokens.shape, BF16)],
+            )[0]
+            return dot(ring_order, from_blocks(over_rings(rows)), TN)
+
+        output = (tokens.astype(F32) + own_rows(out_near, out_far, "output")).astype(BF16)
+        rows = own_rows(in_near, in_far, "rows_back")
         own_x = tokens.astype(F32)
         inverse = lax.rsqrt(jnp.mean(own_x * own_x, axis=1, keepdims=True) + EPSILON)
         hat = own_x * inverse
@@ -967,40 +987,34 @@
             grad - hat * jnp.mean(grad * hat, axis=1, keepdims=True)
         )
     else:
+        output = whole(
+            output_kernel, "output", [xi], (back_place, out_near, out_far, tokens),
+            [shape(tokens.shape, BF16)],
+        )[0]
         input_grad = whole(
             input_kernel, "input_grad", [xi],
-            (back_place, near, far, tokens, cotangent, gain_row), [shape(tokens.shape, F32)],
+            (back_place, in_near, in_far, tokens, cotangent, gain_row),
+            [shape(tokens.shape, F32)],
         )[0]
-    inner_home = jnp.stack(
-        [v.reshape(half_channels, ring_rows).T for v in (stream_home, gate_home)], axis=1
-    ).astype(F32)
-    if rings > 1:
-        inner_home = lax.psum_scatter(inner_home, "r", scatter_dimension=0, tiled=True)
-    gain_grad = jnp.sum(inner_home * inner_weight.astype(F32), axis=(1, 2))
-    gain_grad = (gain_grad + swap(gain_grad, "t", "gain")) / norm_gain.astype(F32)
-
-    small = after(jnp.concatenate([small_a, small_b], axis=0), stream_diagonal)
-    small = plus(small[:, :part], swap(small[:, part:], "t", "small"))
-    small = after(small, late_second)
-    small = plus(small, swap(small, "x", "small"))
-    if rings > 1:
-        small = lax.psum(small.astype(F32), "r").astype(BF16)
-    gathered = []
-    for step in range(zs):
-        with jax.named_scope("small_z"):
-            block = small if step == 0 else lax.ppermute(
-                small, "z", [(i, (i + step) % zs) for i in range(zs)]
-            )
-        gathered += [block, swap(block, "k", "small")]
     one_row = shape((1, half_channels), F32)
     select_grad, step_w_grad, decay_grad, filter_grad, filter_b_grad, step_b_grad, skip_grad = whole(
-        partial(small_kernel, (count, states, taps)), "small", [zi, ki], gathered,
+        partial(small_kernel, (count, states, taps)), "small", [zi, ki], small_blocks,
         [
             shape((half_channels, count), F32), shape((rank_width, half_channels), F32),
             shape((states, half_channels), F32), shape((taps, half_channels), F32),
             one_row, one_row, one_row,
         ],
     )
+    gate_home, outer_home = late_home[:, :part], late_home[:, part:]
+    outer_home = outer_home.reshape(half_channels, ring_rows).astype(F32)
+    inner_home = jnp.stack(
+        [v.reshape(half_channels, ring_rows).T for v in (stream_home, gate_home)], axis=1
+    ).astype(F32)
+    if rings > 1:
+        outer_home = lax.psum_scatter(outer_home, "r", scatter_dimension=1, tiled=True)
+        inner_home = lax.psum_scatter(inner_home, "r", scatter_dimension=0, tiled=True)
+    gain_grad = jnp.sum(inner_home * inner_weight.astype(F32), axis=(1, 2))
+    gain_grad = (gain_grad + swap(gain_grad, "t", "gain")) / norm_gain.astype(F32)
     return (
         output,
         input_grad,

time: 386 us -> 359 us (0.930)
  local copies, waits for them, and re-layouts: 53.9 us -> 23.2 us
  Pallas kernels: 64.8 us -> 87.2 us
  starting transfers between devices: 88.8 us -> 78.3 us
  waiting for transfers between devices: 136 us -> 127 us
    pallas_call x12 -> x13, Pallas kernels: 36.1 us -> 87.2 us  [whole(): pl.pallas_call(copied, in_specs=[pl.BlockSpec(memory_space=pltpu.SMEM)] *...]
    unnamed x205 -> x121, local copies, waits for them, and re-layouts: 45 us -> 15.3 us
    pallas_call x1 -> x0, Pallas kernels: 28.6 us -> none  [mixer(): pl.pallas_call(partial(scan_kernel, layout), grid=(channels // lanes,), i...]
    ppermute x44 -> x42, waiting for transfers between devices: 80.1 us -> 61.7 us  [swap(): return lax.ppermute(value, axis, SWAP)]
    ppermute x16, waiting for transfers between devices: 55.9 us -> 65.3 us  [the longest x12 59.3 us: from_z(): lax.ppermute(blocks[shift], 'z', [(i, (i + shift) % size) for i in range(...]
    ppermute x16, starting transfers between devices: 39.8 us -> 31.3 us  [the longest x12 23.5 us: from_z(): lax.ppermute(blocks[shift], 'z', [(i, (i + shift) % size) for i in range(...]
    ppermute x44 -> x42, starting transfers between devices: 39.6 us -> 37.7 us  [swap(): return lax.ppermute(value, axis, SWAP)]
  transfers between devices with their start and end apart: 66 -> 64, of which waited for: 30 -> 27; matrix products, arithmetic and copies ran while one was open for 8% -> 7% of each run, Pallas kernels for 9% -> 14%
where the time goes in v2:
time: 359 us; the launch traced here: 354 us
  waiting for transfers between devices  127 us (35%)
  Pallas kernels  87.2 us (24%)
  starting transfers between devices  78.3 us (22%)
  local copies, waits for them, and re-layouts  23.2 us (6%)
  other arithmetic  22.7 us (6%)
  between operations  15.2 us (4%)
    pallas_call x13, Pallas kernels, whole(): pl.pallas_call(copied, in_specs=[pl.BlockSpec(memory_space=pltpu.SMEM)] *...  87.2 us
    ppermute x42, waiting for transfers between devices, swap(): return lax.ppermute(value, axis, SWAP)  61.7 us
    ppermute x12, waiting for transfers between devices, from_z(): lax.ppermute(blocks[shift], 'z', [(i, (i + shift) % size) for i in range(...  59.3 us
    ppermute x42, starting transfers between devices, swap(): return lax.ppermute(value, axis, SWAP)  37.7 us
    ppermute x12, starting transfers between devices, from_z(): lax.ppermute(blocks[shift], 'z', [(i, (i + shift) % size) for i in range(...  23.5 us
    unnamed x121, local copies, waits for them, and re-layouts  15.3 us
    all_to_all x2, starting transfers between devices, to_owners(): return lax.all_to_all(value, ZK, 0, 0, tiled=True)  8.46 us
    ppermute x4, starting transfers between devices, exchange_z(): return lax.ppermute(value, 'z', [(i, i ^ distance) for i in range(size)])  7.83 us
  transfers between devices with their start and end apart: 64, of which 27 were waited for; matrix products, arithmetic and copies ran while one was open for 7% of the time, Pallas kernels for 14%

profile of v2, /device:TPU:0, one launch (start us, length us, event | category | flops | bytes accessed | tf_op | source)
XLA Modules:
  0.0 354.2 jit_solution(7978575012486193088)
XLA Ops:
  22.5 3.9 %collective-permute-done.17 = bf16[32,2176]{1,0:T(8,128)(2,1)S(1)} collective-permute-done((bf16[32,2176]{1,0:T(8,128)(2,1)}, bf16[32,2176]{1,0:T(8,128)(2,1)S(1)}, u32[]{:S(2)}, u32[]{:S(2)}) %collective-permute-start.17) | collective-permute-done | bytes 139296 | tf_op jit(solution)/shard_map/tokens_x/ppermute | solution.py:661
  34.2 3.9 %collective-permute-start.3 = (bf16[256,256]{1,0:T(8,128)(2,1)}, bf16[256,256]{1,0:T(8,128)(2,1)S(1)}, u32[]{:S(2)}, u32[]{:S(2)}) collective-permute-start(bf16[256,256]{1,0:T(8,128)(2,1)} %get-tuple-element.177), channel_id=1, source_target_pairs={{0,24},{8,0},{16,8},{24,16},{1,25},{9,1},{17,9},{25,17},{2,26},{10... | collective-permute-start | bytes 393224 | tf_op jit(solution)/shard_map/stream_w_z/ppermute | solution.py:676
  45.0 13.2 %collective-permute-done.2 = bf16[256,256]{1,0:T(8,128)(2,1)S(1)} collective-permute-done((bf16[256,256]{1,0:T(8,128)(2,1)}, bf16[256,256]{1,0:T(8,128)(2,1)S(1)}, u32[]{:S(2)}, u32[]{:S(2)}) %collective-permute-start.2) | collective-permute-done | bytes 131104 | tf_op jit(solution)/shard_map/stream_w_z/ppermute | solution.py:676
  62.8 10.0 %collective-permute-start.9 = (bf16[256,256]{1,0:T(8,128)(2,1)}, bf16[256,256]{1,0:T(8,128)(2,1)S(1)}, u32[]{:S(2)}, u32[]{:S(2)}) collective-permute-start(bf16[256,256]{1,0:T(8,128)(2,1)} %get-tuple-element.189), channel_id=1, source_target_pairs={{0,16},{8,24},{16,0},{24,8},{1,17},{9,25},{17,1},{25,9},{2,18},{10... | collective-permute-start | bytes 393224 | tf_op jit(solution)/shard_map/gate_w_z/ppermute | solution.py:676
  74.8 8.2 %collective-permute-done.9 = bf16[256,256]{1,0:T(8,128)(2,1)S(1)} collective-permute-done((bf16[256,256]{1,0:T(8,128)(2,1)}, bf16[256,256]{1,0:T(8,128)(2,1)S(1)}, u32[]{:S(2)}, u32[]{:S(2)}) %collective-permute-start.9) | collective-permute-done | bytes 131104 | tf_op jit(solution)/shard_map/gate_w_z/ppermute | solution.py:676
  105.3 8.0 %front.1 = (bf16[512,2048]{1,0:T(8,128)(2,1)}, f32[512,512]{1,0:T(8,128)}, f32[512,512]{1,0:T(8,128)}, f32[160,256]{1,0:T(8,128)}, f32[160,256]{1,0:T(8,128)}, /*index=5*/f32[512,128]{1,0:T(8,128)}, f32[8,2048]{1,0:T(8,128)}) custom-call(s32[1]{0:T(128)} %bitcast.3.refs_1_.refs_0_, s32[1]{0:T(128)} %bitcast.4.refs_1_, s32[1]{0:T(128)} %bitcast.5.refs_0_.refs_2_.refs_1_, ...), custom_call_target="tpu_custom_call" | custom-call | flops 2147483648 | bytes 9390080 | tf_op jit(solution)/shard_map/front/pallas_call | solution.py:69
  121.4 5.6 %collective-permute-done.22.refs_6_.refs_11_ = bf16[1024,256]{1,0:T(8,128)(2,1)S(1)} collective-permute-done((bf16[1024,256]{1,0:T(8,128)(2,1)S(1)}, bf16[1024,256]{1,0:T(8,128)(2,1)S(1)}, u32[]{:S(2)}, u32[]{:S(2)}) %collective-permute-start.22) | collective-permute-done | bytes 524320 | tf_op jit(solution)/shard_map/gate_w_t/ppermute | solution.py:661
  128.8 4.5 %collective-permute-done.24 = bf16[160,256]{1,0:T(8,128)(2,1)S(1)} collective-permute-done((bf16[160,256]{1,0:T(8,128)(2,1)S(1)}, bf16[160,256]{1,0:T(8,128)(2,1)S(1)}, u32[]{:S(2)}, u32[]{:S(2)}) %collective-permute-start.24) | collective-permute-done | bytes 81952 | tf_op jit(solution)/shard_map/select_z/ppermute | solution.py:667
  135.5 8.0 %late.1 = (bf16[512,2048]{1,0:T(8,128)(2,1)}, f32[512,512]{1,0:T(8,128)}, f32[512,512]{1,0:T(8,128)}) custom-call(s32[1]{0:T(128)} %bitcast.5.refs_0_.refs_2_.refs_1_, bf16[512,2048]{1,0:T(8,128)(2,1)} %all-gather.5.cloned.1.call-done.refs_1_, s32[1,512]{1,0:T(1,128)} %reshape.372.refs_4_.refs_2_, ...), custom_call_target="tpu_custom_call" | custom-call | flops 3221225472 | bytes 12584960 | tf_op jit(solution)/shard_map/late/pallas_call | solution.py:69
  144.2 29.0 %mixer.1 = (bf16[512,512]{1,0:T(8,128)(2,1)}, bf16[512,512]{1,0:T(8,128)(2,1)}, f32[512,512]{1,0:T(8,128)}, bf16[152,512]{1,0:T(8,128)(2,1)}, f32[160,256]{1,0:T(8,128)}, /*index=5*/f32[160,256]{1,0:T(8,128)}) custom-call(s32[1]{0:T(128)} %bitcast.3.refs_1_.refs_0_, f32[512,128]{1,0:T(8,128)} %get-tuple-element.212.refs_1_.refs_4_, ...), custom_call_target="tpu_custom_call" | custom-call | flops 83886080 | bytes 6496256 | tf_op jit(solution)/shard_map/mixer/pallas_call | solution.py:69
  174.2 4.6 %out_rows.1 = (bf16[256,2048]{1,0:T(8,128)(2,1)}, bf16[256,2048]{1,0:T(8,128)(2,1)}) custom-call(s32[1]{0:T(128)} %bitcast.5.refs_0_.refs_2_.refs_1_, s32[512,1]{1,0:T(8,128)} %reshape.381.refs_1_, bf16[512,512]{1,0:T(8,128)(2,1)} %get-tuple-element.248.refs_2_.refs_4_, bf16[1024,256]{1,0:T(8,128)(2,1)} %copy-done.15, ...), custom_call_target="tpu_custom_call" | custom-call | flops 1073741824 | bytes 4720640 | tf_op jit(solution)/shard_map/out_rows/pallas_call | solution.py:69
  181.2 6.1 %late_grad.1 = (bf16[8,256,128]{2,1,0:T(8,128)(2,1)}, bf16[8,256,128]{2,1,0:T(8,128)(2,1)}, bf16[8,256,128]{2,1,0:T(8,128)(2,1)}, bf16[8,256,128]{2,1,0:T(8,128)...) custom-call(s32[1]{0:T(128)} %bitcast.5.refs_0_.refs_2_.refs_1_, ...), custom_call_target="tpu_custom_call" | custom-call | flops 2147483648 | bytes 9437184 | tf_op jit(solution)/shard_map/late_grad/pallas_call | solution.py:69
  194.2 9.0 %collective-permute-done.32 = bf16[8,256,128]{2,1,0:T(8,128)(2,1)S(1)} collective-permute-done((bf16[8,256,128]{2,1,0:T(8,128)(2,1)}, bf16[8,256,128]{2,1,0:T(8,128)(2,1)S(1)}, u32[]{:S(2)}, u32[]{:S(2)}) %collective-permute-start.32) | collective-permute-done | bytes 524320 | tf_op jit(solution)/shard_map/gate_g_far_x/ppermute | solution.py:661
  206.7 6.9 %back.1 = (bf16[512,512]{1,0:T(8,128)(2,1)}, bf16[168,512]{1,0:T(8,128)(2,1)}, bf16[8,128,128]{2,1,0:T(8,128)(2,1)}, bf16[8,128,128]{2,1,0:T(8,128)(2,1)}, bf16[...) custom-call(s32[1]{0:T(128)} %bitcast.3.refs_1_.refs_0_, ...), custom_call_target="tpu_custom_call" | custom-call | flops 2147483648 | bytes 7790592 | tf_op jit(solution)/shard_map/back/pallas_call | solution.py:69
  216.0 6.8 %collective-permute-done.37 = bf16[320,256]{1,0:T(8,128)(2,1)S(1)} collective-permute-done((bf16[320,256]{1,0:T(8,128)(2,1)S(1)}, bf16[320,256]{1,0:T(8,128)(2,1)S(1)}, u32[]{:S(2)}, u32[]{:S(2)}) %collective-permute-start.37) | collective-permute-done | bytes 163872 | tf_op jit(solution)/shard_map/small_t/ppermute | solution.py:661
  222.9 7.1 %in_rows.1 = (bf16[256,2048]{1,0:T(8,128)(2,1)}, bf16[256,2048]{1,0:T(8,128)(2,1)}) custom-call(s32[1]{0:T(128)} %bitcast.5.refs_0_.refs_2_.refs_1_, s32[512,1]{1,0:T(8,128)} %reshape.381.refs_1_, bf16[512,512]{1,0:T(8,128)(2,1)} %get-tuple-element.293.refs_2_, bf16[512,512]{1,0:T(8,128)(2,1)} %get-tuple-element.247.refs_3_, bf16[1024,256]{1,0:T(8,128)(2,1)} %copy-done.13, ...), custom_call_target="tpu_custom_call" | custom-call | flops 2147483648 | bytes 7342080 | tf_op jit(solution)/shard_map/in_rows/pallas_call | solution.py:69
  234.3 10.4 %collective-permute-done.40 = bf16[8,256,128]{2,1,0:T(8,128)(2,1)} collective-permute-done((bf16[8,256,128]{2,1,0:T(8,128)(2,1)S(1)}, bf16[8,256,128]{2,1,0:T(8,128)(2,1)}, u32[]{:S(2)}, u32[]{:S(2)}) %collective-permute-start.40) | collective-permute-done | bytes 524320 | tf_op jit(solution)/shard_map/gate_g_sum_t/ppermute | solution.py:661
  251.2 3.7 %all-to-all-start = ((bf16[8,512,128]{2,1,0:T(8,128)(2,1)}), bf16[8,512,128]{2,1,0:T(8,128)(2,1)S(1)}, u32[]{:S(2)}, u32[]{:S(2)}) async-start(bf16[8,512,128]{2,1,0:T(8,128)(2,1)} %pad_maximum_fusion), calls=%async_computation.2 | async-start | bytes 2097152 | tf_op jit(solution)/shard_map/all_to_all | solution.py:689
  259.8 12.3 %collective-permute-done.44 = bf16[32,2048]{1,0:T(8,128)(2,1)S(1)} collective-permute-done((bf16[32,2048]{1,0:T(8,128)(2,1)S(1)}, bf16[32,2048]{1,0:T(8,128)(2,1)S(1)}, u32[]{:S(2)}, u32[]{:S(2)}) %collective-permute-start.44) | collective-permute-done | bytes 131104 | tf_op jit(solution)/shard_map/rows_x/ppermute | solution.py:661
  280.3 15.2 %collective-permute-done.48.refs_4_ = bf16[320,256]{1,0:T(8,128)(2,1)S(1)} collective-permute-done((bf16[320,256]{1,0:T(8,128)(2,1)S(1)}, bf16[320,256]{1,0:T(8,128)(2,1)S(1)}, u32[]{:S(2)}, u32[]{:S(2)}) %collective-permute-start.48) | collective-permute-done | bytes 163872 | tf_op jit(solution)/shard_map/small_z/ppermute | solution.py:676
  296.2 10.9 %collective-permute-done.49.refs_6_ = bf16[320,256]{1,0:T(8,128)(2,1)} collective-permute-done((bf16[320,256]{1,0:T(8,128)(2,1)S(1)}, bf16[320,256]{1,0:T(8,128)(2,1)}, u32[]{:S(2)}, u32[]{:S(2)}) %collective-permute-start.49) | collective-permute-done | bytes 163872 | tf_op jit(solution)/shard_map/small_z/ppermute | solution.py:676
  314.5 4.8 %all-to-all-start.1 = ((bf16[8,256,128]{2,1,0:T(8,128)(2,1)}), bf16[8,256,128]{2,1,0:T(8,128)(2,1)S(1)}, u32[]{:S(2)}, u32[]{:S(2)}) async-start(bf16[8,256,128]{2,1,0:T(8,128)(2,1)} %pad_maximum_fusion.4), calls=%async_computation.3 | async-start | bytes 1048576 | tf_op jit(solution)/shard_map/all_to_all | solution.py:689
  327.8 3.6 %small.1 = (f32[2048,160]{1,0:T(8,128)}, f32[128,2048]{1,0:T(8,128)}, f32[16,2048]{1,0:T(8,128)}, f32[4,2048]{1,0:T(4,128)}, f32[1,2048]{1,0:T(1,128)}, /*index=5*/f32[1,2048]{1,0:T(1,128)}, f32[1,2048]{1,0:T(1,128)}) custom-call(s32[1]{0:T(128)} %bitcast.5.refs_0_.refs_2_.refs_1_, s32[1]{0:T(128)} %bitcast.3.refs_1_.refs_0_, bf16[320,256]{1,0:T(8,128)(2,1)} %copy-done.9, ...), custom_call_target="tpu_custom_call" | custom-call | bytes 3858432 | tf_op jit(solution)/shard_map/small/pallas_call | solution.py:69
  343.9 3.5 input_grad.1
  (311 shorter events, 139.9 us)
Async XLA Ops:
  7.2 89.6 %all-gather.3.cloned.1.call-start = ((), (), s32[]{:S(2)}) async-start(), calls=%async_computation.4 | async-start | bytes 2506752 | tf_op jit(solution)/shard_map/all_gather | solution.py:828
  28.0 106.6 %all-gather.5.cloned.1.call-start = ((), (), s32[]{:S(2)}) async-start(), calls=%async_computation.5 | async-start | bytes 2359296 | tf_op jit(solution)/shard_map/all_gather | solution.py:828
  38.1 20.1 %collective-permute-start.2 = (bf16[256,256]{1,0:T(8,128)(2,1)}, bf16[256,256]{1,0:T(8,128)(2,1)S(1)}, u32[]{:S(2)}, u32[]{:S(2)}) collective-permute-start(bf16[256,256]{1,0:T(8,128)(2,1)} %get-tuple-element.176), channel_id=1, source_target_pairs={{0,16},{8,24},{16,0},{24,8},{1,17},{9,25},{17,1},{25,9},{2,18},{10... | collective-permute-start | bytes 393224 | tf_op jit(solution)/shard_map/stream_w_z/ppermute | solution.py:676
  38.1 20.1 %collective-permute-start.1 = (bf16[256,256]{1,0:T(8,128)(2,1)}, bf16[256,256]{1,0:T(8,128)(2,1)S(1)}, u32[]{:S(2)}, u32[]{:S(2)}) collective-permute-start(bf16[256,256]{1,0:T(8,128)(2,1)} %get-tuple-element.175), channel_id=1, source_target_pairs={{0,8},{8,16},{16,24},{24,0},{1,9},{9,17},{17,25},{25,1},{2,10},{10... | collective-permute-start | bytes 393224 | tf_op jit(solution)/shard_map/stream_w_z/ppermute | solution.py:676
  39.1 20.1 %collective-permute-start.5 = (bf16[288,256]{1,0:T(8,128)(2,1)S(1)}, bf16[288,256]{1,0:T(8,128)(2,1)S(1)}, u32[]{:S(2)}, u32[]{:S(2)}) collective-permute-start(bf16[288,256]{1,0:T(8,128)(2,1)S(1)} %pad_maximum_fusion.10), channel_id=1, source_target_pairs={{0,1},{1,0},{2,3},{3,2},{4,5},{5,4},{6,7},{7,6},{8,9},{9,8},{10,11... | collective-permute-start | bytes 442376 | tf_op jit(solution)/shard_map/params_low_t/ppermute | solution.py:661
  41.1 18.2 %collective-permute-start.4 = (f32[24,256]{1,0:T(8,128)S(1)}, f32[24,256]{1,0:T(8,128)S(1)}, u32[]{:S(2)}, u32[]{:S(2)}) collective-permute-start(f32[24,256]{1,0:T(8,128)S(1)} %constant_dynamic-slice_fusion.1), channel_id=1, source_target_pairs={{0,1},{1,0},{2,3},{3,2},{4,5},{5,4},{6,7},{7,6},{8,9},{9,8},{10,11... | collective-permute-start | bytes 73736 | tf_op jit(solution)/shard_map/params_t/ppermute | solution.py:661
  59.3 24.6 %collective-permute-start.6 = (bf16[1024,256]{1,0:T(8,128)(2,1)S(1)}, bf16[1024,256]{1,0:T(8,128)(2,1)S(1)}, u32[]{:S(2)}, u32[]{:S(2)}) collective-permute-start(bf16[1024,256]{1,0:T(8,128)(2,1)S(1)} %pad_maximum_fusion.1.refs_5_.refs_4_), channel_id=1, source_target_pairs={{0,4},{4,0},{1,5},{5,1},{2,6},{6,2},{3,7},{7,3},{8,12},{12,8},{9,1... | collective-permute-start | bytes 1572872 | tf_op jit(solution)/shard_map/stream_w_x/ppermute | solution.py:661
  61.1 22.8 %collective-permute-start.7 = (bf16[1024,256]{1,0:T(8,128)(2,1)S(1)}, bf16[1024,256]{1,0:T(8,128)(2,1)S(1)}, u32[]{:S(2)}, u32[]{:S(2)}) collective-permute-start(bf16[1024,256]{1,0:T(8,128)(2,1)S(1)} %pad_maximum_fusion.1.refs_5_.refs_4_), channel_id=1, source_target_pairs={{0,1},{1,0},{2,3},{3,2},{4,5},{5,4},{6,7},{7,6},{8,9},{9,8},{10,11... | collective-permute-start | bytes 1572872 | tf_op jit(solution)/shard_map/stream_w_t/ppermute | solution.py:661
  62.8 20.1 %collective-permute-start.9 = (bf16[256,256]{1,0:T(8,128)(2,1)}, bf16[256,256]{1,0:T(8,128)(2,1)S(1)}, u32[]{:S(2)}, u32[]{:S(2)}) collective-permute-start(bf16[256,256]{1,0:T(8,128)(2,1)} %get-tuple-element.189), channel_id=1, source_target_pairs={{0,16},{8,24},{16,0},{24,8},{1,17},{9,25},{17,1},{25,9},{2,18},{10... | collective-permute-start | bytes 393224 | tf_op jit(solution)/shard_map/gate_w_z/ppermute | solution.py:676
  97.5 160.9 %reduce-scatter.3.cloned.1.call-start = ((), (), s32[]{:S(2)}) async-start(), calls=%async_computation.6 | async-start | bytes 1310720 | tf_op jit(solution)/shard_map/reduce_scatter | solution.py:912
  102.9 24.1 %collective-permute-start.22 = (bf16[1024,256]{1,0:T(8,128)(2,1)S(1)}, bf16[1024,256]{1,0:T(8,128)(2,1)S(1)}, u32[]{:S(2)}, u32[]{:S(2)}) collective-permute-start(bf16[1024,256]{1,0:T(8,128)(2,1)S(1)} %pad_maximum_fusion.2.refs_4_.refs_9_), channel_id=1, source_target_pairs={{0,1},{1,0},{2,3},{3,2},{4,5},{5,4},{6,7},{7,6},{8,9},{9,8},{10,11... | collective-permute-start | bytes 1572872 | tf_op jit(solution)/shard_map/gate_w_t/ppermute | solution.py:661
  104.9 22.1 %collective-permute-start.23 = (bf16[1024,256]{1,0:T(8,128)(2,1)S(1)}, bf16[1024,256]{1,0:T(8,128)(2,1)}, u32[]{:S(2)}, u32[]{:S(2)}) collective-permute-start(bf16[1024,256]{1,0:T(8,128)(2,1)S(1)} %pad_maximum_fusion.3.refs_8_.refs_3_), channel_id=1, source_target_pairs={{0,4},{4,0},{1,5},{5,1},{2,6},{6,2},{3,7},{7,3},{8,12},{12,8},{9,1... | collective-permute-start | bytes 1572872 | tf_op jit(solution)/shard_map/outer_w_x/ppermute | solution.py:661
  115.9 18.6 %collective-permute-start.25 = (bf16[1024,256]{1,0:T(8,128)(2,1)}, bf16[1024,256]{1,0:T(8,128)(2,1)S(1)}, u32[]{:S(2)}, u32[]{:S(2)}) collective-permute-start(bf16[1024,256]{1,0:T(8,128)(2,1)} %collective-permute-done.18.refs_5_.refs_10_), channel_id=1, source_target_pairs={{0,1},{1,0},{2,3},{3,2},{4,5},{5,4},{6,7},{7,6},{8,9},{9,8},{10,11... | collective-permute-start | bytes 1572872 | tf_op jit(solution)/shard_map/gate_w_far_t/ppermute | solution.py:661
  115.9 18.6 %collective-permute-start.26 = (bf16[1024,256]{1,0:T(8,128)(2,1)}, bf16[1024,256]{1,0:T(8,128)(2,1)S(1)}, u32[]{:S(2)}, u32[]{:S(2)}) collective-permute-start(bf16[1024,256]{1,0:T(8,128)(2,1)} %collective-permute-done.19.refs_10_.refs_5_), channel_id=1, source_target_pairs={{0,4},{4,0},{1,5},{5,1},{2,6},{6,2},{3,7},{7,3},{8,12},{12,8},{9,1... | collective-permute-start | bytes 1572872 | tf_op jit(solution)/shard_map/outer_w_far_x/ppermute | solution.py:661
  204.7 18.1 %collective-permute-start.34 = (bf16[8,256,128]{2,1,0:T(8,128)(2,1)}, bf16[8,256,128]{2,1,0:T(8,128)(2,1)S(1)}, u32[]{:S(2)}, u32[]{:S(2)}) collective-permute-start(bf16[8,256,128]{2,1,0:T(8,128)(2,1)} %get-tuple-element.269), channel_id=1, source_target_pairs={{0,4},{4,0},{1,5},{5,1},{2,6},{6,2},{3,7},{7,3},{8,12},{12,8},{9,1... | collective-permute-start | bytes 1572872 | tf_op jit(solution)/shard_map/gate_g_x/ppermute | solution.py:661
  205.1 17.7 %collective-permute-start.35 = (bf16[8,256,128]{2,1,0:T(8,128)(2,1)}, bf16[8,256,128]{2,1,0:T(8,128)(2,1)S(1)}, u32[]{:S(2)}, u32[]{:S(2)}) collective-permute-start(bf16[8,256,128]{2,1,0:T(8,128)(2,1)} %get-tuple-element.270), channel_id=1, source_target_pairs={{0,1},{1,0},{2,3},{3,2},{4,5},{5,4},{6,7},{7,6},{8,9},{9,8},{10,11... | collective-permute-start | bytes 1572872 | tf_op jit(solution)/shard_map/outer_g_t/ppermute | solution.py:661
  205.5 105.9 %reduce-scatter.5.cloned.1.call-start = ((), (), s32[]{:S(2)}) async-start(), calls=%async_computation.7 | async-start | bytes 1310720 | tf_op jit(solution)/shard_map/reduce_scatter | solution.py:936
  251.2 59.4 %all-to-all-start = ((bf16[8,512,128]{2,1,0:T(8,128)(2,1)}), bf16[8,512,128]{2,1,0:T(8,128)(2,1)S(1)}, u32[]{:S(2)}, u32[]{:S(2)}) async-start(bf16[8,512,128]{2,1,0:T(8,128)(2,1)} %pad_maximum_fusion), calls=%async_computation.2 | async-start | bytes 2097152 | tf_op jit(solution)/shard_map/all_to_all | solution.py:689
  272.3 38.3 %collective-permute-start.45 = (bf16[8,128,128]{2,1,0:T(8,128)(2,1)S(1)}, bf16[8,128,128]{2,1,0:T(8,128)(2,1)}, u32[]{:S(2)}, u32[]{:S(2)}) collective-permute-start(bf16[8,128,128]{2,1,0:T(8,128)(2,1)S(1)} %fusion.5), channel_id=1, source_target_pairs={{0,1},{1,0},{2,3},{3,2},{4,5},{5,4},{6,7},{7,6},{8,9},{9,8},{10,11... | collective-permute-start | bytes 786440 | tf_op jit(solution)/shard_map/stream_g_sum_t/ppermute | solution.py:661
  274.1 21.4 %collective-permute-start.48 = (bf16[320,256]{1,0:T(8,128)(2,1)S(1)}, bf16[320,256]{1,0:T(8,128)(2,1)S(1)}, u32[]{:S(2)}, u32[]{:S(2)}) collective-permute-start(bf16[320,256]{1,0:T(8,128)(2,1)S(1)} %add_convert_fusion.6.refs_2_), channel_id=1, source_target_pairs={{0,8},{8,16},{16,24},{24,0},{1,9},{9,17},{17,25},{25,1},{2,10},{10... | collective-permute-start | bytes 491528 | tf_op jit(solution)/shard_map/small_z/ppermute | solution.py:676
  275.9 34.8 %collective-permute-start.46 = (bf16[8,128,128]{2,1,0:T(8,128)(2,1)S(1)}, bf16[8,128,128]{2,1,0:T(8,128)(2,1)}, u32[]{:S(2)}, u32[]{:S(2)}) collective-permute-start(bf16[8,128,128]{2,1,0:T(8,128)(2,1)S(1)} %fusion.4), channel_id=1, source_target_pairs={{0,4},{4,0},{1,5},{5,1},{2,6},{6,2},{3,7},{7,3},{8,12},{12,8},{9,1... | collective-permute-start | bytes 786440 | tf_op jit(solution)/shard_map/stream_g_sum_x/ppermute | solution.py:661
  277.6 33.0 %collective-permute-start.47 = (bf16[64,2048]{1,0:T(8,128)(2,1)S(1)}, bf16[64,2048]{1,0:T(8,128)(2,1)S(1)}, u32[]{:S(2)}, u32[]{:S(2)}) collective-permute-start(bf16[64,2048]{1,0:T(8,128)(2,1)S(1)} %pad_maximum_fusion.8.refs_2_), channel_id=1, source_target_pairs={{0,1},{1,0},{2,3},{3,2},{4,5},{5,4},{6,7},{7,6},{8,9},{9,8},{10,11... | collective-permute-start | bytes 786440 | tf_op jit(solution)/shard_map/rows_t/ppermute | solution.py:661
  277.9 29.2 %collective-permute-start.49 = (bf16[320,256]{1,0:T(8,128)(2,1)S(1)}, bf16[320,256]{1,0:T(8,128)(2,1)}, u32[]{:S(2)}, u32[]{:S(2)}) collective-permute-start(bf16[320,256]{1,0:T(8,128)(2,1)S(1)} %add_convert_fusion.6.refs_2_), channel_id=1, source_target_pairs={{0,16},{8,24},{16,0},{24,8},{1,17},{9,25},{17,1},{25,9},{2,18},{10... | collective-permute-start | bytes 491528 | tf_op jit(solution)/shard_map/small_z/ppermute | solution.py:676
  314.5 20.1 %all-to-all-start.1 = ((bf16[8,256,128]{2,1,0:T(8,128)(2,1)}), bf16[8,256,128]{2,1,0:T(8,128)(2,1)S(1)}, u32[]{:S(2)}, u32[]{:S(2)}) async-start(bf16[8,256,128]{2,1,0:T(8,128)(2,1)} %pad_maximum_fusion.4), calls=%async_computation.3 | async-start | bytes 1048576 | tf_op jit(solution)/shard_map/all_to_all | solution.py:689
  (98 other events, 1379.5 us)
Sparse Core Ops, SparseCore 0:
  28.1 40.5 all-gather.2
  97.6 29.5 all-gather.4
  205.6 26.9 reduce-scatter.2
  248.5 41.2 reduce-scatter.4

commit v3 on v2

--- a/solution.py
+++ b/solution.py
@@ -15,9 +15,16 @@
 LOG2E = 1.4426950408889634
 RESET_RATE = 1e30
 LANES = 128
+MICROSECONDS = {
+    "pack": 3, "pack_cores": 3, "prep": 2, "front": 8, "late": 8, "mixer": 24, "out_rows": 5,
+    "late_grad": 6, "back": 7, "in_rows": 7, "output": 3, "input_grad": 4, "small": 3,
+    "rows_back": 3,
+}
 SUBLANES = 8
 SIDE = 2
 GROUP = 8
+CHUNK = 64
+UNROLL = 2
 F32 = jnp.float32
 BF16 = jnp.bfloat16
 NT = ((1,), (1,))
@@ -38,9 +45,8 @@
     return jax.ShapeDtypeStruct(dims, dtype)
 
 
-def whole(kernel, name, scalars, arrays, outs, scratch=(), flops=0):
+def whole(kernel, name, scalars, arrays, outs, scratch=()):
     scalars = [jnp.reshape(v, (1,)).astype(jnp.int32) for v in scalars]
-    size = sum(v.size * v.dtype.itemsize for v in (*arrays, *outs))
     few, many, made = len(scalars), len(arrays), len(outs)
 
     def copied(*refs):
@@ -78,7 +84,9 @@
             pltpu.SemaphoreType.DMA((many + made,)),
         ],
         compiler_params=pltpu.CompilerParams(vmem_limit_bytes=60 << 20),
-        cost_estimate=pl.CostEstimate(flops=flops, bytes_accessed=size, transcendentals=0),
+        cost_estimate=pl.CostEstimate(
+            flops=0, bytes_accessed=MICROSECONDS[name] * 3690000, transcendentals=0
+        ),
         name=name,
     )(*scalars, *arrays)
 
@@ -462,14 +470,13 @@
         rest = block[states + 8 + rank :, :].astype(F32)
         filters[:, at] = rest[count : count + taps]
         filter_b[:, at] = rest[count + taps : count + taps + 1]
-        chosen = jnp.concatenate([rest[:count], jnp.zeros((-count % LANES, part), F32)], 0)
-        select[at, :] = chosen.T[:, :count]
+        select[:, at] = rest[:count]
 
 
 def scan_kernel(
     layout, core_ref, pos_ref, act_ref, gate_ref, gg_ref, total_ref, rest_ref, sw_ref, par_ref,
     gated_ref, gateg_ref, sact_ref, small_ref, mine_ref, other_ref,
-    bb, cb, hist, fac, ci_acc, co_acc, rate_s, reff_s, u_s, ds_s, y_s, s2_s, slope_s, decb, sel_t, rate_low, rank_t,
+    bb, cb, hist, fac, ci_acc, co_acc, rate_s, reff_s, u_s, ds_s, y_s, s2_s, slope_s, spre_low, decb, sel_t, rate_low, rank_t,
 ):
     rank_width, states, bias_row, decay_row, skip_row = layout
     rows, channels = act_ref.shape
@@ -485,8 +492,12 @@
     sel_t[:, : rows // 2] = jnp.where(first, total, rest)
     sel_t[:, rows // 2 :] = jnp.where(first, rest, total)
     rate_low[...] = sel_t[:rank_width, :].T.astype(BF16)
-    bb[...] = split_dot(sel_t[rank_width : rank_width + states, :], spread, TN)
-    cb[...] = split_dot(sel_t[rank_width + states :, :], spread, TN)
+    twice = jnp.concatenate([spread, spread], 0)
+    for out, base in ((bb, rank_width), (cb, rank_width + states)):
+        value = sel_t[base : base + states, :]
+        high = value.astype(BF16).astype(F32)
+        parts = jnp.concatenate([high, value - high], 0).astype(BF16)
+        out[...] = dot(parts, twice, TN)
     hist[0:SUBLANES, :] = jnp.zeros((SUBLANES, SIDE * wide), F32)
     ci_acc[...] = jnp.zeros_like(ci_acc)
     co_acc[...] = jnp.zeros_like(co_acc)
@@ -509,17 +520,27 @@
         decay = -jnp.exp(par_ref[decay_row : decay_row + states, at])
         for n in range(states):
             decb[8 * n : 8 * n + 8, :] = jnp.broadcast_to(decay[n : n + 1, :], (8, both))
-        step_pre = dot(rate_low[...], sw_ref[:, at]) + par_ref[bias_row : bias_row + 1, at]
-        rate = jnp.maximum(step_pre, 0.0) + jnp.log1p(jnp.exp(-jnp.abs(step_pre)))
-        rate_s[...] = rate
-        for side in sides:
-            reff_s[:, side_cols(side)] = jnp.where(
-                pos_ref[...] > 0.0, rate[:, side_cols(side)] * LOG2E, RESET_RATE
-            )
-        u_s[...] = rate * act_ref[:, at]
-        slope_s[...] = jax.nn.sigmoid(step_pre)
-        gate = gate_ref[:, at]
-        ds_s[...] = gg_ref[:, at] * (gate * jax.nn.sigmoid(gate))
+        rate_s[...] = dot(rate_low[...], sw_ref[:, at]) + par_ref[bias_row : bias_row + 1, at]
+
+        def before(i, _):
+            row = pl.ds(pl.multiple_of(i * CHUNK, CHUNK), CHUNK)
+            step_pre = rate_s[row, :]
+            small = jnp.exp(-jnp.abs(step_pre))
+            rate = jnp.maximum(step_pre, 0.0) + jnp.log1p(small)
+            inverse = 1.0 / (1.0 + small)
+            slope_s[row, :] = jnp.where(step_pre >= 0.0, inverse, small * inverse)
+            rate_s[row, :] = rate
+            keep = pos_ref[row, :] > 0.0
+            for side in sides:
+                reff_s[row, side_cols(side)] = jnp.where(
+                    keep, rate[:, side_cols(side)] * LOG2E, RESET_RATE
+                )
+            u_s[row, :] = rate * act_ref[row, at]
+            gate = gate_ref[row, at]
+            ds_s[row, :] = gg_ref[row, at] * (gate * jax.nn.sigmoid(gate))
+            return 0
+
+        lax.fori_loop(0, rows // CHUNK, before, 0)
 
         for group in range(states // GROUP):
             names = range(group * GROUP, (group + 1) * GROUP)
@@ -548,16 +569,22 @@
                     y_s[row, side_cols(i)] = y[i]
                 return tuple(fresh)
 
-            lax.fori_loop(0, steps, forward, (zero,) * (GROUP * SIDE))
-
-        act = act_ref[:, at]
+            lax.fori_loop(0, steps, forward, (zero,) * (GROUP * SIDE), unroll=UNROLL)
+
         skip = par_ref[skip_row : skip_row + 1, at]
-        scanned = y_s[...] + skip * act
-        sig = jax.nn.sigmoid(gate)
-        gated_ref[:, at] = (scanned * (gate * sig)).astype(BF16)
-        gateg_ref[:, at] = (
-            gg_ref[:, at] * scanned * (sig * (1.0 + gate * (1.0 - sig)))
-        ).astype(BF16)
+
+        def between(i, _):
+            row = pl.ds(pl.multiple_of(i * CHUNK, CHUNK), CHUNK)
+            scanned = y_s[row, :] + skip * act_ref[row, at]
+            gate = gate_ref[row, at]
+            sig = jax.nn.sigmoid(gate)
+            gated_ref[row, at] = (scanned * (gate * sig)).astype(BF16)
+            gateg_ref[row, at] = (
+                gg_ref[row, at] * scanned * (sig * (1.0 + gate * (1.0 - sig)))
+            ).astype(BF16)
+            return 0
+
+        lax.fori_loop(0, rows // CHUNK, between, 0)
 
         sums = []
         for group in range(states // GROUP):
@@ -592,7 +619,7 @@
                 return tuple(g_new), tuple(d_new)
 
             none = (zero,) * (GROUP * SIDE)
-            _, dacc = lax.fori_loop(0, steps, backward, (none, none))
+            _, dacc = lax.fori_loop(0, steps, backward, (none, none), unroll=UNROLL)
             for n in range(GROUP):
                 row = jnp.concatenate(
                     [jnp.sum(dacc[n * SIDE + k], axis=0, keepdims=True) for k in sides], 1
@@ -600,26 +627,36 @@
                 name = group * GROUP + n
                 sums.append(row * decb[8 * name : 8 * name + 1, :])
 
-        act = act_ref[:, at]
-        skip = par_ref[skip_row : skip_row + 1, at]
-        s2_all = s2_s[...]
-        dscan = ds_s[...]
-        sact_ref[:, at] = rate_s[...] * s2_all + skip * dscan
-        spre = (reff_s[...] + act * s2_all) * slope_s[...]
-        spre_low = spre.astype(BF16)
-        head = [jnp.sum(spre, axis=0, keepdims=True), jnp.sum(dscan * act, axis=0, keepdims=True)]
+        def behind(i, carried):
+            row = pl.ds(pl.multiple_of(i * CHUNK, CHUNK), CHUNK)
+            act, dscan, s2_all = act_ref[row, at], ds_s[row, :], s2_s[row, :]
+            sact_ref[row, at] = rate_s[row, :] * s2_all + skip * dscan
+            spre = (reff_s[row, :] + act * s2_all) * slope_s[row, :]
+            spre_low[row, :] = spre.astype(BF16)
+            totals = []
+            for total, value in zip(carried, (spre, dscan * act)):
+                for j in range(CHUNK // SUBLANES):
+                    total = total + value[j * SUBLANES : (j + 1) * SUBLANES]
+                totals.append(total)
+            return tuple(totals)
+
+        empty = jnp.zeros((SUBLANES, both), F32)
+        head = [
+            jnp.sum(v, axis=0, keepdims=True)
+            for v in lax.fori_loop(0, rows // CHUNK, behind, (empty, empty))
+        ]
         head.append(jnp.zeros((6, both), F32))
         small_ref[: states + 8, at] = jnp.concatenate(head + sums, 0).astype(BF16)
         small_ref[states + 8 :, at] = dot(
-            sel_t[:rank_width, :].astype(BF16), spre_low
+            sel_t[:rank_width, :].astype(BF16), spre_low[...]
         ).astype(BF16)
-        rank_t[...] += dot(sw_ref[:, at], spre_low, NT)
+        rank_t[...] += dot(sw_ref[:, at], spre_low[...], NT)
         return 0
 
     lax.fori_loop(0, channels // both, one_block, 0)
     high, low = slice(0, rows // 2), slice(rows // 2, rows)
     for acc, base in ((ci_acc, rank_width), (co_acc, rank_width + states)):
-        sel_t[base : base + states, :] = split_dot(acc[...], spread, NT).T
+        sel_t[base : base + states, :] = dot(acc[...].astype(BF16), spread, NT).T
     sel_t[:rank_width, :] = rank_t[...]
     mine_ref[...] = jnp.where(first, sel_t[:, high], sel_t[:, low])
     other_ref[...] = jnp.where(first, sel_t[:, low], sel_t[:, high])
@@ -645,10 +682,10 @@
         ]
         + [pltpu.VMEM((rows, SIDE * LANES), F32)] * 7
         + [
+            pltpu.VMEM((rows, SIDE * LANES), BF16),
             pltpu.VMEM((8 * states, SIDE * LANES), F32), pltpu.VMEM((count, rows), F32),
             pltpu.VMEM((rows, rank_width), BF16), pltpu.VMEM((rank_width, rows), F32),
         ],
-        flops=20 * rows * channels * states,
     )
 
 
@@ -858,7 +895,6 @@
         (group_tokens, arrived, *ws, params, select_w),
         [wide_low, full, full, *half_out, shape((group_rows, LANES), F32), shape((8, width), F32)],
         [pltpu.VMEM((group_rows, width), BF16), pltpu.VMEM((group_rows, channels), BF16)],
-        flops=4 * group_rows * width * channels,
     )
     normed, stream, act, sel_mine, sel_other, gate_x, outer_t = step(
         normed, stream, act, sel_mine, sel_other,
@@ -878,7 +914,6 @@
     wg, wo = (gate_own, gate_x, gate_t, gate_d), (outer_own, outer_x, outer_t, outer_d)
     upstream, gate, gated_grad = whole(
         late_kernel, "late", [zi], (group_cot, arrived, normed, *wg, *wo), [wide_low, full, full],
-        flops=6 * group_rows * width * channels,
     )
     rest = swap(total, "k", "select_rest")
     gated, gate_grad, act_grad, small_a, sel_mine, sel_other = mixer(
@@ -887,7 +922,6 @@
 
     out_mine, out_other = whole(
         out_kernel, "out_rows", [zi], (returned, gated, *wo), half_rows,
-        flops=2 * group_rows * width * channels,
     )
     got, out_mine, out_other, gated, gate_grad = step(
         swap(sel_other, "k", "select"), out_mine, out_other, gated, gate_grad
@@ -896,7 +930,6 @@
     pieces = whole(
         late_grad_kernel, "late_grad", [zi], (normed, upstream, gate_grad, gated),
         [shape((2 * zs, part, ring_rows), BF16)] * 8,
-        flops=4 * group_rows * width * channels,
     )
     got, out_got, sent, *pieces = step(
         exchange_z(sent, 1, "select"), swap(out_other, "k", "rows"), sent, *pieces
@@ -904,9 +937,8 @@
     out_total = plus(out_mine, out_got)
     gate_g, outer_g = pieces[:4], pieces[4:]
     sent = plus(sent, got)
-    got, gate_far, outer_far, sent, out_total, *pieces = step(
-        exchange_z(sent, 2, "select"), swap(gate_g[3], "x", "gate_g_far"),
-        swap(outer_g[3], "t", "outer_g_far"), sent, out_total, *pieces,
+    got, sent, out_total, *pieces = step(
+        exchange_z(sent, 2, "select"), sent, out_total, *pieces
     )
     gate_g, outer_g = pieces[:4], pieces[4:]
     out_back = lax.psum_scatter(out_total, "z", scatter_dimension=0, tiled=True)
@@ -919,51 +951,60 @@
         + [shape((2 * zs, part // 2, ring_rows), BF16)] * 4
         + [shape((2, 2 * zs, part // 2, ring_rows), BF16)] * 2,
         [pltpu.VMEM((group_rows, channels), BF16), pltpu.VMEM((channels, group_rows), BF16)],
-        flops=4 * group_rows * width * channels,
-    )
-    small = jnp.concatenate([small_a, small_b], axis=0)
-    gate_first, outer_first, low, small_got, small, *stream_g = step(
-        swap(gate_g[1], "x", "gate_g"), swap(outer_g[2], "t", "outer_g"), low,
-        swap(small[:, part:], "t", "small"), small, *stream_g,
-    )
-    small = plus(small[:, :part], small_got)
+    )
+    gate_far, outer_far, low, small_b, *more = step(
+        swap(gate_g[3], "x", "gate_g_far"), swap(outer_g[3], "t", "outer_g_far"), low, small_b,
+        *pieces, *stream_g,
+    )
+    pieces, stream_g = more[:8], more[8:]
+    gate_g, outer_g = pieces[:4], pieces[4:]
     in_mine, in_other = whole(
         in_kernel, "in_rows", [zi], (returned, low, gate_grad, *ws, *wg),
         half_rows, [pltpu.VMEM((group_rows, 2 * channels), BF16)],
-        flops=4 * group_rows * width * channels,
     )
     in_total = plus(in_mine, swap(in_other, "k", "rows"))
     in_back = lax.psum_scatter(in_total, "z", scatter_dimension=0, tiled=True)
-    gate_second, outer_second, small_got, small, _ = step(
+    gate_first, outer_first, _, out_back, *pieces = step(
+        swap(gate_g[1], "x", "gate_g"), swap(outer_g[2], "t", "outer_g"), in_total, out_back,
+        *pieces,
+    )
+    gate_g, outer_g = pieces[:4], pieces[4:]
+    small = jnp.concatenate([small_a, small_b], axis=0)
+    gate_second, outer_second, small_got, small, in_back, *stream_g = step(
         swap(plus(gate_g[2], gate_far), "t", "gate_g_sum"),
         swap(plus(outer_g[1], outer_far), "x", "outer_g_sum"),
-        swap(small, "x", "small"), small, in_total,
-    )
-    small = plus(small, small_got)
+        swap(small[:, part:], "t", "small"), small, in_back, *stream_g,
+    )
     late_sum = jnp.concatenate(
         [plus(gate_g[0], gate_first, gate_second), plus(outer_g[0], outer_first, outer_second)],
         axis=1,
     )
     late_home = to_owners(late_sum)
     own_low, own_high, by_x_high, by_t_low, x_way, t_way = stream_g
+    small = plus(small[:, :part], small_got)
+
     def near_rows(rows):
         return jnp.concatenate([rows[:share], swap(rows[share:], "x", "rows")], 0)
 
-    x_way, t_way, small, out_near = step(
-        swap(x_way, "x", "stream_g"), swap(t_way, "t", "stream_g"), small, near_rows(out_back),
-    )
+    x_way, t_way, small_got, small, out_near = step(
+        swap(x_way, "x", "stream_g"), swap(t_way, "t", "stream_g"), swap(small, "x", "small"),
+        small, near_rows(out_back),
+    )
+    small = plus(small, small_got)
     if rings > 1:
         small = lax.psum(small.astype(F32), "r").astype(BF16)
-    low_second, high_second, out_far, out_near, in_back, late_home, *gathered_small = step(
+    low_second, high_second, out_far, out_near, in_near, late_home, *gathered_small = step(
         swap(plus(by_t_low, x_way[0]), "t", "stream_g_sum"),
         swap(plus(by_x_high, t_way[0]), "x", "stream_g_sum"),
-        swap(out_near, "t", "rows"), out_near, in_back, late_home, *from_z([small] * zs, "small"),
+        swap(out_near, "t", "rows"), out_near, near_rows(in_back), late_home,
+        *from_z([small] * zs, "small"),
     )
     stream_sum = jnp.concatenate(
         [plus(own_low, x_way[1], low_second), plus(own_high, t_way[1], high_second)], axis=1
     )
-    stream_home, in_near = step(to_owners(stream_sum), near_rows(in_back))
-    in_far = swap(in_near, "t", "rows")
+    stream_home, in_far, in_near = step(
+        to_owners(stream_sum), swap(in_near, "t", "rows"), in_near
+    )
     small_blocks = [v for block in gathered_small for v in (block, swap(block, "k", "small"))]
 
     back_place = send_place[:, None]
@@ -1000,7 +1041,7 @@
     select_grad, step_w_grad, decay_grad, filter_grad, filter_b_grad, step_b_grad, skip_grad = whole(
         partial(small_kernel, (count, states, taps)), "small", [zi, ki], small_blocks,
         [
-            shape((half_channels, count), F32), shape((rank_width, half_channels), F32),
+            shape((count, half_channels), F32), shape((rank_width, half_channels), F32),
             shape((states, half_channels), F32), shape((taps, half_channels), F32),
             one_row, one_row, one_row,
         ],
@@ -1022,7 +1063,7 @@
         inner_home,
         filter_grad,
         filter_b_grad[0],
-        select_grad,
+        select_grad.T,
         step_w_grad,
         step_b_grad[0],
         decay_grad,

time: 359 us -> 337 us (0.939)
  waiting for transfers between devices: 127 us -> 103 us
  starting transfers between devices: 78.3 us -> 87.3 us
  other arithmetic: 22.7 us -> 29.1 us
  Pallas kernels: 87.2 us -> 82 us
  local copies, waits for them, and re-layouts: 23.2 us -> 19.3 us
    ppermute x12, waiting for transfers between devices: 59.3 us -> 35.4 us  [from_z(): lax.ppermute(blocks[shift], 'z', [(i, (i + shift) % size) for i in range(...]
    ppermute x42, waiting for transfers between devices: 61.7 us -> 52.3 us  [swap(): return lax.ppermute(value, axis, SWAP)]
    ppermute x12, starting transfers between devices: 23.5 us -> 29.1 us  [from_z(): lax.ppermute(blocks[shift], 'z', [(i, (i + shift) % size) for i in range(...]
    pallas_call x13, Pallas kernels: 87.2 us -> 82 us  [whole(): pl.pallas_call(copied, in_specs=[pl.BlockSpec(memory_space=pltpu.SMEM)] *...]
    unnamed x121 -> x128, local copies, waits for them, and re-layouts: 15.3 us -> 10.6 us
    ppermute x4, waiting for transfers between devices: 5.98 us -> 10.5 us  [exchange_z(): return lax.ppermute(value, 'z', [(i, i ^ distance) for i in range(size)])]
    all_to_all x2, waiting for transfers between devices: 0.43 us -> 4.68 us  [to_owners(): return lax.all_to_all(value, ZK, 0, 0, tiled=True)]
    ppermute x42, starting transfers between devices: 37.7 us -> 41.4 us  [swap(): return lax.ppermute(value, axis, SWAP)]
  transfers between devices with their start and end apart: 64 -> 64, of which waited for: 27 -> 26; matrix products, arithmetic and copies ran while one was open for 7% -> 9% of each run, Pallas kernels for 14% -> 16%
where the time goes in v3:
time: 337 us; the launch traced here: 336 us
  waiting for transfers between devices  103 us (31%)
  starting transfers between devices  87.3 us (26%)
  Pallas kernels  82 us (24%)
  other arithmetic  29.1 us (9%)
  local copies, waits for them, and re-layouts  19.3 us (6%)
  between operations  15 us (4%)
    pallas_call x13, Pallas kernels, whole(): pl.pallas_call(copied, in_specs=[pl.BlockSpec(memory_space=pltpu.SMEM)] *...  82 us
    ppermute x42, waiting for transfers between devices, swap(): return lax.ppermute(value, axis, SWAP)  52.3 us
    ppermute x42, starting transfers between devices, swap(): return lax.ppermute(value, axis, SWAP)  41.4 us
    ppermute x12, waiting for transfers between devices, from_z(): lax.ppermute(blocks[shift], 'z', [(i, (i + shift) % size) for i in range(...  35.4 us
    ppermute x12, starting transfers between devices, from_z(): lax.ppermute(blocks[shift], 'z', [(i, (i + shift) % size) for i in range(...  29.1 us
    unnamed x128, local copies, waits for them, and re-layouts  10.6 us
    ppermute x4, waiting for transfers between devices, exchange_z(): return lax.ppermute(value, 'z', [(i, i ^ distance) for i in range(size)])  10.5 us
    convert_element_type x13, other arithmetic, plus(): return total.astype(BF16)  9.41 us
  transfers between devices with their start and end apart: 64, of which 26 were waited for; matrix products, arithmetic and copies ran while one was open for 9% of the time, Pallas kernels for 16%

profile of v3, /device:TPU:0, one launch (start us, length us, event | category | flops | bytes accessed | tf_op | source)
XLA Modules:
  0.0 335.7 jit_solution(17000057989733090417)
XLA Ops:
  21.7 3.9 %collective-permute-done.17 = bf16[32,2176]{1,0:T(8,128)(2,1)S(1)} collective-permute-done((bf16[32,2176]{1,0:T(8,128)(2,1)}, bf16[32,2176]{1,0:T(8,128)(2,1)S(1)}, u32[]{:S(2)}, u32[]{:S(2)}) %collective-permute-start.17) | collective-permute-done | bytes 139296 | tf_op jit(solution)/shard_map/tokens_x/ppermute | solution.py:698
  42.6 10.2 %collective-permute-done.2 = bf16[256,256]{1,0:T(8,128)(2,1)S(1)} collective-permute-done((bf16[256,256]{1,0:T(8,128)(2,1)}, bf16[256,256]{1,0:T(8,128)(2,1)S(1)}, u32[]{:S(2)}, u32[]{:S(2)}) %collective-permute-start.2) | collective-permute-done | bytes 131104 | tf_op jit(solution)/shard_map/stream_w_z/ppermute | solution.py:713
  57.3 10.6 %collective-permute-start.10 = (bf16[256,256]{1,0:T(8,128)(2,1)}, bf16[256,256]{1,0:T(8,128)(2,1)S(1)}, u32[]{:S(2)}, u32[]{:S(2)}) collective-permute-start(bf16[256,256]{1,0:T(8,128)(2,1)} %get-tuple-element.211), channel_id=1, source_target_pairs={{0,24},{8,0},{16,8},{24,16},{1,25},{9,1},{17,9},{25,17},{2,26},{10... | collective-permute-start | bytes 393224 | tf_op jit(solution)/shard_map/gate_w_z/ppermute | solution.py:713
  74.9 4.5 %collective-permute-done.9 = bf16[256,256]{1,0:T(8,128)(2,1)S(1)} collective-permute-done((bf16[256,256]{1,0:T(8,128)(2,1)}, bf16[256,256]{1,0:T(8,128)(2,1)S(1)}, u32[]{:S(2)}, u32[]{:S(2)}) %collective-permute-start.9) | collective-permute-done | bytes 131104 | tf_op jit(solution)/shard_map/gate_w_z/ppermute | solution.py:713
  89.9 3.3 collective-permute-done.14
  108.7 8.1 %front.1 = (bf16[512,2048]{1,0:T(8,128)(2,1)}, f32[512,512]{1,0:T(8,128)}, f32[512,512]{1,0:T(8,128)}, f32[160,256]{1,0:T(8,128)}, f32[160,256]{1,0:T(8,128)}, /*index=5*/f32[512,128]{1,0:T(8,128)}, f32[8,2048]{1,0:T(8,128)}) custom-call(s32[1]{0:T(128)} %bitcast.3.refs_1_.refs_0_, s32[1]{0:T(128)} %bitcast.4.refs_1_, s32[1]{0:T(128)} %bitcast.5.refs_0_.refs_2_.refs_1_, ...), custom_call_target="tpu_custom_call" | custom-call | bytes 29520000 | tf_op jit(solution)/shard_map/front/pallas_call | solution.py:75
  127.4 3.8 %collective-permute-done.24 = bf16[160,256]{1,0:T(8,128)(2,1)S(1)} collective-permute-done((bf16[160,256]{1,0:T(8,128)(2,1)S(1)}, bf16[160,256]{1,0:T(8,128)(2,1)S(1)}, u32[]{:S(2)}, u32[]{:S(2)}) %collective-permute-start.24) | collective-permute-done | bytes 81952 | tf_op jit(solution)/shard_map/select_z/ppermute | solution.py:704
  135.4 8.0 %late.1 = (bf16[512,2048]{1,0:T(8,128)(2,1)}, f32[512,512]{1,0:T(8,128)}, f32[512,512]{1,0:T(8,128)}) custom-call(s32[1]{0:T(128)} %bitcast.5.refs_0_.refs_2_.refs_1_, bf16[512,2048]{1,0:T(8,128)(2,1)} %all-gather.5.cloned.1.call-done.refs_1_, s32[1,512]{1,0:T(1,128)} %reshape.372.refs_4_.refs_2_, ...), custom_call_target="tpu_custom_call" | custom-call | bytes 29520000 | tf_op jit(solution)/shard_map/late/pallas_call | solution.py:75
  144.0 24.1 %mixer.1 = (bf16[512,512]{1,0:T(8,128)(2,1)}, bf16[512,512]{1,0:T(8,128)(2,1)}, f32[512,512]{1,0:T(8,128)}, bf16[152,512]{1,0:T(8,128)(2,1)}, f32[160,256]{1,0:T(8,128)}, /*index=5*/f32[160,256]{1,0:T(8,128)}) custom-call(s32[1]{0:T(128)} %bitcast.3.refs_1_.refs_0_, f32[512,128]{1,0:T(8,128)} %get-tuple-element.233.refs_1_.refs_4_, ...), custom_call_target="tpu_custom_call" | custom-call | bytes 88560000 | tf_op jit(solution)/shard_map/mixer/pallas_call | solution.py:75
  169.7 4.6 %out_rows.1 = (bf16[256,2048]{1,0:T(8,128)(2,1)}, bf16[256,2048]{1,0:T(8,128)(2,1)}) custom-call(s32[1]{0:T(128)} %bitcast.5.refs_0_.refs_2_.refs_1_, s32[512,1]{1,0:T(8,128)} %reshape.381.refs_1_, bf16[512,512]{1,0:T(8,128)(2,1)} %get-tuple-element.269.refs_2_.refs_4_, bf16[1024,256]{1,0:T(8,128)(2,1)} %copy-done.2, bf16[1024,256]{1,0:T(8,128)(2,1)} %copy-done.9, ...), custom_call_target="tpu_custom_call" | custom-call | bytes 18450000 | tf_op jit(solution)/shard_map/out_rows/pallas_call | solution.py:75
  174.5 3.4 %collective-permute-start.29 = (bf16[160,256]{1,0:T(8,128)(2,1)S(1)}, bf16[160,256]{1,0:T(8,128)(2,1)S(1)}, u32[]{:S(2)}, u32[]{:S(2)}) collective-permute-start(bf16[160,256]{1,0:T(8,128)(2,1)S(1)} %add_convert_fusion.9), channel_id=1, source_target_pairs={{0,8},{8,0},{16,24},{24,16},{1,9},{9,1},{17,25},{25,17},{2,10},{10... | collective-permute-start | bytes 245768 | tf_op jit(solution)/shard_map/select_z/ppermute | solution.py:704
  177.9 6.1 %late_grad.1 = (bf16[8,256,128]{2,1,0:T(8,128)(2,1)}, bf16[8,256,128]{2,1,0:T(8,128)(2,1)}, bf16[8,256,128]{2,1,0:T(8,128)(2,1)}, bf16[8,256,128]{2,1,0:T(8,128)...) custom-call(s32[1]{0:T(128)} %bitcast.5.refs_0_.refs_2_.refs_1_, ...), custom_call_target="tpu_custom_call" | custom-call | bytes 22140000 | tf_op jit(solution)/shard_map/late_grad/pallas_call | solution.py:75
  186.7 4.4 %collective-permute-done.31 = bf16[160,256]{1,0:T(8,128)(2,1)S(1)} collective-permute-done((bf16[160,256]{1,0:T(8,128)(2,1)S(1)}, bf16[160,256]{1,0:T(8,128)(2,1)S(1)}, u32[]{:S(2)}, u32[]{:S(2)}) %collective-permute-start.31) | collective-permute-done | bytes 81952 | tf_op jit(solution)/shard_map/select_z/ppermute | solution.py:704
  195.7 7.1 %back.1 = (bf16[512,512]{1,0:T(8,128)(2,1)}, bf16[168,512]{1,0:T(8,128)(2,1)}, bf16[8,128,128]{2,1,0:T(8,128)(2,1)}, bf16[8,128,128]{2,1,0:T(8,128)(2,1)}, bf16[...) custom-call(s32[1]{0:T(128)} %bitcast.3.refs_1_.refs_0_, ...), custom_call_target="tpu_custom_call" | custom-call | bytes 25830000 | tf_op jit(solution)/shard_map/back/pallas_call | solution.py:75
  205.8 6.9 %in_rows.1 = (bf16[256,2048]{1,0:T(8,128)(2,1)}, bf16[256,2048]{1,0:T(8,128)(2,1)}) custom-call(s32[1]{0:T(128)} %bitcast.5.refs_0_.refs_2_.refs_1_, s32[512,1]{1,0:T(8,128)} %reshape.381.refs_1_, bf16[512,512]{1,0:T(8,128)(2,1)} %get-tuple-element.312.refs_2_, bf16[512,512]{1,0:T(8,128)(2,1)} %get-tuple-element.268.refs_3_, bf16[1024,256]{1,0:T(8,128)(2,1)} %copy-done.3, ...), custom_call_target="tpu_custom_call" | custom-call | bytes 25830000 | tf_op jit(solution)/shard_map/in_rows/pallas_call | solution.py:75
  221.1 11.5 %collective-permute-done.35 = bf16[8,256,128]{2,1,0:T(8,128)(2,1)} collective-permute-done((bf16[8,256,128]{2,1,0:T(8,128)(2,1)}, bf16[8,256,128]{2,1,0:T(8,128)(2,1)}, u32[]{:S(2)}, u32[]{:S(2)}) %collective-permute-start.35) | collective-permute-done | bytes 524320 | tf_op jit(solution)/shard_map/gate_g_x/ppermute | solution.py:698
  238.6 12.3 %collective-permute-done.40 = bf16[320,256]{1,0:T(8,128)(2,1)S(1)} collective-permute-done((bf16[320,256]{1,0:T(8,128)(2,1)S(1)}, bf16[320,256]{1,0:T(8,128)(2,1)S(1)}, u32[]{:S(2)}, u32[]{:S(2)}) %collective-permute-start.40) | collective-permute-done | bytes 163872 | tf_op jit(solution)/shard_map/small_t/ppermute | solution.py:698
  253.6 3.7 %all-to-all-start = ((bf16[8,512,128]{2,1,0:T(8,128)(2,1)}), bf16[8,512,128]{2,1,0:T(8,128)(2,1)S(1)}, u32[]{:S(2)}, u32[]{:S(2)}) async-start(bf16[8,512,128]{2,1,0:T(8,128)(2,1)} %pad_maximum_fusion), calls=%async_computation.2 | async-start | bytes 2097152 | tf_op jit(solution)/shard_map/all_to_all | solution.py:726
  264.3 12.6 %collective-permute-done.43 = bf16[320,256]{1,0:T(8,128)(2,1)S(1)} collective-permute-done((bf16[320,256]{1,0:T(8,128)(2,1)S(1)}, bf16[320,256]{1,0:T(8,128)(2,1)S(1)}, u32[]{:S(2)}, u32[]{:S(2)}) %collective-permute-start.43) | collective-permute-done | bytes 163872 | tf_op jit(solution)/shard_map/small_x/ppermute | solution.py:698
  284.6 3.8 %collective-permute-start.51 = (bf16[320,256]{1,0:T(8,128)(2,1)S(1)}, bf16[320,256]{1,0:T(8,128)(2,1)}, u32[]{:S(2)}, u32[]{:S(2)}) collective-permute-start(bf16[320,256]{1,0:T(8,128)(2,1)S(1)} %add_convert_fusion.6.refs_2_), channel_id=1, source_target_pairs={{0,24},{8,0},{16,8},{24,16},{1,25},{9,1},{17,9},{25,17},{2,26},{10... | collective-permute-start | bytes 491528 | tf_op jit(solution)/shard_map/small_z/ppermute | solution.py:713
  288.5 6.5 %collective-permute-done.50.refs_6_ = bf16[320,256]{1,0:T(8,128)(2,1)} collective-permute-done((bf16[320,256]{1,0:T(8,128)(2,1)S(1)}, bf16[320,256]{1,0:T(8,128)(2,1)}, u32[]{:S(2)}, u32[]{:S(2)}) %collective-permute-start.50) | collective-permute-done | bytes 163872 | tf_op jit(solution)/shard_map/small_z/ppermute | solution.py:713
  300.8 3.8 %all-to-all-start.1 = ((bf16[8,256,128]{2,1,0:T(8,128)(2,1)}), bf16[8,256,128]{2,1,0:T(8,128)(2,1)S(1)}, u32[]{:S(2)}, u32[]{:S(2)}) async-start(bf16[8,256,128]{2,1,0:T(8,128)(2,1)} %pad_maximum_fusion.4), calls=%async_computation.3 | async-start | bytes 1048576 | tf_op jit(solution)/shard_map/all_to_all | solution.py:726
  315.1 4.7 %all-to-all-done.1 = bf16[8,256,128]{2,1,0:T(8,128)(2,1)S(1)} async-done(((bf16[8,256,128]{2,1,0:T(8,128)(2,1)}), bf16[8,256,128]{2,1,0:T(8,128)(2,1)S(1)}, u32[]{:S(2)}, u32[]{:S(2)}) %all-to-all-start.1) | async-done | bytes 524320 | tf_op jit(solution)/shard_map/all_to_all | solution.py:726
  325.1 3.5 %input_grad.1 = f32[128,2048]{1,0:T(8,128)} custom-call(s32[1]{0:T(128)} %bitcast.refs_0_, s32[128,1]{1,0:T(8,128)} %copy.54.refs_1_, bf16[64,2048]{1,0:T(8,128)(2,1)} %copy-done.16, bf16[64,2048]{1,0:T(8,128)(2,1)} %copy-done.30, bf16[128,2048]{1,0:T(8,128)(2,1)} %refs_4_.3, bf16[128,2048]{1,0:T(8,128)(2,1)} %refs_5_.1, f32[8,2048]{1,0:T(8,128)} %get-tuple-element.360.refs_6_), custom_call_target="tpu_custom_call" | custom-call | bytes 14760000 | tf_op jit(solution)/shard_map/input_grad/pallas_call | solution.py:75
  (318 shorter events, 149.2 us)
Async XLA Ops:
  7.2 87.2 %all-gather.3.cloned.1.call-start = ((), (), s32[]{:S(2)}) async-start(), calls=%async_computation.4 | async-start | bytes 2506752 | tf_op jit(solution)/shard_map/all_gather | solution.py:865
  27.2 108.1 %all-gather.5.cloned.1.call-start = ((), (), s32[]{:S(2)}) async-start(), calls=%async_computation.5 | async-start | bytes 2359296 | tf_op jit(solution)/shard_map/all_gather | solution.py:865
  35.2 17.6 %collective-permute-start.2 = (bf16[256,256]{1,0:T(8,128)(2,1)}, bf16[256,256]{1,0:T(8,128)(2,1)S(1)}, u32[]{:S(2)}, u32[]{:S(2)}) collective-permute-start(bf16[256,256]{1,0:T(8,128)(2,1)} %get-tuple-element.197), channel_id=1, source_target_pairs={{0,16},{8,24},{16,0},{24,8},{1,17},{9,25},{17,1},{25,9},{2,18},{10... | collective-permute-start | bytes 393224 | tf_op jit(solution)/shard_map/stream_w_z/ppermute | solution.py:713
  37.8 15.0 %collective-permute-start.3 = (bf16[256,256]{1,0:T(8,128)(2,1)}, bf16[256,256]{1,0:T(8,128)(2,1)S(1)}, u32[]{:S(2)}, u32[]{:S(2)}) collective-permute-start(bf16[256,256]{1,0:T(8,128)(2,1)} %get-tuple-element.198), channel_id=1, source_target_pairs={{0,24},{8,0},{16,8},{24,16},{1,25},{9,1},{17,9},{25,17},{2,26},{10... | collective-permute-start | bytes 393224 | tf_op jit(solution)/shard_map/stream_w_z/ppermute | solution.py:713
  53.8 26.6 %collective-permute-start.6 = (bf16[1024,256]{1,0:T(8,128)(2,1)S(1)}, bf16[1024,256]{1,0:T(8,128)(2,1)S(1)}, u32[]{:S(2)}, u32[]{:S(2)}) collective-permute-start(bf16[1024,256]{1,0:T(8,128)(2,1)S(1)} %pad_maximum_fusion.1.refs_5_.refs_4_), channel_id=1, source_target_pairs={{0,4},{4,0},{1,5},{5,1},{2,6},{6,2},{3,7},{7,3},{8,12},{12,8},{9,1... | collective-permute-start | bytes 1572872 | tf_op jit(solution)/shard_map/stream_w_x/ppermute | solution.py:698
  55.7 24.7 %collective-permute-start.7 = (bf16[1024,256]{1,0:T(8,128)(2,1)S(1)}, bf16[1024,256]{1,0:T(8,128)(2,1)S(1)}, u32[]{:S(2)}, u32[]{:S(2)}) collective-permute-start(bf16[1024,256]{1,0:T(8,128)(2,1)S(1)} %pad_maximum_fusion.1.refs_5_.refs_4_), channel_id=1, source_target_pairs={{0,1},{1,0},{2,3},{3,2},{4,5},{5,4},{6,7},{7,6},{8,9},{9,8},{10,11... | collective-permute-start | bytes 1572872 | tf_op jit(solution)/shard_map/stream_w_t/ppermute | solution.py:698
  96.3 137.0 %reduce-scatter.3.cloned.1.call-start = ((), (), s32[]{:S(2)}) async-start(), calls=%async_computation.6 | async-start | bytes 1310720 | tf_op jit(solution)/shard_map/reduce_scatter | solution.py:944
  97.3 19.5 %collective-permute-start.18 = (bf16[1024,256]{1,0:T(8,128)(2,1)S(1)}, bf16[1024,256]{1,0:T(8,128)(2,1)}, u32[]{:S(2)}, u32[]{:S(2)}) collective-permute-start(bf16[1024,256]{1,0:T(8,128)(2,1)S(1)} %pad_maximum_fusion.2.refs_4_.refs_9_), channel_id=1, source_target_pairs={{0,4},{4,0},{1,5},{5,1},{2,6},{6,2},{3,7},{7,3},{8,12},{12,8},{9,1... | collective-permute-start | bytes 1572872 | tf_op jit(solution)/shard_map/gate_w_x/ppermute | solution.py:698
  98.7 18.1 %collective-permute-start.19 = (bf16[1024,256]{1,0:T(8,128)(2,1)S(1)}, bf16[1024,256]{1,0:T(8,128)(2,1)S(1)}, u32[]{:S(2)}, u32[]{:S(2)}) collective-permute-start(bf16[1024,256]{1,0:T(8,128)(2,1)S(1)} %pad_maximum_fusion.3.refs_8_.refs_3_), channel_id=1, source_target_pairs={{0,1},{1,0},{2,3},{3,2},{4,5},{5,4},{6,7},{7,6},{8,9},{9,8},{10,11... | collective-permute-start | bytes 1572872 | tf_op jit(solution)/shard_map/outer_w_t/ppermute | solution.py:698
  105.3 17.8 %collective-permute-start.22 = (bf16[1024,256]{1,0:T(8,128)(2,1)S(1)}, bf16[1024,256]{1,0:T(8,128)(2,1)S(1)}, u32[]{:S(2)}, u32[]{:S(2)}) collective-permute-start(bf16[1024,256]{1,0:T(8,128)(2,1)S(1)} %pad_maximum_fusion.2.refs_4_.refs_9_), channel_id=1, source_target_pairs={{0,1},{1,0},{2,3},{3,2},{4,5},{5,4},{6,7},{7,6},{8,9},{9,8},{10,11... | collective-permute-start | bytes 1572872 | tf_op jit(solution)/shard_map/gate_w_t/ppermute | solution.py:698
  105.9 17.2 %collective-permute-start.23 = (bf16[1024,256]{1,0:T(8,128)(2,1)S(1)}, bf16[1024,256]{1,0:T(8,128)(2,1)S(1)}, u32[]{:S(2)}, u32[]{:S(2)}) collective-permute-start(bf16[1024,256]{1,0:T(8,128)(2,1)S(1)} %pad_maximum_fusion.3.refs_8_.refs_3_), channel_id=1, source_target_pairs={{0,4},{4,0},{1,5},{5,1},{2,6},{6,2},{3,7},{7,3},{8,12},{12,8},{9,1... | collective-permute-start | bytes 1572872 | tf_op jit(solution)/shard_map/outer_w_x/ppermute | solution.py:698
  116.9 16.1 %collective-permute-start.25 = (bf16[1024,256]{1,0:T(8,128)(2,1)}, bf16[1024,256]{1,0:T(8,128)(2,1)S(1)}, u32[]{:S(2)}, u32[]{:S(2)}) collective-permute-start(bf16[1024,256]{1,0:T(8,128)(2,1)} %collective-permute-done.18.refs_5_.refs_10_), channel_id=1, source_target_pairs={{0,1},{1,0},{2,3},{3,2},{4,5},{5,4},{6,7},{7,6},{8,9},{9,8},{10,11... | collective-permute-start | bytes 1572872 | tf_op jit(solution)/shard_map/gate_w_far_t/ppermute | solution.py:698
  193.2 57.6 %reduce-scatter.5.cloned.1.call-start = ((), (), s32[]{:S(2)}) async-start(), calls=%async_computation.7 | async-start | bytes 1310720 | tf_op jit(solution)/shard_map/reduce_scatter | solution.py:966
  233.5 17.4 %collective-permute-start.39 = (bf16[8,256,128]{2,1,0:T(8,128)(2,1)S(1)}, bf16[8,256,128]{2,1,0:T(8,128)(2,1)S(1)}, u32[]{:S(2)}, u32[]{:S(2)}) collective-permute-start(bf16[8,256,128]{2,1,0:T(8,128)(2,1)S(1)} %add_convert_fusion.4), channel_id=1, source_target_pairs={{0,4},{4,0},{1,5},{5,1},{2,6},{6,2},{3,7},{7,3},{8,12},{12,8},{9,1... | collective-permute-start | bytes 1572872 | tf_op jit(solution)/shard_map/outer_g_sum_x/ppermute | solution.py:698
  234.7 16.1 %collective-permute-start.38 = (bf16[8,256,128]{2,1,0:T(8,128)(2,1)S(1)}, bf16[8,256,128]{2,1,0:T(8,128)(2,1)S(1)}, u32[]{:S(2)}, u32[]{:S(2)}) collective-permute-start(bf16[8,256,128]{2,1,0:T(8,128)(2,1)S(1)} %add_convert_fusion.5), channel_id=1, source_target_pairs={{0,1},{1,0},{2,3},{3,2},{4,5},{5,4},{6,7},{7,6},{8,9},{9,8},{10,11... | collective-permute-start | bytes 1572872 | tf_op jit(solution)/shard_map/gate_g_sum_t/ppermute | solution.py:698
  237.6 19.7 %collective-permute-start.44 = (bf16[32,2048]{1,0:T(8,128)(2,1)}, bf16[32,2048]{1,0:T(8,128)(2,1)}, u32[]{:S(2)}, u32[]{:S(2)}) collective-permute-start(bf16[32,2048]{1,0:T(8,128)(2,1)} %get-tuple-element.405), channel_id=1, source_target_pairs={{0,4},{4,0},{1,5},{5,1},{2,6},{6,2},{3,7},{7,3},{8,12},{12,8},{9,1... | collective-permute-start | bytes 393224 | tf_op jit(solution)/shard_map/rows_x/ppermute | solution.py:698
  253.6 44.0 %all-to-all-start = ((bf16[8,512,128]{2,1,0:T(8,128)(2,1)}), bf16[8,512,128]{2,1,0:T(8,128)(2,1)S(1)}, u32[]{:S(2)}, u32[]{:S(2)}) async-start(bf16[8,512,128]{2,1,0:T(8,128)(2,1)} %pad_maximum_fusion), calls=%async_computation.2 | async-start | bytes 2097152 | tf_op jit(solution)/shard_map/all_to_all | solution.py:726
  258.3 18.6 %collective-permute-start.41 = (bf16[2,8,128,128]{3,2,1,0:T(8,128)(2,1)}, bf16[2,8,128,128]{3,2,1,0:T(8,128)(2,1)S(1)}, u32[]{:S(2)}, u32[]{:S(2)}) collective-permute-start(bf16[2,8,128,128]{3,2,1,0:T(8,128)(2,1)} %get-tuple-element.333), channel_id=1, source_target_pairs={{0,4},{4,0},{1,5},{5,1},{2,6},{6,2},{3,7},{7,3},{8,12},{12,8},{9,1... | collective-permute-start | bytes 1572872 | tf_op jit(solution)/shard_map/stream_g_x/ppermute | solution.py:698
  259.4 17.5 %collective-permute-start.42 = (bf16[2,8,128,128]{3,2,1,0:T(8,128)(2,1)}, bf16[2,8,128,128]{3,2,1,0:T(8,128)(2,1)S(1)}, u32[]{:S(2)}, u32[]{:S(2)}) collective-permute-start(bf16[2,8,128,128]{3,2,1,0:T(8,128)(2,1)} %get-tuple-element.334), channel_id=1, source_target_pairs={{0,1},{1,0},{2,3},{3,2},{4,5},{5,4},{6,7},{7,6},{8,9},{9,8},{10,11... | collective-permute-start | bytes 1572872 | tf_op jit(solution)/shard_map/stream_g_t/ppermute | solution.py:698
  262.8 19.4 %collective-permute-start.48 = (bf16[32,2048]{1,0:T(8,128)(2,1)S(1)}, bf16[32,2048]{1,0:T(8,128)(2,1)S(1)}, u32[]{:S(2)}, u32[]{:S(2)}) collective-permute-start(bf16[32,2048]{1,0:T(8,128)(2,1)S(1)} %get-tuple-element.403), channel_id=1, source_target_pairs={{0,4},{4,0},{1,5},{5,1},{2,6},{6,2},{3,7},{7,3},{8,12},{12,8},{9,1... | collective-permute-start | bytes 393224 | tf_op jit(solution)/shard_map/rows_x/ppermute | solution.py:698
  279.0 17.9 %collective-permute-start.46 = (bf16[8,128,128]{2,1,0:T(8,128)(2,1)S(1)}, bf16[8,128,128]{2,1,0:T(8,128)(2,1)}, u32[]{:S(2)}, u32[]{:S(2)}) collective-permute-start(bf16[8,128,128]{2,1,0:T(8,128)(2,1)S(1)} %fusion.4), channel_id=1, source_target_pairs={{0,4},{4,0},{1,5},{5,1},{2,6},{6,2},{3,7},{7,3},{8,12},{12,8},{9,1... | collective-permute-start | bytes 786440 | tf_op jit(solution)/shard_map/stream_g_sum_x/ppermute | solution.py:698
  280.1 16.8 %collective-permute-start.45 = (bf16[8,128,128]{2,1,0:T(8,128)(2,1)S(1)}, bf16[8,128,128]{2,1,0:T(8,128)(2,1)S(1)}, u32[]{:S(2)}, u32[]{:S(2)}) collective-permute-start(bf16[8,128,128]{2,1,0:T(8,128)(2,1)S(1)} %fusion.5), channel_id=1, source_target_pairs={{0,1},{1,0},{2,3},{3,2},{4,5},{5,4},{6,7},{7,6},{8,9},{9,8},{10,11... | collective-permute-start | bytes 786440 | tf_op jit(solution)/shard_map/stream_g_sum_t/ppermute | solution.py:698
  281.9 15.7 %collective-permute-start.47 = (bf16[64,2048]{1,0:T(8,128)(2,1)S(1)}, bf16[64,2048]{1,0:T(8,128)(2,1)}, u32[]{:S(2)}, u32[]{:S(2)}) collective-permute-start(bf16[64,2048]{1,0:T(8,128)(2,1)S(1)} %pad_maximum_fusion.8.refs_2_), channel_id=1, source_target_pairs={{0,1},{1,0},{2,3},{3,2},{4,5},{5,4},{6,7},{7,6},{8,9},{9,8},{10,11... | collective-permute-start | bytes 786440 | tf_op jit(solution)/shard_map/rows_t/ppermute | solution.py:698
  300.8 19.0 %all-to-all-start.1 = ((bf16[8,256,128]{2,1,0:T(8,128)(2,1)}), bf16[8,256,128]{2,1,0:T(8,128)(2,1)S(1)}, u32[]{:S(2)}, u32[]{:S(2)}) async-start(bf16[8,256,128]{2,1,0:T(8,128)(2,1)} %pad_maximum_fusion.4), calls=%async_computation.3 | async-start | bytes 1048576 | tf_op jit(solution)/shard_map/all_to_all | solution.py:726
  (102 other events, 1422.0 us)
Sparse Core Ops, SparseCore 0:
  27.3 41.6 all-gather.2
  96.4 28.7 all-gather.4
  193.4 25.0 reduce-scatter.2
  221.3 25.7 reduce-scatter.4

commit v4 on v3

--- a/solution.py
+++ b/solution.py
@@ -1,4 +1,5 @@
 from functools import partial
+from inspect import isgeneratorfunction
 
 import jax
 import jax.numpy as jnp
@@ -25,6 +26,7 @@
 GROUP = 8
 CHUNK = 64
 UNROLL = 2
+LOAD, STORE = 0, 1
 F32 = jnp.float32
 BF16 = jnp.bfloat16
 NT = ((1,), (1,))
@@ -64,11 +66,22 @@
         ]
         for copy in loads:
             copy.start()
-        for copy in loads:
-            copy.wait()
-        kernel(*refs[:few], *held, *results, *rest)
-        for copy in stores:
-            copy.start()
+        asked = {LOAD: set(), STORE: set()}
+
+        def ask(kind, numbers):
+            for i in numbers:
+                if i not in asked[kind]:
+                    asked[kind].add(i)
+                    loads[i].wait() if kind == LOAD else stores[i].start()
+
+        lazy = isgeneratorfunction(getattr(kernel, "func", kernel))
+        if not lazy:
+            ask(LOAD, range(many))
+        parts = kernel(*refs[:few], *held, *results, *rest)
+        for kind, numbers in parts if lazy else ():
+            ask(kind, numbers)
+        ask(LOAD, range(many))
+        ask(STORE, range(made))
         for copy in stores:
             copy.wait()
 
@@ -312,6 +325,7 @@
     sizes, core_ref, tensor_ref, z_ref, x_ref, place_ref, own, by_x, by_t, low, high, par_ref, sel_ref,
     n_ref, stream_ref, act_ref, mine_ref, other_ref, pos_ref, gain_ref, nrm, act_low,
 ):
+    yield LOAD, (0, 1)
     taps, per_device = sizes
     rows = x_ref.shape[0]
     width = n_ref.shape[1]
@@ -344,15 +358,20 @@
 
     lax.fori_loop(0, rows // 64, norm, 0)
     reorder_rows(z_ref, row_matches(place_ref[...], rows), nrm, n_ref)
+    yield STORE, (0, 5, 6)
+    yield LOAD, (2, 3, 4, 5, 6)
     near, far = column_sum(n_ref, (own, by_x, by_t, low, high))
     stream_ref[:, :part] = near
     stream_ref[:, part:] = far
+    yield STORE, (1,)
+    yield LOAD, (7, 8)
     masks = lag_masks(place, taps)
     for at in tiles(2 * part, LANES):
         filtered = filter_sum(stream_ref[:, at], masks, par_ref[:, at])
         act = filtered * jax.nn.sigmoid(filtered)
         act_ref[:, at] = act
         act_low[:, at] = act.astype(BF16)
+    yield STORE, (2,)
     selected = dot(sel_ref[...], act_low[...], NT)
     first = core_ref[0] == 0
     mine_ref[...] = jnp.where(first, selected[:, : rows // 2], selected[:, rows // 2 :])
@@ -363,24 +382,38 @@
     gate_pieces, out_pieces = refs[:4], refs[4:8]
     up_ref, gate_ref, gg_ref = refs[8:]
     part = gate_pieces[0].shape[1]
+    yield LOAD, (0, 1)
     reorder_rows(z_ref, row_matches(place_ref[...], cot_ref.shape[0]), cot_ref, up_ref)
-    for source, out, pieces in ((n_ref, gate_ref, gate_pieces), (up_ref, gg_ref, out_pieces)):
+    yield STORE, (0,)
+    for i, (source, out, pieces) in enumerate(
+        ((n_ref, gate_ref, gate_pieces), (up_ref, gg_ref, out_pieces))
+    ):
+        yield LOAD, (2, *range(3 + 4 * i, 7 + 4 * i))
         near, far = column_sum(source, pieces)
         out[:, :part] = near
         out[:, part:] = far
+        yield STORE, (1 + i,)
 
 
 def out_kernel(z_ref, place_ref, gated_ref, *refs):
+    yield LOAD, (0, 1)
     order = column_matches(place_ref[...], gated_ref.shape[0])
     rows = dot(order, gated_ref[...]).astype(BF16)
+    yield LOAD, (2, 3, 4, 5)
     row_sum(z_ref, [(rows, refs[:4])], refs[4:])
 
 
 def late_grad_kernel(z_ref, n_ref, up_ref, gate_grad_ref, gated_ref, *outs):
-    for i, (source, rows_ref) in enumerate(((gate_grad_ref, n_ref), (gated_ref, up_ref))):
-        grad_pieces(
-            z_ref, source[...].astype(F32).T.astype(BF16), rows_ref, [[v] for v in outs[4 * i : 4 * i + 4]]
-        )
+    gate_own, gate_t, outer_own, outer_x, x_way, t_way = outs
+    for source, rows_ref, pieces, needs, ends in (
+        (gate_grad_ref, n_ref, (gate_own, x_way.at[1], gate_t, x_way.at[0]), (2, 0), (4, 1, 0)),
+        (gated_ref, up_ref, (outer_own, outer_x, t_way.at[1], t_way.at[0]), (3, 1), (5, 3, 2)),
+    ):
+        yield LOAD, needs[:1]
+        channels_t = source[...].astype(F32).T.astype(BF16)
+        yield LOAD, needs[1:]
+        grad_pieces(z_ref, channels_t, rows_ref, [[v] for v in pieces])
+        yield STORE, ends
 
 
 def back_kernel(
@@ -388,6 +421,7 @@
     low_ref, small_ref, *refs,
 ):
     *outs, act_low, grad_t = refs
+    yield LOAD, (0, 1, 2, 3, 4, 5, 6)
     rows, channels = stream_ref.shape
     first = core_ref[0] == 0
     total, rest = total_ref[...], rest_ref[...]
@@ -427,7 +461,10 @@
         small_ref[count:, at] = jnp.concatenate(sums, 0).astype(BF16)
         low_ref[:, at] = stream_grad.astype(BF16)
         grad_t[at, :] = stream_grad.T.astype(BF16)
+    yield STORE, (0,)
     small_ref[:count, :] = dot(selected_low, act_low[...]).astype(BF16)
+    yield STORE, (1,)
+    yield LOAD, (7,)
     own_low, own_high, by_x_high, by_t_low, x_way, t_way = outs
     grad_pieces(
         z_ref, grad_t[...], n_ref,
@@ -441,9 +478,11 @@
 def in_kernel(z_ref, place_ref, low_ref, gate_grad_ref, *refs):
     stream_pieces, gate_pieces, outs, stage = refs[:5], refs[5:9], refs[9:11], refs[11]
     channels = low_ref.shape[1]
+    yield LOAD, (0, 1, 2)
     order = column_matches(place_ref[...], low_ref.shape[0])
     stage[:, :channels] = dot(order, low_ref[...]).astype(BF16)
     stage[:, channels:] = dot(order, gate_grad_ref[...]).astype(BF16)
+    yield LOAD, range(3, 12)
     row_sum(
         z_ref, [(stage[:, :channels], stream_pieces), (stage[:, channels:], gate_pieces)], outs
     )
@@ -488,6 +527,7 @@
         lax.broadcasted_iota(jnp.int32, (states, wide), 1) // lanes
         == lax.broadcasted_iota(jnp.int32, (states, wide), 0)
     ).astype(F32).astype(BF16)
+    yield LOAD, (4, 5)
     total, rest = total_ref[...], rest_ref[...]
     sel_t[:, : rows // 2] = jnp.where(first, total, rest)
     sel_t[:, rows // 2 :] = jnp.where(first, rest, total)
@@ -653,7 +693,9 @@
         rank_t[...] += dot(sw_ref[:, at], spre_low[...], NT)
         return 0
 
+    yield LOAD, (0, 1, 2, 3, 6, 7)
     lax.fori_loop(0, channels // both, one_block, 0)
+    yield STORE, (0, 1, 2, 3)
     high, low = slice(0, rows // 2), slice(rows // 2, rows)
     for acc, base in ((ci_acc, rank_width), (co_acc, rank_width + states)):
         sel_t[base : base + states, :] = dot(acc[...].astype(BF16), spread, NT).T
@@ -832,10 +874,6 @@
     lengths = jnp.concatenate([lengths, jnp.zeros((1, ring_rows - lengths.shape[1]), BF16)], 1)
     note = jnp.concatenate([gain, lengths, jnp.zeros((share - 2, ring_rows), BF16)], 0)
     noted, plain = shape((share, width + LANES), BF16), shape((share, width), BF16)
-    blocks = step(kept, *blocks)[1:]
-    rows_out = whole(
-        prep_kernel, "prep", [xi], (send_place[None], *blocks, note), [noted, noted, plain, plain]
-    )
     first = (zi * 2 + ki) * part
 
     def own_channels(value):
@@ -864,25 +902,29 @@
     def gathered(keep, send):
         return lax.all_gather(jnp.concatenate([keep, send], 0), ZK, axis=0, tiled=True)
 
-    tok_keep, tok_send, cot_keep, cot_send = rows_out
     (other_core,) = step(swap(sent, "k", "weights"))
     packed = whole(
         second_pack_kernel, "pack_cores", [ki], (kept, other_core),
         [shape((2 * ring_rows, part), BF16)] * blocks_w,
     )
-    tok_got = swap(tok_send, "x", "tokens")
+    *packed, tok, cot = step(*packed, *blocks)
+    tok_keep, tok_send, cot_keep, cot_send = whole(
+        prep_kernel, "prep", [xi], (send_place[None], tok, cot, note), [noted, noted, plain, plain]
+    )
+    stream_own, floats_t, lows_t, tok_keep, tok_send, cot_keep, cot_send, *packed = step(
+        jnp.concatenate(from_z(packed[:zs], "stream_w"), 0),
+        swap(floats, "t", "params"), swap(lows, "t", "params_low"),
+        tok_keep, tok_send, cot_keep, cot_send, *packed[zs:],
+    )
+    tok_got, stream_own = step(swap(tok_send, "x", "tokens"), stream_own)
     group_tokens = gathered(tok_keep, tok_got)
-    stream_own, floats_t, lows_t, *packed = step(
-        jnp.concatenate(from_z(packed[:zs], "stream_w"), 0),
-        swap(floats, "t", "params"), swap(lows, "t", "params_low"), *packed[zs:],
-    )
-    stream_x, stream_t, gate_own, *packed = step(
-        swap(stream_own, "x", "stream_w"), swap(stream_own, "t", "stream_w"),
-        jnp.concatenate(from_z(packed[:zs], "gate_w"), 0), *packed[zs:],
-    )
     params = jnp.concatenate([floats, floats_t], axis=1)
     lows = jnp.concatenate([lows, lows_t], axis=1)
-    step_w, select_w = lows[:rank_width], lows[rank_width:]
+    stream_x, stream_t, gate_own, params, step_w, select_w, arrived, returned, *packed = step(
+        swap(stream_own, "x", "stream_w"), swap(stream_own, "t", "stream_w"),
+        jnp.concatenate(from_z(packed[:zs], "gate_w"), 0), params, lows[:rank_width],
+        lows[rank_width:], arrived, returned, *packed[zs:],
+    )
     stream_low, stream_high, outer_own, cot_got, gate_own, group_tokens = step(
         swap(stream_x[:half], "t", "stream_w_far"), swap(stream_t[half:], "x", "stream_w_far"),
         jnp.concatenate(from_z(packed, "outer_w"), 0), swap(cot_send, "x", "cot"),
@@ -929,18 +971,17 @@
     sent = (sel_mine + got).astype(BF16)
     pieces = whole(
         late_grad_kernel, "late_grad", [zi], (normed, upstream, gate_grad, gated),
-        [shape((2 * zs, part, ring_rows), BF16)] * 8,
+        [shape((2 * zs, part, ring_rows), BF16)] * 4
+        + [shape((2, 2 * zs, part, ring_rows), BF16)] * 2,
     )
     got, out_got, sent, *pieces = step(
         exchange_z(sent, 1, "select"), swap(out_other, "k", "rows"), sent, *pieces
     )
     out_total = plus(out_mine, out_got)
-    gate_g, outer_g = pieces[:4], pieces[4:]
     sent = plus(sent, got)
     got, sent, out_total, *pieces = step(
         exchange_z(sent, 2, "select"), sent, out_total, *pieces
     )
-    gate_g, outer_g = pieces[:4], pieces[4:]
     out_back = lax.psum_scatter(out_total, "z", scatter_dimension=0, tiled=True)
     total = sent.astype(F32) + got.astype(F32)
     rest = swap(total, "k", "select_rest")
@@ -952,31 +993,25 @@
         + [shape((2, 2 * zs, part // 2, ring_rows), BF16)] * 2,
         [pltpu.VMEM((group_rows, channels), BF16), pltpu.VMEM((channels, group_rows), BF16)],
     )
-    gate_far, outer_far, low, small_b, *more = step(
-        swap(gate_g[3], "x", "gate_g_far"), swap(outer_g[3], "t", "outer_g_far"), low, small_b,
-        *pieces, *stream_g,
-    )
-    pieces, stream_g = more[:8], more[8:]
-    gate_g, outer_g = pieces[:4], pieces[4:]
+    gate_own_g, gate_t_g, outer_own_g, outer_x_g, x_way_l, t_way_l = pieces
     in_mine, in_other = whole(
         in_kernel, "in_rows", [zi], (returned, low, gate_grad, *ws, *wg),
         half_rows, [pltpu.VMEM((group_rows, 2 * channels), BF16)],
     )
+    x_way_l, t_way_l, in_mine, in_other, out_back, small_b, *stream_g = step(
+        swap(x_way_l, "x", "late_g"), swap(t_way_l, "t", "late_g"), in_mine, in_other, out_back,
+        small_b, *stream_g,
+    )
     in_total = plus(in_mine, swap(in_other, "k", "rows"))
     in_back = lax.psum_scatter(in_total, "z", scatter_dimension=0, tiled=True)
-    gate_first, outer_first, _, out_back, *pieces = step(
-        swap(gate_g[1], "x", "gate_g"), swap(outer_g[2], "t", "outer_g"), in_total, out_back,
-        *pieces,
-    )
-    gate_g, outer_g = pieces[:4], pieces[4:]
     small = jnp.concatenate([small_a, small_b], axis=0)
-    gate_second, outer_second, small_got, small, in_back, *stream_g = step(
-        swap(plus(gate_g[2], gate_far), "t", "gate_g_sum"),
-        swap(plus(outer_g[1], outer_far), "x", "outer_g_sum"),
-        swap(small[:, part:], "t", "small"), small, in_back, *stream_g,
+    gate_second, outer_second, small_got, small, *stream_g = step(
+        swap(plus(gate_t_g, x_way_l[0]), "t", "gate_g_sum"),
+        swap(plus(outer_x_g, t_way_l[0]), "x", "outer_g_sum"),
+        swap(small[:, part:], "t", "small"), small, *stream_g,
     )
     late_sum = jnp.concatenate(
-        [plus(gate_g[0], gate_first, gate_second), plus(outer_g[0], outer_first, outer_second)],
+        [plus(gate_own_g, x_way_l[1], gate_second), plus(outer_own_g, t_way_l[1], outer_second)],
         axis=1,
     )
     late_home = to_owners(late_sum)
@@ -986,25 +1021,23 @@
     def near_rows(rows):
         return jnp.concatenate([rows[:share], swap(rows[share:], "x", "rows")], 0)
 
-    x_way, t_way, small_got, small, out_near = step(
+    x_way, t_way, small_got, small, out_near, in_near = step(
         swap(x_way, "x", "stream_g"), swap(t_way, "t", "stream_g"), swap(small, "x", "small"),
-        small, near_rows(out_back),
+        small, near_rows(out_back), near_rows(in_back),
     )
     small = plus(small, small_got)
     if rings > 1:
         small = lax.psum(small.astype(F32), "r").astype(BF16)
-    low_second, high_second, out_far, out_near, in_near, late_home, *gathered_small = step(
+    low_second, high_second, out_far, in_far, *gathered_small = step(
         swap(plus(by_t_low, x_way[0]), "t", "stream_g_sum"),
         swap(plus(by_x_high, t_way[0]), "x", "stream_g_sum"),
-        swap(out_near, "t", "rows"), out_near, near_rows(in_back), late_home,
+        swap(out_near, "t", "rows"), swap(in_near, "t", "rows"),
         *from_z([small] * zs, "small"),
     )
     stream_sum = jnp.concatenate(
         [plus(own_low, x_way[1], low_second), plus(own_high, t_way[1], high_second)], axis=1
     )
-    stream_home, in_far, in_near = step(
-        to_owners(stream_sum), swap(in_near, "t", "rows"), in_near
-    )
+    stream_home = to_owners(stream_sum)
     small_blocks = [v for block in gathered_small for v in (block, swap(block, "k", "small"))]
 
     back_place = send_place[:, None]
@@ -1046,6 +1079,9 @@
             one_row, one_row, one_row,
         ],
     )
+    late_home, stream_home, output, input_grad, select_grad = step(
+        late_home, stream_home, output, input_grad, select_grad
+    )
     gate_home, outer_home = late_home[:, :part], late_home[:, part:]
     outer_home = outer_home.reshape(half_channels, ring_rows).astype(F32)
     inner_home = jnp.stack(

time: 337 us -> 320 us (0.950)
  starting transfers between devices: 87.3 us -> 76 us
  other arithmetic: 29.1 us -> 23.1 us
    ppermute x42 -> x40, starting transfers between devices: 41.4 us -> 35.7 us  [swap(): return lax.ppermute(value, axis, SWAP)]
    ppermute x4, starting transfers between devices: 8.77 us -> 4.25 us  [exchange_z(): return lax.ppermute(value, 'z', [(i, i ^ distance) for i in range(size)])]
    ppermute x42 -> x40, waiting for transfers between devices: 52.3 us -> 49.6 us  [swap(): return lax.ppermute(value, axis, SWAP)]
    convert_element_type x13 -> x12, other arithmetic: 9.41 us -> 8.2 us  [plus(): return total.astype(BF16)]
  transfers between devices with their start and end apart: 64 -> 62, of which waited for: 26 -> 23; matrix products, arithmetic and copies ran while one was open for 9% -> 7% of each run, Pallas kernels for 16% -> 16%
where the time goes in v4:
time: 320 us; the launch traced here: 319 us
  waiting for transfers between devices  106 us (33%)
  Pallas kernels  79 us (25%)
  starting transfers between devices  76 us (24%)
  other arithmetic  23.1 us (7%)
  local copies, waits for them, and re-layouts  20.2 us (6%)
  between operations  14.9 us (5%)
    pallas_call x13, Pallas kernels, whole(): pl.pallas_call(copied, in_specs=[pl.BlockSpec(memory_space=pltpu.SMEM)] *...  79 us
    ppermute x40, waiting for transfers between devices, swap(): return lax.ppermute(value, axis, SWAP)  49.6 us
    ppermute x12, waiting for transfers between devices, from_z(): lax.ppermute(blocks[shift], 'z', [(i, (i + shift) % size) for i in range(...  37.2 us
    ppermute x40, starting transfers between devices, swap(): return lax.ppermute(value, axis, SWAP)  35.7 us
    ppermute x12, starting transfers between devices, from_z(): lax.ppermute(blocks[shift], 'z', [(i, (i + shift) % size) for i in range(...  27.4 us
    ppermute x4, waiting for transfers between devices, exchange_z(): return lax.ppermute(value, 'z', [(i, i ^ distance) for i in range(size)])  13.6 us
    unnamed x128, local copies, waits for them, and re-layouts  13 us
    convert_element_type x12, other arithmetic, plus(): return total.astype(BF16)  8.2 us
  transfers between devices with their start and end apart: 62, of which 23 were waited for; matrix products, arithmetic and copies ran while one was open for 7% of the time, Pallas kernels for 16%

profile of v4, /device:TPU:0, one launch (start us, length us, event | category | flops | bytes accessed | tf_op | source)
XLA Modules:
  0.0 318.9 jit_solution(16573404739382416277)
XLA Ops:
  22.6 4.1 %collective-permute-start.3 = (bf16[256,256]{1,0:T(8,128)(2,1)}, bf16[256,256]{1,0:T(8,128)(2,1)S(1)}, u32[]{:S(2)}, u32[]{:S(2)}) collective-permute-start(bf16[256,256]{1,0:T(8,128)(2,1)} %get-tuple-element.216), channel_id=1, source_target_pairs={{0,24},{8,0},{16,8},{24,16},{1,25},{9,1},{17,9},{25,17},{2,26},{10... | collective-permute-start | bytes 393224 | tf_op jit(solution)/shard_map/stream_w_z/ppermute | solution.py:755
  31.3 7.0 %collective-permute-done.2 = bf16[256,256]{1,0:T(8,128)(2,1)S(1)} collective-permute-done((bf16[256,256]{1,0:T(8,128)(2,1)}, bf16[256,256]{1,0:T(8,128)(2,1)S(1)}, u32[]{:S(2)}, u32[]{:S(2)}) %collective-permute-start.2) | collective-permute-done | bytes 131104 | tf_op jit(solution)/shard_map/stream_w_z/ppermute | solution.py:755
  40.8 3.8 %collective-permute-done.6 = bf16[32,2176]{1,0:T(8,128)(2,1)S(1)} collective-permute-done((bf16[32,2176]{1,0:T(8,128)(2,1)}, bf16[32,2176]{1,0:T(8,128)(2,1)S(1)}, u32[]{:S(2)}, u32[]{:S(2)}) %collective-permute-start.6) | collective-permute-done | bytes 139296 | tf_op jit(solution)/shard_map/tokens_x/ppermute | solution.py:740
  57.2 15.1 %collective-permute-done.10 = bf16[256,256]{1,0:T(8,128)(2,1)S(1)} collective-permute-done((bf16[256,256]{1,0:T(8,128)(2,1)S(1)}, bf16[256,256]{1,0:T(8,128)(2,1)S(1)}, u32[]{:S(2)}, u32[]{:S(2)}) %collective-permute-start.10) | collective-permute-done | bytes 131104 | tf_op jit(solution)/shard_map/gate_w_z/ppermute | solution.py:755
  73.5 10.2 %collective-permute-start.15 = (bf16[256,256]{1,0:T(8,128)(2,1)}, bf16[256,256]{1,0:T(8,128)(2,1)S(1)}, u32[]{:S(2)}, u32[]{:S(2)}) collective-permute-start(bf16[256,256]{1,0:T(8,128)(2,1)} %get-tuple-element.248), channel_id=1, source_target_pairs={{0,16},{8,24},{16,0},{24,8},{1,17},{9,25},{17,1},{25,9},{2,18},{10... | collective-permute-start | bytes 393224 | tf_op jit(solution)/shard_map/outer_w_z/ppermute | solution.py:755
  87.6 4.4 %collective-permute-done.15 = bf16[256,256]{1,0:T(8,128)(2,1)S(1)} collective-permute-done((bf16[256,256]{1,0:T(8,128)(2,1)}, bf16[256,256]{1,0:T(8,128)(2,1)S(1)}, u32[]{:S(2)}, u32[]{:S(2)}) %collective-permute-start.15) | collective-permute-done | bytes 131104 | tf_op jit(solution)/shard_map/outer_w_z/ppermute | solution.py:755
  99.9 7.6 %front.1 = (bf16[512,2048]{1,0:T(8,128)(2,1)}, f32[512,512]{1,0:T(8,128)}, f32[512,512]{1,0:T(8,128)}, f32[160,256]{1,0:T(8,128)}, f32[160,256]{1,0:T(8,128)}, /*index=5*/f32[512,128]{1,0:T(8,128)}, f32[8,2048]{1,0:T(8,128)}) custom-call(s32[1]{0:T(128)} %bitcast.refs_1_.refs_0_, s32[1]{0:T(128)} %bitcast.1.refs_1_, s32[1]{0:T(128)} %bitcast.2.refs_0_.refs_2_.refs_1_, ...), custom_call_target="tpu_custom_call" | custom-call | bytes 29520000 | tf_op jit(solution)/shard_map/front/pallas_call | solution.py:88
  114.8 3.9 %collective-permute-done.22.refs_6_.refs_11_ = bf16[1024,256]{1,0:T(8,128)(2,1)} collective-permute-done((bf16[1024,256]{1,0:T(8,128)(2,1)S(1)}, bf16[1024,256]{1,0:T(8,128)(2,1)}, u32[]{:S(2)}, u32[]{:S(2)}) %collective-permute-start.22) | collective-permute-done | bytes 524320 | tf_op jit(solution)/shard_map/gate_w_t/ppermute | solution.py:740
  118.7 4.4 %collective-permute-done.21 = bf16[160,256]{1,0:T(8,128)(2,1)S(1)} collective-permute-done((bf16[160,256]{1,0:T(8,128)(2,1)S(1)}, bf16[160,256]{1,0:T(8,128)(2,1)S(1)}, u32[]{:S(2)}, u32[]{:S(2)}) %collective-permute-start.21) | collective-permute-done | bytes 81952 | tf_op jit(solution)/shard_map/select_z/ppermute | solution.py:746
  123.3 6.0 %collective-permute-done.24 = bf16[160,256]{1,0:T(8,128)(2,1)S(1)} collective-permute-done((bf16[160,256]{1,0:T(8,128)(2,1)S(1)}, bf16[160,256]{1,0:T(8,128)(2,1)S(1)}, u32[]{:S(2)}, u32[]{:S(2)}) %collective-permute-start.24) | collective-permute-done | bytes 81952 | tf_op jit(solution)/shard_map/select_z/ppermute | solution.py:746
  130.3 6.5 %late.1 = (bf16[512,2048]{1,0:T(8,128)(2,1)}, f32[512,512]{1,0:T(8,128)}, f32[512,512]{1,0:T(8,128)}) custom-call(s32[1]{0:T(128)} %bitcast.2.refs_0_.refs_2_.refs_1_, bf16[512,2048]{1,0:T(8,128)(2,1)} %all-gather.5.cloned.1.call-done.refs_1_, s32[1,512]{1,0:T(1,128)} %reshape.380.refs_4_.refs_2_, ...), custom_call_target="tpu_custom_call" | custom-call | bytes 29520000 | tf_op jit(solution)/shard_map/late/pallas_call | solution.py:88
  137.4 24.1 %mixer.1 = (bf16[512,512]{1,0:T(8,128)(2,1)}, bf16[512,512]{1,0:T(8,128)(2,1)}, f32[512,512]{1,0:T(8,128)}, bf16[152,512]{1,0:T(8,128)(2,1)}, f32[160,256]{1,0:T(8,128)}, /*index=5*/f32[160,256]{1,0:T(8,128)}) custom-call(s32[1]{0:T(128)} %bitcast.refs_1_.refs_0_, f32[512,128]{1,0:T(8,128)} %get-tuple-element.260.refs_1_.refs_4_, ...), custom_call_target="tpu_custom_call" | custom-call | bytes 88560000 | tf_op jit(solution)/shard_map/mixer/pallas_call | solution.py:88
  162.5 4.4 %out_rows.1 = (bf16[256,2048]{1,0:T(8,128)(2,1)}, bf16[256,2048]{1,0:T(8,128)(2,1)}) custom-call(s32[1]{0:T(128)} %bitcast.2.refs_0_.refs_2_.refs_1_, s32[512,1]{1,0:T(8,128)} %copy.52.refs_1_, bf16[512,512]{1,0:T(8,128)(2,1)} %get-tuple-element.298.refs_2_.refs_4_, bf16[1024,256]{1,0:T(8,128)(2,1)} %copy-done.2, bf16[1024,256]{1,0:T(8,128)(2,1)} %copy-done.9, ...), custom_call_target="tpu_custom_call" | custom-call | bytes 18450000 | tf_op jit(solution)/shard_map/out_rows/pallas_call | solution.py:88
  167.6 6.7 %late_grad.1 = (bf16[8,256,128]{2,1,0:T(8,128)(2,1)}, bf16[8,256,128]{2,1,0:T(8,128)(2,1)}, bf16[8,256,128]{2,1,0:T(8,128)(2,1)}, bf16[8,256,128]{2,1,0:T(8,128)...) custom-call(s32[1]{0:T(128)} %bitcast.2.refs_0_.refs_2_.refs_1_, ...), custom_call_target="tpu_custom_call" | custom-call | bytes 22140000 | tf_op jit(solution)/shard_map/late_grad/pallas_call | solution.py:88
  186.9 6.3 %back.1 = (bf16[512,512]{1,0:T(8,128)(2,1)}, bf16[168,512]{1,0:T(8,128)(2,1)}, bf16[8,128,128]{2,1,0:T(8,128)(2,1)}, bf16[8,128,128]{2,1,0:T(8,128)(2,1)}, bf16[...) custom-call(s32[1]{0:T(128)} %bitcast.refs_1_.refs_0_, ...), custom_call_target="tpu_custom_call" | custom-call | bytes 25830000 | tf_op jit(solution)/shard_map/back/pallas_call | solution.py:88
  193.3 6.3 %in_rows.1 = (bf16[256,2048]{1,0:T(8,128)(2,1)}, bf16[256,2048]{1,0:T(8,128)(2,1)}) custom-call(s32[1]{0:T(128)} %bitcast.2.refs_0_.refs_2_.refs_1_, s32[512,1]{1,0:T(8,128)} %copy.52.refs_1_, bf16[512,512]{1,0:T(8,128)(2,1)} %get-tuple-element.322.refs_2_, bf16[512,512]{1,0:T(8,128)(2,1)} %get-tuple-element.297.refs_3_, bf16[1024,256]{1,0:T(8,128)(2,1)} %copy-done.3, ...), custom_call_target="tpu_custom_call" | custom-call | bytes 25830000 | tf_op jit(solution)/shard_map/in_rows/pallas_call | solution.py:88
  199.6 4.7 %collective-permute-done.32 = bf16[2,8,256,128]{3,2,1,0:T(8,128)(2,1)S(1)} collective-permute-done((bf16[2,8,256,128]{3,2,1,0:T(8,128)(2,1)}, bf16[2,8,256,128]{3,2,1,0:T(8,128)(2,1)S(1)}, u32[]{:S(2)}, u32[]{:S(2)}) %collective-permute-start.32) | collective-permute-done | bytes 1048608 | tf_op jit(solution)/shard_map/late_g_x/ppermute | solution.py:740
  218.9 13.5 %collective-permute-done.41 = bf16[32,2048]{1,0:T(8,128)(2,1)S(1)} collective-permute-done((bf16[32,2048]{1,0:T(8,128)(2,1)S(1)}, bf16[32,2048]{1,0:T(8,128)(2,1)S(1)}, u32[]{:S(2)}, u32[]{:S(2)}) %collective-permute-start.41) | collective-permute-done | bytes 131104 | tf_op jit(solution)/shard_map/rows_x/ppermute | solution.py:740
  234.7 3.6 %all-to-all-start = ((bf16[8,512,128]{2,1,0:T(8,128)(2,1)}), bf16[8,512,128]{2,1,0:T(8,128)(2,1)S(1)}, u32[]{:S(2)}, u32[]{:S(2)}) async-start(bf16[8,512,128]{2,1,0:T(8,128)(2,1)} %pad_maximum_fusion), calls=%async_computation.1 | async-start | bytes 2097152 | tf_op jit(solution)/shard_map/all_to_all | solution.py:768
  244.0 12.1 %collective-permute-done.43 = bf16[32,2048]{1,0:T(8,128)(2,1)S(1)} collective-permute-done((bf16[32,2048]{1,0:T(8,128)(2,1)S(1)}, bf16[32,2048]{1,0:T(8,128)(2,1)S(1)}, u32[]{:S(2)}, u32[]{:S(2)}) %collective-permute-start.43) | collective-permute-done | bytes 131104 | tf_op jit(solution)/shard_map/rows_x/ppermute | solution.py:740
  269.9 5.4 %collective-permute-done.49.refs_6_ = bf16[320,256]{1,0:T(8,128)(2,1)S(1)} collective-permute-done((bf16[320,256]{1,0:T(8,128)(2,1)S(1)}, bf16[320,256]{1,0:T(8,128)(2,1)S(1)}, u32[]{:S(2)}, u32[]{:S(2)}) %collective-permute-start.49) | collective-permute-done | bytes 163872 | tf_op jit(solution)/shard_map/small_z/ppermute | solution.py:755
  276.5 4.5 %collective-permute-done.50.refs_8_ = bf16[320,256]{1,0:T(8,128)(2,1)S(1)} collective-permute-done((bf16[320,256]{1,0:T(8,128)(2,1)S(1)}, bf16[320,256]{1,0:T(8,128)(2,1)S(1)}, u32[]{:S(2)}, u32[]{:S(2)}) %collective-permute-start.50) | collective-permute-done | bytes 163872 | tf_op jit(solution)/shard_map/small_z/ppermute | solution.py:755
  284.7 4.5 %all-to-all-start.1 = ((bf16[8,256,128]{2,1,0:T(8,128)(2,1)}), bf16[8,256,128]{2,1,0:T(8,128)(2,1)S(1)}, u32[]{:S(2)}, u32[]{:S(2)}) async-start(bf16[8,256,128]{2,1,0:T(8,128)(2,1)} %pad_maximum_fusion.4), calls=%async_computation.3 | async-start | bytes 1048576 | tf_op jit(solution)/shard_map/all_to_all | solution.py:768
  293.9 3.5 %input_grad.1 = f32[128,2048]{1,0:T(8,128)} custom-call(s32[1]{0:T(128)} %bitcast.10.refs_0_, s32[128,1]{1,0:T(8,128)} %copy.54.refs_1_, bf16[64,2048]{1,0:T(8,128)(2,1)} %copy-done.17, bf16[64,2048]{1,0:T(8,128)(2,1)} %copy-done.28, bf16[128,2048]{1,0:T(8,128)(2,1)} %refs_4_.3, bf16[128,2048]{1,0:T(8,128)(2,1)} %refs_5_.1, f32[8,2048]{1,0:T(8,128)} %get-tuple-element.369.refs_6_), custom_call_target="tpu_custom_call" | custom-call | bytes 14760000 | tf_op jit(solution)/shard_map/input_grad/pallas_call | solution.py:88
  (313 shorter events, 131.4 us)
Async XLA Ops:
  7.2 86.6 %all-gather.3.cloned.1.call-start = ((), (), s32[]{:S(2)}) async-start(), calls=%async_computation.4 | async-start | bytes 2506752 | tf_op jit(solution)/shard_map/all_gather | solution.py:903
  14.6 24.7 %collective-permute-start.4 = (f32[24,256]{1,0:T(8,128)S(1)}, f32[24,256]{1,0:T(8,128)S(1)}, u32[]{:S(2)}, u32[]{:S(2)}) collective-permute-start(f32[24,256]{1,0:T(8,128)S(1)} %constant_dynamic-slice_fusion.4), channel_id=1, source_target_pairs={{0,1},{1,0},{2,3},{3,2},{4,5},{5,4},{6,7},{7,6},{8,9},{9,8},{10,11... | collective-permute-start | bytes 73736 | tf_op jit(solution)/shard_map/params_t/ppermute | solution.py:740
  18.0 21.2 %collective-permute-start.5 = (bf16[288,256]{1,0:T(8,128)(2,1)S(1)}, bf16[288,256]{1,0:T(8,128)(2,1)S(1)}, u32[]{:S(2)}, u32[]{:S(2)}) collective-permute-start(bf16[288,256]{1,0:T(8,128)(2,1)S(1)} %pad_maximum_fusion.11), channel_id=1, source_target_pairs={{0,1},{1,0},{2,3},{3,2},{4,5},{5,4},{6,7},{7,6},{8,9},{9,8},{10,11... | collective-permute-start | bytes 442376 | tf_op jit(solution)/shard_map/params_low_t/ppermute | solution.py:740
  46.3 83.2 %all-gather.5.cloned.1.call-start = ((), (), s32[]{:S(2)}) async-start(), calls=%async_computation.5 | async-start | bytes 2359296 | tf_op jit(solution)/shard_map/all_gather | solution.py:903
  46.8 25.6 %collective-permute-start.7 = (bf16[1024,256]{1,0:T(8,128)(2,1)S(1)}, bf16[1024,256]{1,0:T(8,128)(2,1)S(1)}, u32[]{:S(2)}, u32[]{:S(2)}) collective-permute-start(bf16[1024,256]{1,0:T(8,128)(2,1)S(1)} %pad_maximum_fusion.1.refs_5_.refs_4_), channel_id=1, source_target_pairs={{0,4},{4,0},{1,5},{5,1},{2,6},{6,2},{3,7},{7,3},{8,12},{12,8},{9,1... | collective-permute-start | bytes 1572872 | tf_op jit(solution)/shard_map/stream_w_x/ppermute | solution.py:740
  48.3 24.1 %collective-permute-start.8 = (bf16[1024,256]{1,0:T(8,128)(2,1)S(1)}, bf16[1024,256]{1,0:T(8,128)(2,1)S(1)}, u32[]{:S(2)}, u32[]{:S(2)}) collective-permute-start(bf16[1024,256]{1,0:T(8,128)(2,1)S(1)} %pad_maximum_fusion.1.refs_5_.refs_4_), channel_id=1, source_target_pairs={{0,1},{1,0},{2,3},{3,2},{4,5},{5,4},{6,7},{7,6},{8,9},{9,8},{10,11... | collective-permute-start | bytes 1572872 | tf_op jit(solution)/shard_map/stream_w_t/ppermute | solution.py:740
  52.2 20.1 %collective-permute-start.10 = (bf16[256,256]{1,0:T(8,128)(2,1)S(1)}, bf16[256,256]{1,0:T(8,128)(2,1)S(1)}, u32[]{:S(2)}, u32[]{:S(2)}) collective-permute-start(bf16[256,256]{1,0:T(8,128)(2,1)S(1)} %copy-done.59), channel_id=1, source_target_pairs={{0,16},{8,24},{16,0},{24,8},{1,17},{9,25},{17,1},{25,9},{2,18},{10... | collective-permute-start | bytes 393224 | tf_op jit(solution)/shard_map/gate_w_z/ppermute | solution.py:755
  53.3 19.0 %collective-permute-start.9 = (bf16[256,256]{1,0:T(8,128)(2,1)S(1)}, bf16[256,256]{1,0:T(8,128)(2,1)S(1)}, u32[]{:S(2)}, u32[]{:S(2)}) collective-permute-start(bf16[256,256]{1,0:T(8,128)(2,1)S(1)} %copy-done.58), channel_id=1, source_target_pairs={{0,8},{8,16},{16,24},{24,0},{1,9},{9,17},{17,25},{25,1},{2,10},{10... | collective-permute-start | bytes 393224 | tf_op jit(solution)/shard_map/gate_w_z/ppermute | solution.py:755
  72.6 20.4 %collective-permute-start.12 = (bf16[512,256]{1,0:T(8,128)(2,1)S(1)}, bf16[512,256]{1,0:T(8,128)(2,1)S(1)}, u32[]{:S(2)}, u32[]{:S(2)}) collective-permute-start(bf16[512,256]{1,0:T(8,128)(2,1)S(1)} %slice.70), channel_id=1, source_target_pairs={{0,1},{1,0},{2,3},{3,2},{4,5},{5,4},{6,7},{7,6},{8,9},{9,8},{10,11... | collective-permute-start | bytes 786440 | tf_op jit(solution)/shard_map/stream_w_far_t/ppermute | solution.py:740
  73.1 20.6 %collective-permute-start.13 = (bf16[512,256]{1,0:T(8,128)(2,1)S(1)}, bf16[512,256]{1,0:T(8,128)(2,1)S(1)}, u32[]{:S(2)}, u32[]{:S(2)}) collective-permute-start(bf16[512,256]{1,0:T(8,128)(2,1)S(1)} %slice.71), channel_id=1, source_target_pairs={{0,4},{4,0},{1,5},{5,1},{2,6},{6,2},{3,7},{7,3},{8,12},{12,8},{9,1... | collective-permute-start | bytes 786440 | tf_op jit(solution)/shard_map/stream_w_far_x/ppermute | solution.py:740
  73.5 18.5 %collective-permute-start.15 = (bf16[256,256]{1,0:T(8,128)(2,1)}, bf16[256,256]{1,0:T(8,128)(2,1)S(1)}, u32[]{:S(2)}, u32[]{:S(2)}) collective-permute-start(bf16[256,256]{1,0:T(8,128)(2,1)} %get-tuple-element.248), channel_id=1, source_target_pairs={{0,16},{8,24},{16,0},{24,8},{1,17},{9,25},{17,1},{25,9},{2,18},{10... | collective-permute-start | bytes 393224 | tf_op jit(solution)/shard_map/outer_w_z/ppermute | solution.py:755
  95.6 112.9 %reduce-scatter.3.cloned.1.call-start = ((), (), s32[]{:S(2)}) async-start(), calls=%async_computation.6 | async-start | bytes 1310720 | tf_op jit(solution)/shard_map/reduce_scatter | solution.py:985
  98.3 20.4 %collective-permute-start.22 = (bf16[1024,256]{1,0:T(8,128)(2,1)S(1)}, bf16[1024,256]{1,0:T(8,128)(2,1)}, u32[]{:S(2)}, u32[]{:S(2)}) collective-permute-start(bf16[1024,256]{1,0:T(8,128)(2,1)S(1)} %pad_maximum_fusion.2.refs_4_.refs_9_), channel_id=1, source_target_pairs={{0,1},{1,0},{2,3},{3,2},{4,5},{5,4},{6,7},{7,6},{8,9},{9,8},{10,11... | collective-permute-start | bytes 1572872 | tf_op jit(solution)/shard_map/gate_w_t/ppermute | solution.py:740
  98.5 20.2 %collective-permute-start.23 = (bf16[1024,256]{1,0:T(8,128)(2,1)S(1)}, bf16[1024,256]{1,0:T(8,128)(2,1)S(1)}, u32[]{:S(2)}, u32[]{:S(2)}) collective-permute-start(bf16[1024,256]{1,0:T(8,128)(2,1)S(1)} %pad_maximum_fusion.3.refs_8_.refs_3_), channel_id=1, source_target_pairs={{0,4},{4,0},{1,5},{5,1},{2,6},{6,2},{3,7},{7,3},{8,12},{12,8},{9,1... | collective-permute-start | bytes 1572872 | tf_op jit(solution)/shard_map/outer_w_x/ppermute | solution.py:740
  110.5 18.8 %collective-permute-start.25 = (bf16[1024,256]{1,0:T(8,128)(2,1)S(1)}, bf16[1024,256]{1,0:T(8,128)(2,1)S(1)}, u32[]{:S(2)}, u32[]{:S(2)}) collective-permute-start(bf16[1024,256]{1,0:T(8,128)(2,1)S(1)} %collective-permute-done.18.refs_5_.refs_10_), channel_id=1, source_target_pairs={{0,1},{1,0},{2,3},{3,2},{4,5},{5,4},{6,7},{7,6},{8,9},{9,8},{10,11... | collective-permute-start | bytes 1572872 | tf_op jit(solution)/shard_map/gate_w_far_t/ppermute | solution.py:740
  111.4 17.9 %collective-permute-start.26 = (bf16[1024,256]{1,0:T(8,128)(2,1)S(1)}, bf16[1024,256]{1,0:T(8,128)(2,1)S(1)}, u32[]{:S(2)}, u32[]{:S(2)}) collective-permute-start(bf16[1024,256]{1,0:T(8,128)(2,1)S(1)} %collective-permute-done.19.refs_10_.refs_5_), channel_id=1, source_target_pairs={{0,4},{4,0},{1,5},{5,1},{2,6},{6,2},{3,7},{7,3},{8,12},{12,8},{9,1... | collective-permute-start | bytes 1572872 | tf_op jit(solution)/shard_map/outer_w_far_x/ppermute | solution.py:740
  181.6 59.2 %reduce-scatter.5.cloned.1.call-start = ((), (), s32[]{:S(2)}) async-start(), calls=%async_computation.7 | async-start | bytes 1310720 | tf_op jit(solution)/shard_map/reduce_scatter | solution.py:1006
  181.9 22.4 %collective-permute-start.32 = (bf16[2,8,256,128]{3,2,1,0:T(8,128)(2,1)}, bf16[2,8,256,128]{3,2,1,0:T(8,128)(2,1)S(1)}, u32[]{:S(2)}, u32[]{:S(2)}) collective-permute-start(bf16[2,8,256,128]{3,2,1,0:T(8,128)(2,1)} %get-tuple-element.316), channel_id=1, source_target_pairs={{0,4},{4,0},{1,5},{5,1},{2,6},{6,2},{3,7},{7,3},{8,12},{12,8},{9,1... | collective-permute-start | bytes 3145736 | tf_op jit(solution)/shard_map/late_g_x/ppermute | solution.py:740
  183.7 22.0 %collective-permute-start.33 = (bf16[2,8,256,128]{3,2,1,0:T(8,128)(2,1)}, bf16[2,8,256,128]{3,2,1,0:T(8,128)(2,1)S(1)}, u32[]{:S(2)}, u32[]{:S(2)}) collective-permute-start(bf16[2,8,256,128]{3,2,1,0:T(8,128)(2,1)} %get-tuple-element.317), channel_id=1, source_target_pairs={{0,1},{1,0},{2,3},{3,2},{4,5},{5,4},{6,7},{7,6},{8,9},{9,8},{10,11... | collective-permute-start | bytes 3145736 | tf_op jit(solution)/shard_map/late_g_t/ppermute | solution.py:740
  214.1 18.3 %collective-permute-start.35 = (bf16[8,256,128]{2,1,0:T(8,128)(2,1)S(1)}, bf16[8,256,128]{2,1,0:T(8,128)(2,1)S(1)}, u32[]{:S(2)}, u32[]{:S(2)}) collective-permute-start(bf16[8,256,128]{2,1,0:T(8,128)(2,1)S(1)} %fusion.3), channel_id=1, source_target_pairs={{0,1},{1,0},{2,3},{3,2},{4,5},{5,4},{6,7},{7,6},{8,9},{9,8},{10,11... | collective-permute-start | bytes 1572872 | tf_op jit(solution)/shard_map/gate_g_sum_t/ppermute | solution.py:740
  234.7 50.0 %all-to-all-start = ((bf16[8,512,128]{2,1,0:T(8,128)(2,1)}), bf16[8,512,128]{2,1,0:T(8,128)(2,1)S(1)}, u32[]{:S(2)}, u32[]{:S(2)}) async-start(bf16[8,512,128]{2,1,0:T(8,128)(2,1)} %pad_maximum_fusion), calls=%async_computation.1 | async-start | bytes 2097152 | tf_op jit(solution)/shard_map/all_to_all | solution.py:768
  238.2 20.8 %collective-permute-start.38 = (bf16[2,8,128,128]{3,2,1,0:T(8,128)(2,1)}, bf16[2,8,128,128]{3,2,1,0:T(8,128)(2,1)S(1)}, u32[]{:S(2)}, u32[]{:S(2)}) collective-permute-start(bf16[2,8,128,128]{3,2,1,0:T(8,128)(2,1)} %get-tuple-element.349), channel_id=1, source_target_pairs={{0,4},{4,0},{1,5},{5,1},{2,6},{6,2},{3,7},{7,3},{8,12},{12,8},{9,1... | collective-permute-start | bytes 1572872 | tf_op jit(solution)/shard_map/stream_g_x/ppermute | solution.py:740
  239.8 19.2 %collective-permute-start.39 = (bf16[2,8,128,128]{3,2,1,0:T(8,128)(2,1)}, bf16[2,8,128,128]{3,2,1,0:T(8,128)(2,1)S(1)}, u32[]{:S(2)}, u32[]{:S(2)}) collective-permute-start(bf16[2,8,128,128]{3,2,1,0:T(8,128)(2,1)} %get-tuple-element.350), channel_id=1, source_target_pairs={{0,1},{1,0},{2,3},{3,2},{4,5},{5,4},{6,7},{7,6},{8,9},{9,8},{10,11... | collective-permute-start | bytes 1572872 | tf_op jit(solution)/shard_map/stream_g_t/ppermute | solution.py:740
  284.7 19.9 %all-to-all-start.1 = ((bf16[8,256,128]{2,1,0:T(8,128)(2,1)}), bf16[8,256,128]{2,1,0:T(8,128)(2,1)S(1)}, u32[]{:S(2)}, u32[]{:S(2)}) async-start(bf16[8,256,128]{2,1,0:T(8,128)(2,1)} %pad_maximum_fusion.4), calls=%async_computation.3 | async-start | bytes 1048576 | tf_op jit(solution)/shard_map/all_to_all | solution.py:768
  (100 other events, 1104.5 us)
Sparse Core Ops, SparseCore 0:
  46.4 41.6 all-gather.2
  95.7 29.3 all-gather.4
  181.8 26.6 reduce-scatter.2
  214.0 25.7 reduce-scatter.4

commit v5 on v4

--- a/solution.py
+++ b/solution.py
@@ -25,7 +25,7 @@
 SIDE = 2
 GROUP = 8
 CHUNK = 64
-UNROLL = 2
+UNROLL = 4
 LOAD, STORE = 0, 1
 F32 = jnp.float32
 BF16 = jnp.bfloat16
@@ -488,28 +488,30 @@
     )
 
 
-def small_kernel(
-    sizes, z_ref, k_ref, *refs,
-):
-    count, states, taps = sizes
-    blocks = refs[:-7]
-    select, step_w, decay, filters, filter_b, step_b, skip = refs[-7:]
-    part = blocks[0].shape[1]
-    zs = len(blocks) // 2
+def small_kernel(sizes, z_ref, x_ref, k_ref, mine, other, *outs):
+    count, states, taps, zs = sizes
+    select, step_w, decay, filters, filter_b, step_b, skip = outs
+    part = mine.shape[1]
     rank = step_w.shape[0]
-    for i, block in enumerate(blocks):
-        core = k_ref[0] if i % 2 == 0 else 1 - k_ref[0]
-        place = (z_block(z_ref, i // 2, zs) * 2 + core) * part
-        at = pl.ds(pl.multiple_of(place, part), part)
-        first = block[: states + 8, :].astype(F32)
-        step_b[:, at] = first[0:1]
-        skip[:, at] = first[1:2]
-        decay[:, at] = first[8:]
-        step_w[:, at] = block[states + 8 : states + 8 + rank, :].astype(F32)
-        rest = block[states + 8 + rank :, :].astype(F32)
-        filters[:, at] = rest[count : count + taps]
-        filter_b[:, at] = rest[count + taps : count + taps + 1]
-        select[:, at] = rest[:count]
+    half = mine.shape[0] // (2 * zs)
+    first_x = x_ref[0] == 0
+    for source, core in ((mine, k_ref[0]), (other, 1 - k_ref[0])):
+        for shift in range(zs):
+            near = source[shift * half : (shift + 1) * half, :].astype(F32)
+            far = source[(zs + shift) * half : (zs + shift + 1) * half, :].astype(F32)
+            block = jnp.concatenate(
+                [jnp.where(first_x, near, far), jnp.where(first_x, far, near)], 0
+            )
+            place = (z_block(z_ref, shift, zs) * 2 + core) * part
+            at = pl.ds(pl.multiple_of(place, part), part)
+            step_b[:, at] = block[0:1]
+            skip[:, at] = block[1:2]
+            decay[:, at] = block[8 : states + 8]
+            step_w[:, at] = block[states + 8 : states + 8 + rank]
+            rest = block[states + 8 + rank :]
+            filters[:, at] = rest[count : count + taps]
+            filter_b[:, at] = rest[count + taps : count + taps + 1]
+            select[:, at] = rest[:count]
 
 
 def scan_kernel(
@@ -920,18 +922,17 @@
     group_tokens = gathered(tok_keep, tok_got)
     params = jnp.concatenate([floats, floats_t], axis=1)
     lows = jnp.concatenate([lows, lows_t], axis=1)
-    stream_x, stream_t, gate_own, params, step_w, select_w, arrived, returned, *packed = step(
+    stream_x, stream_t, gate_own, params, step_w, select_w, arrived, returned, cot_got, *packed = step(
         swap(stream_own, "x", "stream_w"), swap(stream_own, "t", "stream_w"),
         jnp.concatenate(from_z(packed[:zs], "gate_w"), 0), params, lows[:rank_width],
-        lows[rank_width:], arrived, returned, *packed[zs:],
-    )
-    stream_low, stream_high, outer_own, cot_got, gate_own, group_tokens = step(
+        lows[rank_width:], arrived, returned, swap(cot_send, "x", "cot"), *packed[zs:],
+    )
+    group_cot = gathered(cot_keep, cot_got)
+    stream_low, stream_high, outer_own, gate_own, group_tokens = step(
         swap(stream_x[:half], "t", "stream_w_far"), swap(stream_t[half:], "x", "stream_w_far"),
-        jnp.concatenate(from_z(packed, "outer_w"), 0), swap(cot_send, "x", "cot"),
-        gate_own, group_tokens,
+        jnp.concatenate(from_z(packed, "outer_w"), 0), gate_own, group_tokens,
     )
     ws = (stream_own, stream_x, stream_t, stream_low, stream_high)
-    group_cot = gathered(cot_keep, cot_got)
     normed, stream, act, sel_mine, sel_other, position, gain_row = whole(
         partial(front_kernel, (taps, sequence_lengths.shape[1])), "front", [ki, ti, zi],
         (group_tokens, arrived, *ws, params, select_w),
@@ -1017,13 +1018,16 @@
     late_home = to_owners(late_sum)
     own_low, own_high, by_x_high, by_t_low, x_way, t_way = stream_g
     small = plus(small[:, :part], small_got)
+    small_half = small.shape[0] // 2
+    small_kept = lax.dynamic_slice_in_dim(small, xi * small_half, small_half, 0)
+    small_sent = lax.dynamic_slice_in_dim(small, (1 - xi) * small_half, small_half, 0)
 
     def near_rows(rows):
         return jnp.concatenate([rows[:share], swap(rows[share:], "x", "rows")], 0)
 
     x_way, t_way, small_got, small, out_near, in_near = step(
-        swap(x_way, "x", "stream_g"), swap(t_way, "t", "stream_g"), swap(small, "x", "small"),
-        small, near_rows(out_back), near_rows(in_back),
+        swap(x_way, "x", "stream_g"), swap(t_way, "t", "stream_g"), swap(small_sent, "x", "small"),
+        small_kept, near_rows(out_back), near_rows(in_back),
     )
     small = plus(small, small_got)
     if rings > 1:
@@ -1038,7 +1042,8 @@
         [plus(own_low, x_way[1], low_second), plus(own_high, t_way[1], high_second)], axis=1
     )
     stream_home = to_owners(stream_sum)
-    small_blocks = [v for block in gathered_small for v in (block, swap(block, "k", "small"))]
+    small_near = jnp.concatenate(gathered_small, 0)
+    small_near = jnp.concatenate([small_near, swap(small_near, "x", "small_all")], 0)
 
     back_place = send_place[:, None]
     if rings > 1:
@@ -1072,7 +1077,8 @@
         )[0]
     one_row = shape((1, half_channels), F32)
     select_grad, step_w_grad, decay_grad, filter_grad, filter_b_grad, step_b_grad, skip_grad = whole(
-        partial(small_kernel, (count, states, taps)), "small", [zi, ki], small_blocks,
+        partial(small_kernel, (count, states, taps, zs)), "small", [zi, xi, ki],
+        (small_near, swap(small_near, "k", "small")),
         [
             shape((count, half_channels), F32), shape((rank_width, half_channels), F32),
             shape((states, half_channels), F32), shape((taps, half_channels), F32),

time: 320 us -> 315 us (0.984)
  starting transfers between devices: 76 us -> 71.9 us
    ppermute x12, waiting for transfers between devices: 37.2 us -> 42.4 us  [from_z(): lax.ppermute(blocks[shift], 'z', [(i, (i + shift) % size) for i in range(...]
    ppermute x40 -> x38, starting transfers between devices: 35.7 us -> 32.8 us  [swap(): return lax.ppermute(value, axis, SWAP)]
    ppermute x40 -> x38, waiting for transfers between devices: 49.6 us -> 52.1 us  [swap(): return lax.ppermute(value, axis, SWAP)]
    unnamed x128 -> x116, local copies, waits for them, and re-layouts: 13 us -> 11.2 us
  transfers between devices with their start and end apart: 62 -> 60, of which waited for: 23 -> 22; matrix products, arithmetic and copies ran while one was open for 7% -> 8% of each run, Pallas kernels for 16% -> 17%
where the time goes in v5:
time: 315 us; the launch traced here: 314 us
  waiting for transfers between devices  109 us (35%)
  Pallas kernels  78.3 us (25%)
  starting transfers between devices  71.9 us (23%)
  other arithmetic  20.8 us (7%)
  local copies, waits for them, and re-layouts  19.4 us (6%)
  between operations  14.9 us (5%)
    pallas_call x13, Pallas kernels, whole(): pl.pallas_call(copied, in_specs=[pl.BlockSpec(memory_space=pltpu.SMEM)] *...  78.3 us
    ppermute x38, waiting for transfers between devices, swap(): return lax.ppermute(value, axis, SWAP)  52.1 us
    ppermute x12, waiting for transfers between devices, from_z(): lax.ppermute(blocks[shift], 'z', [(i, (i + shift) % size) for i in range(...  42.4 us
    ppermute x38, starting transfers between devices, swap(): return lax.ppermute(value, axis, SWAP)  32.8 us
    ppermute x12, starting transfers between devices, from_z(): lax.ppermute(blocks[shift], 'z', [(i, (i + shift) % size) for i in range(...  24.6 us
    ppermute x4, waiting for transfers between devices, exchange_z(): return lax.ppermute(value, 'z', [(i, i ^ distance) for i in range(size)])  11.7 us
    unnamed x116, local copies, waits for them, and re-layouts  11.2 us
    all_to_all x2, starting transfers between devices, to_owners(): return lax.all_to_all(value, ZK, 0, 0, tiled=True)  8.44 us
  transfers between devices with their start and end apart: 60, of which 22 were waited for; matrix products, arithmetic and copies ran while one was open for 8% of the time, Pallas kernels for 17%

profile of v5, /device:TPU:0, one launch (start us, length us, event | category | flops | bytes accessed | tf_op | source)
XLA Modules:
  0.0 313.8 jit_solution(13140019997373587561)
XLA Ops:
  22.6 4.1 %collective-permute-start.3 = (bf16[256,256]{1,0:T(8,128)(2,1)}, bf16[256,256]{1,0:T(8,128)(2,1)S(1)}, u32[]{:S(2)}, u32[]{:S(2)}) collective-permute-start(bf16[256,256]{1,0:T(8,128)(2,1)} %get-tuple-element.216), channel_id=1, source_target_pairs={{0,24},{8,0},{16,8},{24,16},{1,25},{9,1},{17,9},{25,17},{2,26},{10... | collective-permute-start | bytes 393224 | tf_op jit(solution)/shard_map/stream_w_z/ppermute | solution.py:757
  31.3 7.0 %collective-permute-done.2 = bf16[256,256]{1,0:T(8,128)(2,1)S(1)} collective-permute-done((bf16[256,256]{1,0:T(8,128)(2,1)}, bf16[256,256]{1,0:T(8,128)(2,1)S(1)}, u32[]{:S(2)}, u32[]{:S(2)}) %collective-permute-start.2) | collective-permute-done | bytes 131104 | tf_op jit(solution)/shard_map/stream_w_z/ppermute | solution.py:757
  40.9 3.8 %collective-permute-done.6 = bf16[32,2176]{1,0:T(8,128)(2,1)S(1)} collective-permute-done((bf16[32,2176]{1,0:T(8,128)(2,1)}, bf16[32,2176]{1,0:T(8,128)(2,1)S(1)}, u32[]{:S(2)}, u32[]{:S(2)}) %collective-permute-start.6) | collective-permute-done | bytes 139296 | tf_op jit(solution)/shard_map/tokens_x/ppermute | solution.py:742
  57.7 15.9 %collective-permute-done.10 = bf16[256,256]{1,0:T(8,128)(2,1)S(1)} collective-permute-done((bf16[256,256]{1,0:T(8,128)(2,1)S(1)}, bf16[256,256]{1,0:T(8,128)(2,1)S(1)}, u32[]{:S(2)}, u32[]{:S(2)}) %collective-permute-start.10) | collective-permute-done | bytes 131104 | tf_op jit(solution)/shard_map/gate_w_z/ppermute | solution.py:757
  74.9 8.6 %collective-permute-start.16 = (bf16[256,256]{1,0:T(8,128)(2,1)}, bf16[256,256]{1,0:T(8,128)(2,1)S(1)}, u32[]{:S(2)}, u32[]{:S(2)}) collective-permute-start(bf16[256,256]{1,0:T(8,128)(2,1)} %get-tuple-element.249), channel_id=1, source_target_pairs={{0,16},{8,24},{16,0},{24,8},{1,17},{9,25},{17,1},{25,9},{2,18},{10... | collective-permute-start | bytes 393224 | tf_op jit(solution)/shard_map/outer_w_z/ppermute | solution.py:757
  87.2 5.0 %collective-permute-done.16 = bf16[256,256]{1,0:T(8,128)(2,1)S(1)} collective-permute-done((bf16[256,256]{1,0:T(8,128)(2,1)}, bf16[256,256]{1,0:T(8,128)(2,1)S(1)}, u32[]{:S(2)}, u32[]{:S(2)}) %collective-permute-start.16) | collective-permute-done | bytes 131104 | tf_op jit(solution)/shard_map/outer_w_z/ppermute | solution.py:757
  97.1 7.6 %front.1 = (bf16[512,2048]{1,0:T(8,128)(2,1)}, f32[512,512]{1,0:T(8,128)}, f32[512,512]{1,0:T(8,128)}, f32[160,256]{1,0:T(8,128)}, f32[160,256]{1,0:T(8,128)}, /*index=5*/f32[512,128]{1,0:T(8,128)}, f32[8,2048]{1,0:T(8,128)}) custom-call(s32[1]{0:T(128)} %bitcast.refs_1_.refs_0_.refs_2_, s32[1]{0:T(128)} %bitcast.1.refs_1_, ...), custom_call_target="tpu_custom_call" | custom-call | bytes 29520000 | tf_op jit(solution)/shard_map/front/pallas_call | solution.py:88
  111.5 4.5 %collective-permute-done.22.refs_6_.refs_11_ = bf16[1024,256]{1,0:T(8,128)(2,1)} collective-permute-done((bf16[1024,256]{1,0:T(8,128)(2,1)S(1)}, bf16[1024,256]{1,0:T(8,128)(2,1)}, u32[]{:S(2)}, u32[]{:S(2)}) %collective-permute-start.22) | collective-permute-done | bytes 524320 | tf_op jit(solution)/shard_map/gate_w_t/ppermute | solution.py:742
  116.0 3.5 %collective-permute-done.21 = bf16[160,256]{1,0:T(8,128)(2,1)S(1)} collective-permute-done((bf16[160,256]{1,0:T(8,128)(2,1)S(1)}, bf16[160,256]{1,0:T(8,128)(2,1)S(1)}, u32[]{:S(2)}, u32[]{:S(2)}) %collective-permute-start.21) | collective-permute-done | bytes 81952 | tf_op jit(solution)/shard_map/select_z/ppermute | solution.py:748
  120.4 5.4 %collective-permute-done.24 = bf16[160,256]{1,0:T(8,128)(2,1)S(1)} collective-permute-done((bf16[160,256]{1,0:T(8,128)(2,1)S(1)}, bf16[160,256]{1,0:T(8,128)(2,1)S(1)}, u32[]{:S(2)}, u32[]{:S(2)}) %collective-permute-start.24) | collective-permute-done | bytes 81952 | tf_op jit(solution)/shard_map/select_z/ppermute | solution.py:748
  126.8 6.5 %late.1 = (bf16[512,2048]{1,0:T(8,128)(2,1)}, f32[512,512]{1,0:T(8,128)}, f32[512,512]{1,0:T(8,128)}) custom-call(s32[1]{0:T(128)} %bitcast.2.refs_0_.refs_2_.refs_1_, bf16[512,2048]{1,0:T(8,128)(2,1)} %all-gather.5.cloned.1.call-done.refs_1_, s32[1,512]{1,0:T(1,128)} %reshape.381.refs_4_.refs_2_, ...), custom_call_target="tpu_custom_call" | custom-call | bytes 29520000 | tf_op jit(solution)/shard_map/late/pallas_call | solution.py:88
  134.0 23.3 %mixer.1 = (bf16[512,512]{1,0:T(8,128)(2,1)}, bf16[512,512]{1,0:T(8,128)(2,1)}, f32[512,512]{1,0:T(8,128)}, bf16[152,512]{1,0:T(8,128)(2,1)}, f32[160,256]{1,0:T(8,128)}, /*index=5*/f32[160,256]{1,0:T(8,128)}) custom-call(s32[1]{0:T(128)} %bitcast.refs_1_.refs_0_.refs_2_, f32[512,128]{1,0:T(8,128)} %get-tuple-element.260.refs_1_.refs_4_, ...), custom_call_target="tpu_custom_call" | custom-call | bytes 88560000 | tf_op jit(solution)/shard_map/mixer/pallas_call | solution.py:88
  158.2 4.4 %out_rows.1 = (bf16[256,2048]{1,0:T(8,128)(2,1)}, bf16[256,2048]{1,0:T(8,128)(2,1)}) custom-call(s32[1]{0:T(128)} %bitcast.2.refs_0_.refs_2_.refs_1_, s32[512,1]{1,0:T(8,128)} %copy.52.refs_1_, bf16[512,512]{1,0:T(8,128)(2,1)} %get-tuple-element.298.refs_2_.refs_4_, bf16[1024,256]{1,0:T(8,128)(2,1)} %copy-done.2, bf16[1024,256]{1,0:T(8,128)(2,1)} %copy-done.9, ...), custom_call_target="tpu_custom_call" | custom-call | bytes 18450000 | tf_op jit(solution)/shard_map/out_rows/pallas_call | solution.py:88
  163.9 6.8 %late_grad.1 = (bf16[8,256,128]{2,1,0:T(8,128)(2,1)}, bf16[8,256,128]{2,1,0:T(8,128)(2,1)}, bf16[8,256,128]{2,1,0:T(8,128)(2,1)}, bf16[8,256,128]{2,1,0:T(8,128)...) custom-call(s32[1]{0:T(128)} %bitcast.2.refs_0_.refs_2_.refs_1_, ...), custom_call_target="tpu_custom_call" | custom-call | bytes 22140000 | tf_op jit(solution)/shard_map/late_grad/pallas_call | solution.py:88
  182.8 6.5 %back.1 = (bf16[512,512]{1,0:T(8,128)(2,1)}, bf16[168,512]{1,0:T(8,128)(2,1)}, bf16[8,128,128]{2,1,0:T(8,128)(2,1)}, bf16[8,128,128]{2,1,0:T(8,128)(2,1)}, bf16[...) custom-call(s32[1]{0:T(128)} %bitcast.refs_1_.refs_0_.refs_2_, ...), custom_call_target="tpu_custom_call" | custom-call | bytes 25830000 | tf_op jit(solution)/shard_map/back/pallas_call | solution.py:88
  189.4 6.3 %in_rows.1 = (bf16[256,2048]{1,0:T(8,128)(2,1)}, bf16[256,2048]{1,0:T(8,128)(2,1)}) custom-call(s32[1]{0:T(128)} %bitcast.2.refs_0_.refs_2_.refs_1_, s32[512,1]{1,0:T(8,128)} %copy.52.refs_1_, bf16[512,512]{1,0:T(8,128)(2,1)} %get-tuple-element.322.refs_2_, bf16[512,512]{1,0:T(8,128)(2,1)} %get-tuple-element.297.refs_3_, bf16[1024,256]{1,0:T(8,128)(2,1)} %copy-done.3, ...), custom_call_target="tpu_custom_call" | custom-call | bytes 25830000 | tf_op jit(solution)/shard_map/in_rows/pallas_call | solution.py:88
  195.7 8.2 %collective-permute-done.32 = bf16[2,8,256,128]{3,2,1,0:T(8,128)(2,1)S(1)} collective-permute-done((bf16[2,8,256,128]{3,2,1,0:T(8,128)(2,1)}, bf16[2,8,256,128]{3,2,1,0:T(8,128)(2,1)S(1)}, u32[]{:S(2)}, u32[]{:S(2)}) %collective-permute-start.32) | collective-permute-done | bytes 1048608 | tf_op jit(solution)/shard_map/late_g_x/ppermute | solution.py:742
  215.6 13.5 %collective-permute-done.41 = bf16[32,2048]{1,0:T(8,128)(2,1)S(1)} collective-permute-done((bf16[32,2048]{1,0:T(8,128)(2,1)S(1)}, bf16[32,2048]{1,0:T(8,128)(2,1)S(1)}, u32[]{:S(2)}, u32[]{:S(2)}) %collective-permute-start.41) | collective-permute-done | bytes 131104 | tf_op jit(solution)/shard_map/rows_x/ppermute | solution.py:742
  230.6 3.7 %all-to-all-start = ((bf16[8,512,128]{2,1,0:T(8,128)(2,1)}), bf16[8,512,128]{2,1,0:T(8,128)(2,1)S(1)}, u32[]{:S(2)}, u32[]{:S(2)}) async-start(bf16[8,512,128]{2,1,0:T(8,128)(2,1)} %pad_maximum_fusion), calls=%async_computation.1 | async-start | bytes 2097152 | tf_op jit(solution)/shard_map/all_to_all | solution.py:770
  241.0 11.1 %collective-permute-done.43 = bf16[32,2048]{1,0:T(8,128)(2,1)S(1)} collective-permute-done((bf16[32,2048]{1,0:T(8,128)(2,1)S(1)}, bf16[32,2048]{1,0:T(8,128)(2,1)S(1)}, u32[]{:S(2)}, u32[]{:S(2)}) %collective-permute-start.43) | collective-permute-done | bytes 131104 | tf_op jit(solution)/shard_map/rows_x/ppermute | solution.py:742
  260.8 4.6 %collective-permute-done.48 = bf16[160,256]{1,0:T(8,128)(2,1)S(1)} collective-permute-done((bf16[160,256]{1,0:T(8,128)(2,1)S(1)}, bf16[160,256]{1,0:T(8,128)(2,1)S(1)}, u32[]{:S(2)}, u32[]{:S(2)}) %collective-permute-start.48) | collective-permute-done | bytes 81952 | tf_op jit(solution)/shard_map/small_z/ppermute | solution.py:757
  266.2 5.5 %collective-permute-done.49 = bf16[160,256]{1,0:T(8,128)(2,1)S(1)} collective-permute-done((bf16[160,256]{1,0:T(8,128)(2,1)S(1)}, bf16[160,256]{1,0:T(8,128)(2,1)S(1)}, u32[]{:S(2)}, u32[]{:S(2)}) %collective-permute-start.49) | collective-permute-done | bytes 81952 | tf_op jit(solution)/shard_map/small_z/ppermute | solution.py:757
  279.4 4.7 %all-to-all-start.1 = ((bf16[8,256,128]{2,1,0:T(8,128)(2,1)}), bf16[8,256,128]{2,1,0:T(8,128)(2,1)S(1)}, u32[]{:S(2)}, u32[]{:S(2)}) async-start(bf16[8,256,128]{2,1,0:T(8,128)(2,1)} %pad_maximum_fusion.4), calls=%async_computation.3 | async-start | bytes 1048576 | tf_op jit(solution)/shard_map/all_to_all | solution.py:770
  289.8 3.5 %input_grad.1 = f32[128,2048]{1,0:T(8,128)} custom-call(s32[1]{0:T(128)} %bitcast.10.refs_0_.refs_1_, s32[128,1]{1,0:T(8,128)} %copy.54.refs_1_, bf16[64,2048]{1,0:T(8,128)(2,1)} %copy-done.17, bf16[64,2048]{1,0:T(8,128)(2,1)} %copy-done.30, bf16[128,2048]{1,0:T(8,128)(2,1)} %refs_4_.3, bf16[128,2048]{1,0:T(8,128)(2,1)} %refs_5_.1, ...), custom_call_target="tpu_custom_call" | custom-call | bytes 14760000 | tf_op jit(solution)/shard_map/input_grad/pallas_call | solution.py:88
  (300 shorter events, 125.0 us)
Async XLA Ops:
  7.2 85.1 %all-gather.3.cloned.1.call-start = ((), (), s32[]{:S(2)}) async-start(), calls=%async_computation.4 | async-start | bytes 2506752 | tf_op jit(solution)/shard_map/all_gather | solution.py:905
  14.6 24.7 %collective-permute-start.4 = (f32[24,256]{1,0:T(8,128)S(1)}, f32[24,256]{1,0:T(8,128)S(1)}, u32[]{:S(2)}, u32[]{:S(2)}) collective-permute-start(f32[24,256]{1,0:T(8,128)S(1)} %constant_dynamic-slice_fusion.6), channel_id=1, source_target_pairs={{0,1},{1,0},{2,3},{3,2},{4,5},{5,4},{6,7},{7,6},{8,9},{9,8},{10,11... | collective-permute-start | bytes 73736 | tf_op jit(solution)/shard_map/params_t/ppermute | solution.py:742
  18.0 21.2 %collective-permute-start.5 = (bf16[288,256]{1,0:T(8,128)(2,1)S(1)}, bf16[288,256]{1,0:T(8,128)(2,1)S(1)}, u32[]{:S(2)}, u32[]{:S(2)}) collective-permute-start(bf16[288,256]{1,0:T(8,128)(2,1)S(1)} %pad_maximum_fusion.12), channel_id=1, source_target_pairs={{0,1},{1,0},{2,3},{3,2},{4,5},{5,4},{6,7},{7,6},{8,9},{9,8},{10,11... | collective-permute-start | bytes 442376 | tf_op jit(solution)/shard_map/params_low_t/ppermute | solution.py:742
  46.3 79.7 %all-gather.5.cloned.1.call-start = ((), (), s32[]{:S(2)}) async-start(), calls=%async_computation.5 | async-start | bytes 2359296 | tf_op jit(solution)/shard_map/all_gather | solution.py:905
  46.8 26.9 %collective-permute-start.7 = (bf16[1024,256]{1,0:T(8,128)(2,1)S(1)}, bf16[1024,256]{1,0:T(8,128)(2,1)S(1)}, u32[]{:S(2)}, u32[]{:S(2)}) collective-permute-start(bf16[1024,256]{1,0:T(8,128)(2,1)S(1)} %pad_maximum_fusion.1.refs_5_.refs_4_), channel_id=1, source_target_pairs={{0,4},{4,0},{1,5},{5,1},{2,6},{6,2},{3,7},{7,3},{8,12},{12,8},{9,1... | collective-permute-start | bytes 1572872 | tf_op jit(solution)/shard_map/stream_w_x/ppermute | solution.py:742
  48.3 25.4 %collective-permute-start.8 = (bf16[1024,256]{1,0:T(8,128)(2,1)S(1)}, bf16[1024,256]{1,0:T(8,128)(2,1)S(1)}, u32[]{:S(2)}, u32[]{:S(2)}) collective-permute-start(bf16[1024,256]{1,0:T(8,128)(2,1)S(1)} %pad_maximum_fusion.1.refs_5_.refs_4_), channel_id=1, source_target_pairs={{0,1},{1,0},{2,3},{3,2},{4,5},{5,4},{6,7},{7,6},{8,9},{9,8},{10,11... | collective-permute-start | bytes 1572872 | tf_op jit(solution)/shard_map/stream_w_t/ppermute | solution.py:742
  52.2 21.4 %collective-permute-start.10 = (bf16[256,256]{1,0:T(8,128)(2,1)S(1)}, bf16[256,256]{1,0:T(8,128)(2,1)S(1)}, u32[]{:S(2)}, u32[]{:S(2)}) collective-permute-start(bf16[256,256]{1,0:T(8,128)(2,1)S(1)} %copy-done.52), channel_id=1, source_target_pairs={{0,16},{8,24},{16,0},{24,8},{1,17},{9,25},{17,1},{25,9},{2,18},{10... | collective-permute-start | bytes 393224 | tf_op jit(solution)/shard_map/gate_w_z/ppermute | solution.py:757
  53.3 20.3 %collective-permute-start.9 = (bf16[256,256]{1,0:T(8,128)(2,1)S(1)}, bf16[256,256]{1,0:T(8,128)(2,1)S(1)}, u32[]{:S(2)}, u32[]{:S(2)}) collective-permute-start(bf16[256,256]{1,0:T(8,128)(2,1)S(1)} %copy-done.51), channel_id=1, source_target_pairs={{0,8},{8,16},{16,24},{24,0},{1,9},{9,17},{17,25},{25,1},{2,10},{10... | collective-permute-start | bytes 393224 | tf_op jit(solution)/shard_map/gate_w_z/ppermute | solution.py:757
  74.6 130.7 %reduce-scatter.3.cloned.1.call-start = ((), (), s32[]{:S(2)}) async-start(), calls=%async_computation.6 | async-start | bytes 1310720 | tf_op jit(solution)/shard_map/reduce_scatter | solution.py:986
  95.7 20.2 %collective-permute-start.22 = (bf16[1024,256]{1,0:T(8,128)(2,1)S(1)}, bf16[1024,256]{1,0:T(8,128)(2,1)}, u32[]{:S(2)}, u32[]{:S(2)}) collective-permute-start(bf16[1024,256]{1,0:T(8,128)(2,1)S(1)} %pad_maximum_fusion.2.refs_4_.refs_9_), channel_id=1, source_target_pairs={{0,1},{1,0},{2,3},{3,2},{4,5},{5,4},{6,7},{7,6},{8,9},{9,8},{10,11... | collective-permute-start | bytes 1572872 | tf_op jit(solution)/shard_map/gate_w_t/ppermute | solution.py:742
  95.8 20.2 %collective-permute-start.23 = (bf16[1024,256]{1,0:T(8,128)(2,1)S(1)}, bf16[1024,256]{1,0:T(8,128)(2,1)S(1)}, u32[]{:S(2)}, u32[]{:S(2)}) collective-permute-start(bf16[1024,256]{1,0:T(8,128)(2,1)S(1)} %pad_maximum_fusion.3.refs_8_.refs_3_), channel_id=1, source_target_pairs={{0,4},{4,0},{1,5},{5,1},{2,6},{6,2},{3,7},{7,3},{8,12},{12,8},{9,1... | collective-permute-start | bytes 1572872 | tf_op jit(solution)/shard_map/outer_w_x/ppermute | solution.py:742
  108.0 17.9 %collective-permute-start.25 = (bf16[1024,256]{1,0:T(8,128)(2,1)S(1)}, bf16[1024,256]{1,0:T(8,128)(2,1)S(1)}, u32[]{:S(2)}, u32[]{:S(2)}) collective-permute-start(bf16[1024,256]{1,0:T(8,128)(2,1)S(1)} %collective-permute-done.18.refs_5_.refs_10_), channel_id=1, source_target_pairs={{0,1},{1,0},{2,3},{3,2},{4,5},{5,4},{6,7},{7,6},{8,9},{9,8},{10,11... | collective-permute-start | bytes 1572872 | tf_op jit(solution)/shard_map/gate_w_far_t/ppermute | solution.py:742
  108.2 17.7 %collective-permute-start.26 = (bf16[1024,256]{1,0:T(8,128)(2,1)S(1)}, bf16[1024,256]{1,0:T(8,128)(2,1)S(1)}, u32[]{:S(2)}, u32[]{:S(2)}) collective-permute-start(bf16[1024,256]{1,0:T(8,128)(2,1)S(1)} %collective-permute-done.19.refs_10_.refs_5_), channel_id=1, source_target_pairs={{0,4},{4,0},{1,5},{5,1},{2,6},{6,2},{3,7},{7,3},{8,12},{12,8},{9,1... | collective-permute-start | bytes 1572872 | tf_op jit(solution)/shard_map/outer_w_far_x/ppermute | solution.py:742
  178.3 58.6 %reduce-scatter.5.cloned.1.call-start = ((), (), s32[]{:S(2)}) async-start(), calls=%async_computation.7 | async-start | bytes 1310720 | tf_op jit(solution)/shard_map/reduce_scatter | solution.py:1007
  178.6 25.3 %collective-permute-start.32 = (bf16[2,8,256,128]{3,2,1,0:T(8,128)(2,1)}, bf16[2,8,256,128]{3,2,1,0:T(8,128)(2,1)S(1)}, u32[]{:S(2)}, u32[]{:S(2)}) collective-permute-start(bf16[2,8,256,128]{3,2,1,0:T(8,128)(2,1)} %get-tuple-element.316), channel_id=1, source_target_pairs={{0,4},{4,0},{1,5},{5,1},{2,6},{6,2},{3,7},{7,3},{8,12},{12,8},{9,1... | collective-permute-start | bytes 3145736 | tf_op jit(solution)/shard_map/late_g_x/ppermute | solution.py:742
  180.4 25.0 %collective-permute-start.33 = (bf16[2,8,256,128]{3,2,1,0:T(8,128)(2,1)}, bf16[2,8,256,128]{3,2,1,0:T(8,128)(2,1)S(1)}, u32[]{:S(2)}, u32[]{:S(2)}) collective-permute-start(bf16[2,8,256,128]{3,2,1,0:T(8,128)(2,1)} %get-tuple-element.317), channel_id=1, source_target_pairs={{0,1},{1,0},{2,3},{3,2},{4,5},{5,4},{6,7},{7,6},{8,9},{9,8},{10,11... | collective-permute-start | bytes 3145736 | tf_op jit(solution)/shard_map/late_g_t/ppermute | solution.py:742
  211.0 18.1 %collective-permute-start.35 = (bf16[8,256,128]{2,1,0:T(8,128)(2,1)S(1)}, bf16[8,256,128]{2,1,0:T(8,128)(2,1)S(1)}, u32[]{:S(2)}, u32[]{:S(2)}) collective-permute-start(bf16[8,256,128]{2,1,0:T(8,128)(2,1)S(1)} %fusion.3), channel_id=1, source_target_pairs={{0,1},{1,0},{2,3},{3,2},{4,5},{5,4},{6,7},{7,6},{8,9},{9,8},{10,11... | collective-permute-start | bytes 1572872 | tf_op jit(solution)/shard_map/gate_g_sum_t/ppermute | solution.py:742
  230.6 48.7 %all-to-all-start = ((bf16[8,512,128]{2,1,0:T(8,128)(2,1)}), bf16[8,512,128]{2,1,0:T(8,128)(2,1)S(1)}, u32[]{:S(2)}, u32[]{:S(2)}) async-start(bf16[8,512,128]{2,1,0:T(8,128)(2,1)} %pad_maximum_fusion), calls=%async_computation.1 | async-start | bytes 2097152 | tf_op jit(solution)/shard_map/all_to_all | solution.py:770
  234.3 19.0 %collective-permute-start.38 = (bf16[2,8,128,128]{3,2,1,0:T(8,128)(2,1)}, bf16[2,8,128,128]{3,2,1,0:T(8,128)(2,1)S(1)}, u32[]{:S(2)}, u32[]{:S(2)}) collective-permute-start(bf16[2,8,128,128]{3,2,1,0:T(8,128)(2,1)} %get-tuple-element.349), channel_id=1, source_target_pairs={{0,4},{4,0},{1,5},{5,1},{2,6},{6,2},{3,7},{7,3},{8,12},{12,8},{9,1... | collective-permute-start | bytes 1572872 | tf_op jit(solution)/shard_map/stream_g_x/ppermute | solution.py:742
  254.4 21.7 %collective-permute-start.44 = (bf16[8,128,128]{2,1,0:T(8,128)(2,1)S(1)}, bf16[8,128,128]{2,1,0:T(8,128)(2,1)S(1)}, u32[]{:S(2)}, u32[]{:S(2)}) collective-permute-start(bf16[8,128,128]{2,1,0:T(8,128)(2,1)S(1)} %fusion.9), channel_id=1, source_target_pairs={{0,1},{1,0},{2,3},{3,2},{4,5},{5,4},{6,7},{7,6},{8,9},{9,8},{10,11... | collective-permute-start | bytes 786440 | tf_op jit(solution)/shard_map/stream_g_sum_t/ppermute | solution.py:742
  255.5 20.6 %collective-permute-start.45 = (bf16[8,128,128]{2,1,0:T(8,128)(2,1)S(1)}, bf16[8,128,128]{2,1,0:T(8,128)(2,1)S(1)}, u32[]{:S(2)}, u32[]{:S(2)}) collective-permute-start(bf16[8,128,128]{2,1,0:T(8,128)(2,1)S(1)} %fusion.8), channel_id=1, source_target_pairs={{0,4},{4,0},{1,5},{5,1},{2,6},{6,2},{3,7},{7,3},{8,12},{12,8},{9,1... | collective-permute-start | bytes 786440 | tf_op jit(solution)/shard_map/stream_g_sum_x/ppermute | solution.py:742
  257.1 19.0 %collective-permute-start.46 = (bf16[64,2048]{1,0:T(8,128)(2,1)S(1)}, bf16[64,2048]{1,0:T(8,128)(2,1)S(1)}, u32[]{:S(2)}, u32[]{:S(2)}) collective-permute-start(bf16[64,2048]{1,0:T(8,128)(2,1)S(1)} %pad_maximum_fusion.8.refs_2_), channel_id=1, source_target_pairs={{0,1},{1,0},{2,3},{3,2},{4,5},{5,4},{6,7},{7,6},{8,9},{9,8},{10,11... | collective-permute-start | bytes 786440 | tf_op jit(solution)/shard_map/rows_t/ppermute | solution.py:742
  258.1 18.7 %collective-permute-start.47 = (bf16[64,2048]{1,0:T(8,128)(2,1)S(1)}, bf16[64,2048]{1,0:T(8,128)(2,1)S(1)}, u32[]{:S(2)}, u32[]{:S(2)}) collective-permute-start(bf16[64,2048]{1,0:T(8,128)(2,1)S(1)} %pad_maximum_fusion.9.refs_2_), channel_id=1, source_target_pairs={{0,1},{1,0},{2,3},{3,2},{4,5},{5,4},{6,7},{7,6},{8,9},{9,8},{10,11... | collective-permute-start | bytes 786440 | tf_op jit(solution)/shard_map/rows_t/ppermute | solution.py:742
  279.4 20.1 %all-to-all-start.1 = ((bf16[8,256,128]{2,1,0:T(8,128)(2,1)}), bf16[8,256,128]{2,1,0:T(8,128)(2,1)S(1)}, u32[]{:S(2)}, u32[]{:S(2)}) async-start(bf16[8,256,128]{2,1,0:T(8,128)(2,1)} %pad_maximum_fusion.4), calls=%async_computation.3 | async-start | bytes 1048576 | tf_op jit(solution)/shard_map/all_to_all | solution.py:770
  (90 other events, 1061.9 us)
Sparse Core Ops, SparseCore 0:
  46.4 41.7 all-gather.2
  90.4 30.6 all-gather.4
  178.4 26.6 reduce-scatter.2
  211.0 25.5 reduce-scatter.4

commit v6 on v5

--- a/solution.py
+++ b/solution.py
@@ -397,8 +397,8 @@
 
 def out_kernel(z_ref, place_ref, gated_ref, *refs):
     yield LOAD, (0, 1)
-    order = column_matches(place_ref[...], gated_ref.shape[0])
-    rows = dot(order, gated_ref[...]).astype(BF16)
+    order = row_matches(place_ref[...], gated_ref.shape[0])
+    rows = dot(order, gated_ref[...], TN).astype(BF16)
     yield LOAD, (2, 3, 4, 5)
     row_sum(z_ref, [(rows, refs[:4])], refs[4:])
 
@@ -479,9 +479,9 @@
     stream_pieces, gate_pieces, outs, stage = refs[:5], refs[5:9], refs[9:11], refs[11]
     channels = low_ref.shape[1]
     yield LOAD, (0, 1, 2)
-    order = column_matches(place_ref[...], low_ref.shape[0])
-    stage[:, :channels] = dot(order, low_ref[...]).astype(BF16)
-    stage[:, channels:] = dot(order, gate_grad_ref[...]).astype(BF16)
+    order = row_matches(place_ref[...], low_ref.shape[0])
+    stage[:, :channels] = dot(order, low_ref[...], TN).astype(BF16)
+    stage[:, channels:] = dot(order, gate_grad_ref[...], TN).astype(BF16)
     yield LOAD, range(3, 12)
     row_sum(
         z_ref, [(stage[:, :channels], stream_pieces), (stage[:, channels:], gate_pieces)], outs
@@ -869,7 +869,7 @@
     arrival = jnp.where(xi == 0, arrival, arrival[:, ::-1]).transpose(0, 2, 1, 3)
     arrived = arrival.reshape(1, group_rows)
     returned = jnp.where(ki == 0, arrival, arrival[:, ::-1]).transpose(1, 0, 2, 3)
-    returned = returned.reshape(group_rows, 1)
+    returned = returned.reshape(1, group_rows)
 
     blocks = [to_blocks(tok), to_blocks(cot)]
     lengths = sequence_lengths.reshape(1, -1).astype(BF16)
@@ -1032,18 +1032,31 @@
     small = plus(small, small_got)
     if rings > 1:
         small = lax.psum(small.astype(F32), "r").astype(BF16)
-    low_second, high_second, out_far, in_far, *gathered_small = step(
+    low_second, high_second, out_near, in_near, *gathered_small = step(
         swap(plus(by_t_low, x_way[0]), "t", "stream_g_sum"),
         swap(plus(by_x_high, t_way[0]), "x", "stream_g_sum"),
-        swap(out_near, "t", "rows"), swap(in_near, "t", "rows"),
-        *from_z([small] * zs, "small"),
+        out_near, in_near, *from_z([small] * zs, "small"),
     )
     stream_sum = jnp.concatenate(
         [plus(own_low, x_way[1], low_second), plus(own_high, t_way[1], high_second)], axis=1
     )
+    stream_sum, out_far, in_near = step(stream_sum, swap(out_near, "t", "rows"), in_near)
     stream_home = to_owners(stream_sum)
+    in_far = swap(in_near, "t", "rows")
     small_near = jnp.concatenate(gathered_small, 0)
     small_near = jnp.concatenate([small_near, swap(small_near, "x", "small_all")], 0)
+
+    one_row = shape((1, half_channels), F32)
+    select_grad, step_w_grad, decay_grad, filter_grad, filter_b_grad, step_b_grad, skip_grad = whole(
+        partial(small_kernel, (count, states, taps, zs)), "small", [zi, xi, ki],
+        (small_near, swap(small_near, "k", "small")),
+        [
+            shape((count, half_channels), F32), shape((rank_width, half_channels), F32),
+            shape((states, half_channels), F32), shape((taps, half_channels), F32),
+            one_row, one_row, one_row,
+        ],
+    )
+    in_far, select_grad = step(in_far, select_grad)
 
     back_place = send_place[:, None]
     if rings > 1:
@@ -1075,16 +1088,6 @@
             (back_place, in_near, in_far, tokens, cotangent, gain_row),
             [shape(tokens.shape, F32)],
         )[0]
-    one_row = shape((1, half_channels), F32)
-    select_grad, step_w_grad, decay_grad, filter_grad, filter_b_grad, step_b_grad, skip_grad = whole(
-        partial(small_kernel, (count, states, taps, zs)), "small", [zi, xi, ki],
-        (small_near, swap(small_near, "k", "small")),
-        [
-            shape((count, half_channels), F32), shape((rank_width, half_channels), F32),
-            shape((states, half_channels), F32), shape((taps, half_channels), F32),
-            one_row, one_row, one_row,
-        ],
-    )
     late_home, stream_home, output, input_grad, select_grad = step(
         late_home, stream_home, output, input_grad, select_grad
     )

time: 315 us -> 308 us (0.978)
  waiting for transfers between devices: 109 us -> 99.4 us
    ppermute x12, waiting for transfers between devices: 42.4 us -> 33.5 us  [from_z(): lax.ppermute(blocks[shift], 'z', [(i, (i + shift) % size) for i in range(...]
    unnamed x116 -> x122, local copies, waits for them, and re-layouts: 11.2 us -> 11.1 us
  transfers between devices with their start and end apart: 60 -> 60, of which waited for: 22 -> 25; matrix products, arithmetic and copies ran while one was open for 8% -> 8% of each run, Pallas kernels for 17% -> 17%
where the time goes in v6:
time: 308 us; the launch traced here: 307 us
  waiting for transfers between devices  99.4 us (32%)
  Pallas kernels  78.1 us (25%)
  starting transfers between devices  74.3 us (24%)
  other arithmetic  21.9 us (7%)
  local copies, waits for them, and re-layouts  18.9 us (6%)
  between operations  14.9 us (5%)
    pallas_call x13, Pallas kernels, whole(): pl.pallas_call(copied, in_specs=[pl.BlockSpec(memory_space=pltpu.SMEM)] *...  78.1 us
    ppermute x38, waiting for transfers between devices, swap(): return lax.ppermute(value, axis, SWAP)  52.4 us
    ppermute x38, starting transfers between devices, swap(): return lax.ppermute(value, axis, SWAP)  33.9 us
    ppermute x12, waiting for transfers between devices, from_z(): lax.ppermute(blocks[shift], 'z', [(i, (i + shift) % size) for i in range(...  33.5 us
    ppermute x12, starting transfers between devices, from_z(): lax.ppermute(blocks[shift], 'z', [(i, (i + shift) % size) for i in range(...  26.1 us
    ppermute x4, waiting for transfers between devices, exchange_z(): return lax.ppermute(value, 'z', [(i, i ^ distance) for i in range(size)])  12.1 us
    unnamed x122, local copies, waits for them, and re-layouts  11.1 us
    convert_element_type x12, other arithmetic, plus(): return total.astype(BF16)  8.13 us
  transfers between devices with their start and end apart: 60, of which 25 were waited for; matrix products, arithmetic and copies ran while one was open for 8% of the time, Pallas kernels for 17%

profile of v6, /device:TPU:0, one launch (start us, length us, event | category | flops | bytes accessed | tf_op | source)
XLA Modules:
  0.0 307.5 jit_solution(12860960590924439220)
XLA Ops:
  22.6 4.1 %collective-permute-start.3 = (bf16[256,256]{1,0:T(8,128)(2,1)}, bf16[256,256]{1,0:T(8,128)(2,1)S(1)}, u32[]{:S(2)}, u32[]{:S(2)}) collective-permute-start(bf16[256,256]{1,0:T(8,128)(2,1)} %get-tuple-element.221), channel_id=1, source_target_pairs={{0,24},{8,0},{16,8},{24,16},{1,25},{9,1},{17,9},{25,17},{2,26},{10... | collective-permute-start | bytes 393224 | tf_op jit(solution)/shard_map/stream_w_z/ppermute | solution.py:757
  31.3 7.0 %collective-permute-done.2 = bf16[256,256]{1,0:T(8,128)(2,1)S(1)} collective-permute-done((bf16[256,256]{1,0:T(8,128)(2,1)}, bf16[256,256]{1,0:T(8,128)(2,1)S(1)}, u32[]{:S(2)}, u32[]{:S(2)}) %collective-permute-start.2) | collective-permute-done | bytes 131104 | tf_op jit(solution)/shard_map/stream_w_z/ppermute | solution.py:757
  40.8 3.8 %collective-permute-done.6 = bf16[32,2176]{1,0:T(8,128)(2,1)S(1)} collective-permute-done((bf16[32,2176]{1,0:T(8,128)(2,1)}, bf16[32,2176]{1,0:T(8,128)(2,1)S(1)}, u32[]{:S(2)}, u32[]{:S(2)}) %collective-permute-start.6) | collective-permute-done | bytes 139296 | tf_op jit(solution)/shard_map/tokens_x/ppermute | solution.py:742
  58.4 16.0 %collective-permute-done.10 = bf16[256,256]{1,0:T(8,128)(2,1)S(1)} collective-permute-done((bf16[256,256]{1,0:T(8,128)(2,1)S(1)}, bf16[256,256]{1,0:T(8,128)(2,1)S(1)}, u32[]{:S(2)}, u32[]{:S(2)}) %collective-permute-start.10) | collective-permute-done | bytes 131104 | tf_op jit(solution)/shard_map/gate_w_z/ppermute | solution.py:757
  75.7 8.8 %collective-permute-start.16 = (bf16[256,256]{1,0:T(8,128)(2,1)}, bf16[256,256]{1,0:T(8,128)(2,1)S(1)}, u32[]{:S(2)}, u32[]{:S(2)}) collective-permute-start(bf16[256,256]{1,0:T(8,128)(2,1)} %get-tuple-element.254), channel_id=1, source_target_pairs={{0,16},{8,24},{16,0},{24,8},{1,17},{9,25},{17,1},{25,9},{2,18},{10... | collective-permute-start | bytes 393224 | tf_op jit(solution)/shard_map/outer_w_z/ppermute | solution.py:757
  87.6 5.0 %collective-permute-done.16 = bf16[256,256]{1,0:T(8,128)(2,1)S(1)} collective-permute-done((bf16[256,256]{1,0:T(8,128)(2,1)}, bf16[256,256]{1,0:T(8,128)(2,1)S(1)}, u32[]{:S(2)}, u32[]{:S(2)}) %collective-permute-start.16) | collective-permute-done | bytes 131104 | tf_op jit(solution)/shard_map/outer_w_z/ppermute | solution.py:757
  97.5 7.6 %front.1 = (bf16[512,2048]{1,0:T(8,128)(2,1)}, f32[512,512]{1,0:T(8,128)}, f32[512,512]{1,0:T(8,128)}, f32[160,256]{1,0:T(8,128)}, f32[160,256]{1,0:T(8,128)}, /*index=5*/f32[512,128]{1,0:T(8,128)}, f32[8,2048]{1,0:T(8,128)}) custom-call(s32[1]{0:T(128)} %bitcast.refs_1_.refs_0_.refs_2_, s32[1]{0:T(128)} %bitcast.1.refs_1_, ...), custom_call_target="tpu_custom_call" | custom-call | bytes 29520000 | tf_op jit(solution)/shard_map/front/pallas_call | solution.py:88
  112.4 3.5 %collective-permute-done.22.refs_6_.refs_11_ = bf16[1024,256]{1,0:T(8,128)(2,1)S(1)} collective-permute-done((bf16[1024,256]{1,0:T(8,128)(2,1)S(1)}, bf16[1024,256]{1,0:T(8,128)(2,1)S(1)}, u32[]{:S(2)}, u32[]{:S(2)}) %collective-permute-start.22) | collective-permute-done | bytes 524320 | tf_op jit(solution)/shard_map/gate_w_t/ppermute | solution.py:742
  116.0 3.9 %collective-permute-done.21 = bf16[160,256]{1,0:T(8,128)(2,1)S(1)} collective-permute-done((bf16[160,256]{1,0:T(8,128)(2,1)S(1)}, bf16[160,256]{1,0:T(8,128)(2,1)S(1)}, u32[]{:S(2)}, u32[]{:S(2)}) %collective-permute-start.21) | collective-permute-done | bytes 81952 | tf_op jit(solution)/shard_map/select_z/ppermute | solution.py:748
  120.9 5.5 %collective-permute-done.24 = bf16[160,256]{1,0:T(8,128)(2,1)S(1)} collective-permute-done((bf16[160,256]{1,0:T(8,128)(2,1)S(1)}, bf16[160,256]{1,0:T(8,128)(2,1)S(1)}, u32[]{:S(2)}, u32[]{:S(2)}) %collective-permute-start.24) | collective-permute-done | bytes 81952 | tf_op jit(solution)/shard_map/select_z/ppermute | solution.py:748
  127.4 6.5 %late.1 = (bf16[512,2048]{1,0:T(8,128)(2,1)}, f32[512,512]{1,0:T(8,128)}, f32[512,512]{1,0:T(8,128)}) custom-call(s32[1]{0:T(128)} %bitcast.2.refs_0_.refs_2_.refs_1_, bf16[512,2048]{1,0:T(8,128)(2,1)} %all-gather.5.cloned.1.call-done.refs_1_, s32[1,512]{1,0:T(1,128)} %reshape.381.refs_4_.refs_2_, ...), custom_call_target="tpu_custom_call" | custom-call | bytes 29520000 | tf_op jit(solution)/shard_map/late/pallas_call | solution.py:88
  134.5 23.3 %mixer.1 = (bf16[512,512]{1,0:T(8,128)(2,1)}, bf16[512,512]{1,0:T(8,128)(2,1)}, f32[512,512]{1,0:T(8,128)}, bf16[152,512]{1,0:T(8,128)(2,1)}, f32[160,256]{1,0:T(8,128)}, /*index=5*/f32[160,256]{1,0:T(8,128)}) custom-call(s32[1]{0:T(128)} %bitcast.refs_1_.refs_0_.refs_2_, f32[512,128]{1,0:T(8,128)} %get-tuple-element.265.refs_1_.refs_4_, ...), custom_call_target="tpu_custom_call" | custom-call | bytes 88560000 | tf_op jit(solution)/shard_map/mixer/pallas_call | solution.py:88
  158.0 4.3 %out_rows.1 = (bf16[256,2048]{1,0:T(8,128)(2,1)}, bf16[256,2048]{1,0:T(8,128)(2,1)}) custom-call(s32[1]{0:T(128)} %bitcast.2.refs_0_.refs_2_.refs_1_, s32[1,512]{1,0:T(1,128)} %reshape.382.refs_1_, bf16[512,512]{1,0:T(8,128)(2,1)} %get-tuple-element.303.refs_2_.refs_4_, bf16[1024,256]{1,0:T(8,128)(2,1)} %copy-done.4, ...), custom_call_target="tpu_custom_call" | custom-call | bytes 18450000 | tf_op jit(solution)/shard_map/out_rows/pallas_call | solution.py:88
  163.3 6.7 %late_grad.1 = (bf16[8,256,128]{2,1,0:T(8,128)(2,1)}, bf16[8,256,128]{2,1,0:T(8,128)(2,1)}, bf16[8,256,128]{2,1,0:T(8,128)(2,1)}, bf16[8,256,128]{2,1,0:T(8,128)...) custom-call(s32[1]{0:T(128)} %bitcast.2.refs_0_.refs_2_.refs_1_, ...), custom_call_target="tpu_custom_call" | custom-call | bytes 22140000 | tf_op jit(solution)/shard_map/late_grad/pallas_call | solution.py:88
  170.1 3.6 %collective-permute-start.31 = (bf16[160,256]{1,0:T(8,128)(2,1)S(1)}, bf16[160,256]{1,0:T(8,128)(2,1)S(1)}, u32[]{:S(2)}, u32[]{:S(2)}) collective-permute-start(bf16[160,256]{1,0:T(8,128)(2,1)S(1)} %add_convert_fusion.4), channel_id=1, source_target_pairs={{0,16},{8,24},{16,0},{24,8},{1,17},{9,25},{17,1},{25,9},{2,18},{10... | collective-permute-start | bytes 245768 | tf_op jit(solution)/shard_map/select_z/ppermute | solution.py:748
  182.2 6.5 %back.1 = (bf16[512,512]{1,0:T(8,128)(2,1)}, bf16[168,512]{1,0:T(8,128)(2,1)}, bf16[8,128,128]{2,1,0:T(8,128)(2,1)}, bf16[8,128,128]{2,1,0:T(8,128)(2,1)}, bf16[...) custom-call(s32[1]{0:T(128)} %bitcast.refs_1_.refs_0_.refs_2_, ...), custom_call_target="tpu_custom_call" | custom-call | bytes 25830000 | tf_op jit(solution)/shard_map/back/pallas_call | solution.py:88
  188.7 6.3 %in_rows.1 = (bf16[256,2048]{1,0:T(8,128)(2,1)}, bf16[256,2048]{1,0:T(8,128)(2,1)}) custom-call(s32[1]{0:T(128)} %bitcast.2.refs_0_.refs_2_.refs_1_, s32[1,512]{1,0:T(1,128)} %reshape.382.refs_1_, bf16[512,512]{1,0:T(8,128)(2,1)} %get-tuple-element.327.refs_2_, bf16[512,512]{1,0:T(8,128)(2,1)} %get-tuple-element.302.refs_3_, bf16[1024,256]{1,0:T(8,128)(2,1)} %copy-done.2, ...), custom_call_target="tpu_custom_call" | custom-call | bytes 25830000 | tf_op jit(solution)/shard_map/in_rows/pallas_call | solution.py:88
  194.9 8.1 %collective-permute-done.32 = bf16[2,8,256,128]{3,2,1,0:T(8,128)(2,1)S(1)} collective-permute-done((bf16[2,8,256,128]{3,2,1,0:T(8,128)(2,1)}, bf16[2,8,256,128]{3,2,1,0:T(8,128)(2,1)S(1)}, u32[]{:S(2)}, u32[]{:S(2)}) %collective-permute-start.32) | collective-permute-done | bytes 1048608 | tf_op jit(solution)/shard_map/late_g_x/ppermute | solution.py:742
  215.1 13.5 %collective-permute-done.41 = bf16[32,2048]{1,0:T(8,128)(2,1)S(1)} collective-permute-done((bf16[32,2048]{1,0:T(8,128)(2,1)S(1)}, bf16[32,2048]{1,0:T(8,128)(2,1)S(1)}, u32[]{:S(2)}, u32[]{:S(2)}) %collective-permute-start.41) | collective-permute-done | bytes 131104 | tf_op jit(solution)/shard_map/rows_x/ppermute | solution.py:742
  230.8 3.7 %all-to-all-start = ((bf16[8,512,128]{2,1,0:T(8,128)(2,1)}), bf16[8,512,128]{2,1,0:T(8,128)(2,1)S(1)}, u32[]{:S(2)}, u32[]{:S(2)}) async-start(bf16[8,512,128]{2,1,0:T(8,128)(2,1)} %pad_maximum_fusion), calls=%async_computation.1 | async-start | bytes 2097152 | tf_op jit(solution)/shard_map/all_to_all | solution.py:770
  241.3 11.1 %collective-permute-done.43 = bf16[32,2048]{1,0:T(8,128)(2,1)S(1)} collective-permute-done((bf16[32,2048]{1,0:T(8,128)(2,1)S(1)}, bf16[32,2048]{1,0:T(8,128)(2,1)S(1)}, u32[]{:S(2)}, u32[]{:S(2)}) %collective-permute-start.43) | collective-permute-done | bytes 131104 | tf_op jit(solution)/shard_map/rows_x/ppermute | solution.py:742
  274.2 3.8 %all-to-all-start.1 = ((bf16[8,256,128]{2,1,0:T(8,128)(2,1)}), bf16[8,256,128]{2,1,0:T(8,128)(2,1)S(1)}, u32[]{:S(2)}, u32[]{:S(2)}) async-start(bf16[8,256,128]{2,1,0:T(8,128)(2,1)} %pad_maximum_fusion.4), calls=%async_computation.3 | async-start | bytes 1048576 | tf_op jit(solution)/shard_map/all_to_all | solution.py:770
  284.1 3.0 small.1
  288.5 3.5 %input_grad.1 = f32[128,2048]{1,0:T(8,128)} custom-call(s32[1]{0:T(128)} %bitcast.10.refs_0_.refs_1_, s32[128,1]{1,0:T(8,128)} %copy.50.refs_1_, bf16[64,2048]{1,0:T(8,128)(2,1)} %copy-done.17, bf16[64,2048]{1,0:T(8,128)(2,1)} %copy-done.30, bf16[128,2048]{1,0:T(8,128)(2,1)} %refs_4_.3, bf16[128,2048]{1,0:T(8,128)(2,1)} %refs_5_.1, ...), custom_call_target="tpu_custom_call" | custom-call | bytes 14760000 | tf_op jit(solution)/shard_map/input_grad/pallas_call | solution.py:88
  (305 shorter events, 123.7 us)
Async XLA Ops:
  7.2 86.2 %all-gather.3.cloned.1.call-start = ((), (), s32[]{:S(2)}) async-start(), calls=%async_computation.4 | async-start | bytes 2506752 | tf_op jit(solution)/shard_map/all_gather | solution.py:905
  14.6 24.7 %collective-permute-start.4 = (f32[24,256]{1,0:T(8,128)S(1)}, f32[24,256]{1,0:T(8,128)S(1)}, u32[]{:S(2)}, u32[]{:S(2)}) collective-permute-start(f32[24,256]{1,0:T(8,128)S(1)} %constant_dynamic-slice_fusion.6), channel_id=1, source_target_pairs={{0,1},{1,0},{2,3},{3,2},{4,5},{5,4},{6,7},{7,6},{8,9},{9,8},{10,11... | collective-permute-start | bytes 73736 | tf_op jit(solution)/shard_map/params_t/ppermute | solution.py:742
  18.0 21.2 %collective-permute-start.5 = (bf16[288,256]{1,0:T(8,128)(2,1)S(1)}, bf16[288,256]{1,0:T(8,128)(2,1)S(1)}, u32[]{:S(2)}, u32[]{:S(2)}) collective-permute-start(bf16[288,256]{1,0:T(8,128)(2,1)S(1)} %pad_maximum_fusion.12), channel_id=1, source_target_pairs={{0,1},{1,0},{2,3},{3,2},{4,5},{5,4},{6,7},{7,6},{8,9},{9,8},{10,11... | collective-permute-start | bytes 442376 | tf_op jit(solution)/shard_map/params_low_t/ppermute | solution.py:742
  46.3 80.3 %all-gather.5.cloned.1.call-start = ((), (), s32[]{:S(2)}) async-start(), calls=%async_computation.5 | async-start | bytes 2359296 | tf_op jit(solution)/shard_map/all_gather | solution.py:905
  46.8 27.7 %collective-permute-start.7 = (bf16[1024,256]{1,0:T(8,128)(2,1)S(1)}, bf16[1024,256]{1,0:T(8,128)(2,1)S(1)}, u32[]{:S(2)}, u32[]{:S(2)}) collective-permute-start(bf16[1024,256]{1,0:T(8,128)(2,1)S(1)} %pad_maximum_fusion.1.refs_5_.refs_4_), channel_id=1, source_target_pairs={{0,4},{4,0},{1,5},{5,1},{2,6},{6,2},{3,7},{7,3},{8,12},{12,8},{9,1... | collective-permute-start | bytes 1572872 | tf_op jit(solution)/shard_map/stream_w_x/ppermute | solution.py:742
  48.3 26.2 %collective-permute-start.8 = (bf16[1024,256]{1,0:T(8,128)(2,1)S(1)}, bf16[1024,256]{1,0:T(8,128)(2,1)S(1)}, u32[]{:S(2)}, u32[]{:S(2)}) collective-permute-start(bf16[1024,256]{1,0:T(8,128)(2,1)S(1)} %pad_maximum_fusion.1.refs_5_.refs_4_), channel_id=1, source_target_pairs={{0,1},{1,0},{2,3},{3,2},{4,5},{5,4},{6,7},{7,6},{8,9},{9,8},{10,11... | collective-permute-start | bytes 1572872 | tf_op jit(solution)/shard_map/stream_w_t/ppermute | solution.py:742
  52.8 21.6 %collective-permute-start.10 = (bf16[256,256]{1,0:T(8,128)(2,1)S(1)}, bf16[256,256]{1,0:T(8,128)(2,1)S(1)}, u32[]{:S(2)}, u32[]{:S(2)}) collective-permute-start(bf16[256,256]{1,0:T(8,128)(2,1)S(1)} %copy-done.53), channel_id=1, source_target_pairs={{0,16},{8,24},{16,0},{24,8},{1,17},{9,25},{17,1},{25,9},{2,18},{10... | collective-permute-start | bytes 393224 | tf_op jit(solution)/shard_map/gate_w_z/ppermute | solution.py:757
  53.9 20.5 %collective-permute-start.9 = (bf16[256,256]{1,0:T(8,128)(2,1)S(1)}, bf16[256,256]{1,0:T(8,128)(2,1)S(1)}, u32[]{:S(2)}, u32[]{:S(2)}) collective-permute-start(bf16[256,256]{1,0:T(8,128)(2,1)S(1)} %copy-done.52), channel_id=1, source_target_pairs={{0,8},{8,16},{16,24},{24,0},{1,9},{9,17},{17,25},{25,1},{2,10},{10... | collective-permute-start | bytes 393224 | tf_op jit(solution)/shard_map/gate_w_z/ppermute | solution.py:757
  75.4 129.2 %reduce-scatter.3.cloned.1.call-start = ((), (), s32[]{:S(2)}) async-start(), calls=%async_computation.6 | async-start | bytes 1310720 | tf_op jit(solution)/shard_map/reduce_scatter | solution.py:986
  75.5 17.2 %collective-permute-start.13 = (bf16[512,256]{1,0:T(8,128)(2,1)S(1)}, bf16[512,256]{1,0:T(8,128)(2,1)S(1)}, u32[]{:S(2)}, u32[]{:S(2)}) collective-permute-start(bf16[512,256]{1,0:T(8,128)(2,1)S(1)} %slice.70), channel_id=1, source_target_pairs={{0,1},{1,0},{2,3},{3,2},{4,5},{5,4},{6,7},{7,6},{8,9},{9,8},{10,11... | collective-permute-start | bytes 786440 | tf_op jit(solution)/shard_map/stream_w_far_t/ppermute | solution.py:742
  75.6 17.1 %collective-permute-start.14 = (bf16[512,256]{1,0:T(8,128)(2,1)S(1)}, bf16[512,256]{1,0:T(8,128)(2,1)S(1)}, u32[]{:S(2)}, u32[]{:S(2)}) collective-permute-start(bf16[512,256]{1,0:T(8,128)(2,1)S(1)} %slice.71), channel_id=1, source_target_pairs={{0,4},{4,0},{1,5},{5,1},{2,6},{6,2},{3,7},{7,3},{8,12},{12,8},{9,1... | collective-permute-start | bytes 786440 | tf_op jit(solution)/shard_map/stream_w_far_x/ppermute | solution.py:742
  96.7 19.2 %collective-permute-start.22 = (bf16[1024,256]{1,0:T(8,128)(2,1)S(1)}, bf16[1024,256]{1,0:T(8,128)(2,1)S(1)}, u32[]{:S(2)}, u32[]{:S(2)}) collective-permute-start(bf16[1024,256]{1,0:T(8,128)(2,1)S(1)} %pad_maximum_fusion.2.refs_4_.refs_9_), channel_id=1, source_target_pairs={{0,1},{1,0},{2,3},{3,2},{4,5},{5,4},{6,7},{7,6},{8,9},{9,8},{10,11... | collective-permute-start | bytes 1572872 | tf_op jit(solution)/shard_map/gate_w_t/ppermute | solution.py:742
  96.7 19.3 %collective-permute-start.23 = (bf16[1024,256]{1,0:T(8,128)(2,1)S(1)}, bf16[1024,256]{1,0:T(8,128)(2,1)}, u32[]{:S(2)}, u32[]{:S(2)}) collective-permute-start(bf16[1024,256]{1,0:T(8,128)(2,1)S(1)} %pad_maximum_fusion.3.refs_8_.refs_3_), channel_id=1, source_target_pairs={{0,4},{4,0},{1,5},{5,1},{2,6},{6,2},{3,7},{7,3},{8,12},{12,8},{9,1... | collective-permute-start | bytes 1572872 | tf_op jit(solution)/shard_map/outer_w_x/ppermute | solution.py:742
  108.0 18.4 %collective-permute-start.25 = (bf16[1024,256]{1,0:T(8,128)(2,1)S(1)}, bf16[1024,256]{1,0:T(8,128)(2,1)S(1)}, u32[]{:S(2)}, u32[]{:S(2)}) collective-permute-start(bf16[1024,256]{1,0:T(8,128)(2,1)S(1)} %collective-permute-done.18.refs_5_.refs_10_), channel_id=1, source_target_pairs={{0,1},{1,0},{2,3},{3,2},{4,5},{5,4},{6,7},{7,6},{8,9},{9,8},{10,11... | collective-permute-start | bytes 1572872 | tf_op jit(solution)/shard_map/gate_w_far_t/ppermute | solution.py:742
  108.2 18.2 %collective-permute-start.26 = (bf16[1024,256]{1,0:T(8,128)(2,1)S(1)}, bf16[1024,256]{1,0:T(8,128)(2,1)S(1)}, u32[]{:S(2)}, u32[]{:S(2)}) collective-permute-start(bf16[1024,256]{1,0:T(8,128)(2,1)S(1)} %collective-permute-done.19.refs_10_.refs_5_), channel_id=1, source_target_pairs={{0,4},{4,0},{1,5},{5,1},{2,6},{6,2},{3,7},{7,3},{8,12},{12,8},{9,1... | collective-permute-start | bytes 1572872 | tf_op jit(solution)/shard_map/outer_w_far_x/ppermute | solution.py:742
  177.8 59.3 %reduce-scatter.5.cloned.1.call-start = ((), (), s32[]{:S(2)}) async-start(), calls=%async_computation.7 | async-start | bytes 1310720 | tf_op jit(solution)/shard_map/reduce_scatter | solution.py:1007
  177.8 25.2 %collective-permute-start.32 = (bf16[2,8,256,128]{3,2,1,0:T(8,128)(2,1)}, bf16[2,8,256,128]{3,2,1,0:T(8,128)(2,1)S(1)}, u32[]{:S(2)}, u32[]{:S(2)}) collective-permute-start(bf16[2,8,256,128]{3,2,1,0:T(8,128)(2,1)} %get-tuple-element.321), channel_id=1, source_target_pairs={{0,4},{4,0},{1,5},{5,1},{2,6},{6,2},{3,7},{7,3},{8,12},{12,8},{9,1... | collective-permute-start | bytes 3145736 | tf_op jit(solution)/shard_map/late_g_x/ppermute | solution.py:742
  179.6 24.8 %collective-permute-start.33 = (bf16[2,8,256,128]{3,2,1,0:T(8,128)(2,1)}, bf16[2,8,256,128]{3,2,1,0:T(8,128)(2,1)S(1)}, u32[]{:S(2)}, u32[]{:S(2)}) collective-permute-start(bf16[2,8,256,128]{3,2,1,0:T(8,128)(2,1)} %get-tuple-element.322), channel_id=1, source_target_pairs={{0,1},{1,0},{2,3},{3,2},{4,5},{5,4},{6,7},{7,6},{8,9},{9,8},{10,11... | collective-permute-start | bytes 3145736 | tf_op jit(solution)/shard_map/late_g_t/ppermute | solution.py:742
  210.3 18.3 %collective-permute-start.35 = (bf16[8,256,128]{2,1,0:T(8,128)(2,1)S(1)}, bf16[8,256,128]{2,1,0:T(8,128)(2,1)S(1)}, u32[]{:S(2)}, u32[]{:S(2)}) collective-permute-start(bf16[8,256,128]{2,1,0:T(8,128)(2,1)S(1)} %fusion.3), channel_id=1, source_target_pairs={{0,1},{1,0},{2,3},{3,2},{4,5},{5,4},{6,7},{7,6},{8,9},{9,8},{10,11... | collective-permute-start | bytes 1572872 | tf_op jit(solution)/shard_map/gate_g_sum_t/ppermute | solution.py:742
  212.0 17.3 %collective-permute-start.36 = (bf16[8,256,128]{2,1,0:T(8,128)(2,1)S(1)}, bf16[8,256,128]{2,1,0:T(8,128)(2,1)S(1)}, u32[]{:S(2)}, u32[]{:S(2)}) collective-permute-start(bf16[8,256,128]{2,1,0:T(8,128)(2,1)S(1)} %fusion.2), channel_id=1, source_target_pairs={{0,4},{4,0},{1,5},{5,1},{2,6},{6,2},{3,7},{7,3},{8,12},{12,8},{9,1... | collective-permute-start | bytes 1572872 | tf_op jit(solution)/shard_map/outer_g_sum_x/ppermute | solution.py:742
  230.8 43.4 %all-to-all-start = ((bf16[8,512,128]{2,1,0:T(8,128)(2,1)}), bf16[8,512,128]{2,1,0:T(8,128)(2,1)S(1)}, u32[]{:S(2)}, u32[]{:S(2)}) async-start(bf16[8,512,128]{2,1,0:T(8,128)(2,1)} %pad_maximum_fusion), calls=%async_computation.1 | async-start | bytes 2097152 | tf_op jit(solution)/shard_map/all_to_all | solution.py:770
  234.5 19.0 %collective-permute-start.38 = (bf16[2,8,128,128]{3,2,1,0:T(8,128)(2,1)}, bf16[2,8,128,128]{3,2,1,0:T(8,128)(2,1)S(1)}, u32[]{:S(2)}, u32[]{:S(2)}) collective-permute-start(bf16[2,8,128,128]{3,2,1,0:T(8,128)(2,1)} %get-tuple-element.354), channel_id=1, source_target_pairs={{0,4},{4,0},{1,5},{5,1},{2,6},{6,2},{3,7},{7,3},{8,12},{12,8},{9,1... | collective-permute-start | bytes 1572872 | tf_op jit(solution)/shard_map/stream_g_x/ppermute | solution.py:742
  236.1 17.5 %collective-permute-start.39 = (bf16[2,8,128,128]{3,2,1,0:T(8,128)(2,1)}, bf16[2,8,128,128]{3,2,1,0:T(8,128)(2,1)S(1)}, u32[]{:S(2)}, u32[]{:S(2)}) collective-permute-start(bf16[2,8,128,128]{3,2,1,0:T(8,128)(2,1)} %get-tuple-element.355), channel_id=1, source_target_pairs={{0,1},{1,0},{2,3},{3,2},{4,5},{5,4},{6,7},{7,6},{8,9},{9,8},{10,11... | collective-permute-start | bytes 1572872 | tf_op jit(solution)/shard_map/stream_g_t/ppermute | solution.py:742
  274.2 18.9 %all-to-all-start.1 = ((bf16[8,256,128]{2,1,0:T(8,128)(2,1)}), bf16[8,256,128]{2,1,0:T(8,128)(2,1)S(1)}, u32[]{:S(2)}, u32[]{:S(2)}) async-start(bf16[8,256,128]{2,1,0:T(8,128)(2,1)} %pad_maximum_fusion.4), calls=%async_computation.3 | async-start | bytes 1048576 | tf_op jit(solution)/shard_map/all_to_all | solution.py:770
  (93 other events, 1109.5 us)
Sparse Core Ops, SparseCore 0:
  46.4 41.7 all-gather.2
  90.4 31.1 all-gather.4
  177.9 26.6 reduce-scatter.2
  210.2 25.8 reduce-scatter.4

commit v7 on v6

--- a/solution.py
+++ b/solution.py
@@ -25,7 +25,7 @@
 SIDE = 2
 GROUP = 8
 CHUNK = 64
-UNROLL = 4
+UNROLL = 8
 LOAD, STORE = 0, 1
 F32 = jnp.float32
 BF16 = jnp.bfloat16
@@ -928,9 +928,10 @@
         lows[rank_width:], arrived, returned, swap(cot_send, "x", "cot"), *packed[zs:],
     )
     group_cot = gathered(cot_keep, cot_got)
-    stream_low, stream_high, outer_own, gate_own, group_tokens = step(
+    stream_low, stream_high, outer_own, gate_x, gate_t, gate_own, group_tokens = step(
         swap(stream_x[:half], "t", "stream_w_far"), swap(stream_t[half:], "x", "stream_w_far"),
-        jnp.concatenate(from_z(packed, "outer_w"), 0), gate_own, group_tokens,
+        jnp.concatenate(from_z(packed, "outer_w"), 0), swap(gate_own, "x", "gate_w"),
+        swap(gate_own, "t", "gate_w"), gate_own, group_tokens,
     )
     ws = (stream_own, stream_x, stream_t, stream_low, stream_high)
     normed, stream, act, sel_mine, sel_other, position, gain_row = whole(
@@ -939,15 +940,12 @@
         [wide_low, full, full, *half_out, shape((group_rows, LANES), F32), shape((8, width), F32)],
         [pltpu.VMEM((group_rows, width), BF16), pltpu.VMEM((group_rows, channels), BF16)],
     )
-    normed, stream, act, sel_mine, sel_other, gate_x, outer_t = step(
+    normed, stream, act, sel_mine, sel_other, outer_x, outer_t = step(
         normed, stream, act, sel_mine, sel_other,
-        swap(gate_own, "x", "gate_w"), swap(outer_own, "t", "outer_w"),
+        swap(outer_own, "x", "outer_w"), swap(outer_own, "t", "outer_w"),
     )
     sent = (sel_mine + swap(sel_other, "k", "select")).astype(BF16)
-    got, gate_t, outer_x, sent = step(
-        exchange_z(sent, 1, "select"), swap(gate_own, "t", "gate_w"),
-        swap(outer_own, "x", "outer_w"), sent,
-    )
+    got, sent = step(exchange_z(sent, 1, "select"), sent)
     sent = plus(sent, got)
     got, gate_d, outer_d, sent = step(
         exchange_z(sent, 2, "select"), swap(gate_x, "t", "gate_w_far"),

time: 308 us -> 307 us (level)
    ppermute x4, starting transfers between devices: 6.6 us -> 1.75 us  [exchange_z(): return lax.ppermute(value, 'z', [(i, i ^ distance) for i in range(size)])]
    ppermute x38, starting transfers between devices: 33.9 us -> 38.2 us  [swap(): return lax.ppermute(value, axis, SWAP)]
  transfers between devices with their start and end apart: 60 -> 60, of which waited for: 25 -> 23; matrix products, arithmetic and copies ran while one was open for 8% -> 8% of each run, Pallas kernels for 17% -> 17%
where the time goes in v7:
time: 307 us; the launch traced here: 306 us
  waiting for transfers between devices  97.5 us (32%)
  Pallas kernels  77.6 us (25%)
  starting transfers between devices  75.4 us (25%)
  other arithmetic  21.9 us (7%)
  local copies, waits for them, and re-layouts  18.7 us (6%)
  between operations  15 us (5%)
    pallas_call x13, Pallas kernels, whole(): pl.pallas_call(copied, in_specs=[pl.BlockSpec(memory_space=pltpu.SMEM)] *...  77.6 us
    ppermute x38, waiting for transfers between devices, swap(): return lax.ppermute(value, axis, SWAP)  50.6 us
    ppermute x38, starting transfers between devices, swap(): return lax.ppermute(value, axis, SWAP)  38.2 us
    ppermute x12, waiting for transfers between devices, from_z(): lax.ppermute(blocks[shift], 'z', [(i, (i + shift) % size) for i in range(...  33.1 us
    ppermute x12, starting transfers between devices, from_z(): lax.ppermute(blocks[shift], 'z', [(i, (i + shift) % size) for i in range(...  27.9 us
    unnamed x122, local copies, waits for them, and re-layouts  10.9 us
    ppermute x4, waiting for transfers between devices, exchange_z(): return lax.ppermute(value, 'z', [(i, i ^ distance) for i in range(size)])  9.91 us
    convert_element_type x12, other arithmetic, plus(): return total.astype(BF16)  8.13 us
  transfers between devices with their start and end apart: 60, of which 23 were waited for; matrix products, arithmetic and copies ran while one was open for 8% of the time, Pallas kernels for 17%

profile of v7, /device:TPU:0, one launch (start us, length us, event | category | flops | bytes accessed | tf_op | source)
XLA Modules:
  0.0 306.1 jit_solution(15585307493928824581)
XLA Ops:
  22.6 4.1 %collective-permute-start.3 = (bf16[256,256]{1,0:T(8,128)(2,1)}, bf16[256,256]{1,0:T(8,128)(2,1)S(1)}, u32[]{:S(2)}, u32[]{:S(2)}) collective-permute-start(bf16[256,256]{1,0:T(8,128)(2,1)} %get-tuple-element.221), channel_id=1, source_target_pairs={{0,24},{8,0},{16,8},{24,16},{1,25},{9,1},{17,9},{25,17},{2,26},{10... | collective-permute-start | bytes 393224 | tf_op jit(solution)/shard_map/stream_w_z/ppermute | solution.py:757
  31.3 7.0 %collective-permute-done.2 = bf16[256,256]{1,0:T(8,128)(2,1)S(1)} collective-permute-done((bf16[256,256]{1,0:T(8,128)(2,1)}, bf16[256,256]{1,0:T(8,128)(2,1)S(1)}, u32[]{:S(2)}, u32[]{:S(2)}) %collective-permute-start.2) | collective-permute-done | bytes 131104 | tf_op jit(solution)/shard_map/stream_w_z/ppermute | solution.py:757
  40.8 3.8 %collective-permute-done.6 = bf16[32,2176]{1,0:T(8,128)(2,1)S(1)} collective-permute-done((bf16[32,2176]{1,0:T(8,128)(2,1)}, bf16[32,2176]{1,0:T(8,128)(2,1)S(1)}, u32[]{:S(2)}, u32[]{:S(2)}) %collective-permute-start.6) | collective-permute-done | bytes 139296 | tf_op jit(solution)/shard_map/tokens_x/ppermute | solution.py:742
  58.4 16.0 %collective-permute-done.10 = bf16[256,256]{1,0:T(8,128)(2,1)S(1)} collective-permute-done((bf16[256,256]{1,0:T(8,128)(2,1)S(1)}, bf16[256,256]{1,0:T(8,128)(2,1)S(1)}, u32[]{:S(2)}, u32[]{:S(2)}) %collective-permute-start.10) | collective-permute-done | bytes 131104 | tf_op jit(solution)/shard_map/gate_w_z/ppermute | solution.py:757
  75.6 10.0 %collective-permute-start.16 = (bf16[256,256]{1,0:T(8,128)(2,1)}, bf16[256,256]{1,0:T(8,128)(2,1)S(1)}, u32[]{:S(2)}, u32[]{:S(2)}) collective-permute-start(bf16[256,256]{1,0:T(8,128)(2,1)} %get-tuple-element.254), channel_id=1, source_target_pairs={{0,16},{8,24},{16,0},{24,8},{1,17},{9,25},{17,1},{25,9},{2,18},{10... | collective-permute-start | bytes 393224 | tf_op jit(solution)/shard_map/outer_w_z/ppermute | solution.py:757
  93.5 4.4 %collective-permute-done.15 = bf16[256,256]{1,0:T(8,128)(2,1)S(1)} collective-permute-done((bf16[256,256]{1,0:T(8,128)(2,1)}, bf16[256,256]{1,0:T(8,128)(2,1)S(1)}, u32[]{:S(2)}, u32[]{:S(2)}) %collective-permute-start.15) | collective-permute-done | bytes 131104 | tf_op jit(solution)/shard_map/outer_w_z/ppermute | solution.py:757
  98.8 4.0 %collective-permute-start.20 = (bf16[1024,256]{1,0:T(8,128)(2,1)S(1)}, bf16[1024,256]{1,0:T(8,128)(2,1)S(1)}, u32[]{:S(2)}, u32[]{:S(2)}) collective-permute-start(bf16[1024,256]{1,0:T(8,128)(2,1)S(1)} %pad_maximum_fusion.3.refs_8_.refs_3_), channel_id=1, source_target_pairs={{0,4},{4,0},{1,5},{5,1},{2,6},{6,2},{3,7},{7,3},{8,12},{12,8},{9,1... | collective-permute-start | bytes 1572872 | tf_op jit(solution)/shard_map/outer_w_x/ppermute | solution.py:742
  104.7 7.5 %front.1 = (bf16[512,2048]{1,0:T(8,128)(2,1)}, f32[512,512]{1,0:T(8,128)}, f32[512,512]{1,0:T(8,128)}, f32[160,256]{1,0:T(8,128)}, f32[160,256]{1,0:T(8,128)}, /*index=5*/f32[512,128]{1,0:T(8,128)}, f32[8,2048]{1,0:T(8,128)}) custom-call(s32[1]{0:T(128)} %bitcast.refs_1_.refs_0_.refs_2_, s32[1]{0:T(128)} %bitcast.1.refs_1_, ...), custom_call_target="tpu_custom_call" | custom-call | bytes 29520000 | tf_op jit(solution)/shard_map/front/pallas_call | solution.py:88
  115.2 4.4 %collective-permute-done.23 = bf16[160,256]{1,0:T(8,128)(2,1)S(1)} collective-permute-done((bf16[160,256]{1,0:T(8,128)(2,1)S(1)}, bf16[160,256]{1,0:T(8,128)(2,1)S(1)}, u32[]{:S(2)}, u32[]{:S(2)}) %collective-permute-start.23) | collective-permute-done | bytes 81952 | tf_op jit(solution)/shard_map/select_z/ppermute | solution.py:748
  120.9 5.8 %collective-permute-done.25.refs_7_.refs_12_ = bf16[1024,256]{1,0:T(8,128)(2,1)S(1)} collective-permute-done((bf16[1024,256]{1,0:T(8,128)(2,1)S(1)}, bf16[1024,256]{1,0:T(8,128)(2,1)S(1)}, u32[]{:S(2)}, u32[]{:S(2)}) %collective-permute-start.25) | collective-permute-done | bytes 524320 | tf_op jit(solution)/shard_map/gate_w_far_t/ppermute | solution.py:742
  129.0 6.5 %late.1 = (bf16[512,2048]{1,0:T(8,128)(2,1)}, f32[512,512]{1,0:T(8,128)}, f32[512,512]{1,0:T(8,128)}) custom-call(s32[1]{0:T(128)} %bitcast.2.refs_0_.refs_2_.refs_1_, bf16[512,2048]{1,0:T(8,128)(2,1)} %all-gather.5.cloned.1.call-done.refs_1_, s32[1,512]{1,0:T(1,128)} %reshape.381.refs_4_.refs_2_, ...), custom_call_target="tpu_custom_call" | custom-call | bytes 29520000 | tf_op jit(solution)/shard_map/late/pallas_call | solution.py:88
  136.2 22.9 %mixer.1 = (bf16[512,512]{1,0:T(8,128)(2,1)}, bf16[512,512]{1,0:T(8,128)(2,1)}, f32[512,512]{1,0:T(8,128)}, bf16[152,512]{1,0:T(8,128)(2,1)}, f32[160,256]{1,0:T(8,128)}, /*index=5*/f32[160,256]{1,0:T(8,128)}) custom-call(s32[1]{0:T(128)} %bitcast.refs_1_.refs_0_.refs_2_, f32[512,128]{1,0:T(8,128)} %get-tuple-element.265.refs_1_.refs_4_, ...), custom_call_target="tpu_custom_call" | custom-call | bytes 88560000 | tf_op jit(solution)/shard_map/mixer/pallas_call | solution.py:88
  159.1 4.3 %out_rows.1 = (bf16[256,2048]{1,0:T(8,128)(2,1)}, bf16[256,2048]{1,0:T(8,128)(2,1)}) custom-call(s32[1]{0:T(128)} %bitcast.2.refs_0_.refs_2_.refs_1_, s32[1,512]{1,0:T(1,128)} %reshape.382.refs_1_, bf16[512,512]{1,0:T(8,128)(2,1)} %get-tuple-element.303.refs_2_.refs_4_, bf16[1024,256]{1,0:T(8,128)(2,1)} %copy-done.4, bf16[1024,256]{1,0:T(8,128)(2,1)} %copy-done.11, ...), custom_call_target="tpu_custom_call" | custom-call | bytes 18450000 | tf_op jit(solution)/shard_map/out_rows/pallas_call | solution.py:88
  164.1 6.8 %late_grad.1 = (bf16[8,256,128]{2,1,0:T(8,128)(2,1)}, bf16[8,256,128]{2,1,0:T(8,128)(2,1)}, bf16[8,256,128]{2,1,0:T(8,128)(2,1)}, bf16[8,256,128]{2,1,0:T(8,128)...) custom-call(s32[1]{0:T(128)} %bitcast.2.refs_0_.refs_2_.refs_1_, ...), custom_call_target="tpu_custom_call" | custom-call | bytes 22140000 | tf_op jit(solution)/shard_map/late_grad/pallas_call | solution.py:88
  172.6 5.5 %collective-permute-done.31 = bf16[160,256]{1,0:T(8,128)(2,1)S(1)} collective-permute-done((bf16[160,256]{1,0:T(8,128)(2,1)S(1)}, bf16[160,256]{1,0:T(8,128)(2,1)S(1)}, u32[]{:S(2)}, u32[]{:S(2)}) %collective-permute-start.31) | collective-permute-done | bytes 81952 | tf_op jit(solution)/shard_map/select_z/ppermute | solution.py:748
  181.1 6.5 %back.1 = (bf16[512,512]{1,0:T(8,128)(2,1)}, bf16[168,512]{1,0:T(8,128)(2,1)}, bf16[8,128,128]{2,1,0:T(8,128)(2,1)}, bf16[8,128,128]{2,1,0:T(8,128)(2,1)}, bf16[...) custom-call(s32[1]{0:T(128)} %bitcast.refs_1_.refs_0_.refs_2_, ...), custom_call_target="tpu_custom_call" | custom-call | bytes 25830000 | tf_op jit(solution)/shard_map/back/pallas_call | solution.py:88
  187.6 6.3 %in_rows.1 = (bf16[256,2048]{1,0:T(8,128)(2,1)}, bf16[256,2048]{1,0:T(8,128)(2,1)}) custom-call(s32[1]{0:T(128)} %bitcast.2.refs_0_.refs_2_.refs_1_, s32[1,512]{1,0:T(1,128)} %reshape.382.refs_1_, bf16[512,512]{1,0:T(8,128)(2,1)} %get-tuple-element.327.refs_2_, bf16[512,512]{1,0:T(8,128)(2,1)} %get-tuple-element.302.refs_3_, bf16[1024,256]{1,0:T(8,128)(2,1)} %copy-done.2, ...), custom_call_target="tpu_custom_call" | custom-call | bytes 25830000 | tf_op jit(solution)/shard_map/in_rows/pallas_call | solution.py:88
  193.8 6.8 %collective-permute-done.32 = bf16[2,8,256,128]{3,2,1,0:T(8,128)(2,1)S(1)} collective-permute-done((bf16[2,8,256,128]{3,2,1,0:T(8,128)(2,1)}, bf16[2,8,256,128]{3,2,1,0:T(8,128)(2,1)S(1)}, u32[]{:S(2)}, u32[]{:S(2)}) %collective-permute-start.32) | collective-permute-done | bytes 1048608 | tf_op jit(solution)/shard_map/late_g_x/ppermute | solution.py:742
  213.7 13.5 %collective-permute-done.41 = bf16[32,2048]{1,0:T(8,128)(2,1)S(1)} collective-permute-done((bf16[32,2048]{1,0:T(8,128)(2,1)S(1)}, bf16[32,2048]{1,0:T(8,128)(2,1)S(1)}, u32[]{:S(2)}, u32[]{:S(2)}) %collective-permute-start.41) | collective-permute-done | bytes 131104 | tf_op jit(solution)/shard_map/rows_x/ppermute | solution.py:742
  229.5 3.7 %all-to-all-start = ((bf16[8,512,128]{2,1,0:T(8,128)(2,1)}), bf16[8,512,128]{2,1,0:T(8,128)(2,1)S(1)}, u32[]{:S(2)}, u32[]{:S(2)}) async-start(bf16[8,512,128]{2,1,0:T(8,128)(2,1)} %pad_maximum_fusion), calls=%async_computation.1 | async-start | bytes 2097152 | tf_op jit(solution)/shard_map/all_to_all | solution.py:770
  239.9 11.1 %collective-permute-done.43 = bf16[32,2048]{1,0:T(8,128)(2,1)S(1)} collective-permute-done((bf16[32,2048]{1,0:T(8,128)(2,1)S(1)}, bf16[32,2048]{1,0:T(8,128)(2,1)S(1)}, u32[]{:S(2)}, u32[]{:S(2)}) %collective-permute-start.43) | collective-permute-done | bytes 131104 | tf_op jit(solution)/shard_map/rows_x/ppermute | solution.py:742
  272.8 3.8 %all-to-all-start.1 = ((bf16[8,256,128]{2,1,0:T(8,128)(2,1)}), bf16[8,256,128]{2,1,0:T(8,128)(2,1)S(1)}, u32[]{:S(2)}, u32[]{:S(2)}) async-start(bf16[8,256,128]{2,1,0:T(8,128)(2,1)} %pad_maximum_fusion.4), calls=%async_computation.3 | async-start | bytes 1048576 | tf_op jit(solution)/shard_map/all_to_all | solution.py:770
  282.7 3.0 small.1
  287.1 3.5 %input_grad.1 = f32[128,2048]{1,0:T(8,128)} custom-call(s32[1]{0:T(128)} %bitcast.10.refs_0_.refs_1_, s32[128,1]{1,0:T(8,128)} %copy.50.refs_1_, bf16[64,2048]{1,0:T(8,128)(2,1)} %copy-done.17, bf16[64,2048]{1,0:T(8,128)(2,1)} %copy-done.30, bf16[128,2048]{1,0:T(8,128)(2,1)} %refs_4_.3, bf16[128,2048]{1,0:T(8,128)(2,1)} %refs_5_.1, ...), custom_call_target="tpu_custom_call" | custom-call | bytes 14760000 | tf_op jit(solution)/shard_map/input_grad/pallas_call | solution.py:88
  (305 shorter events, 120.2 us)
Async XLA Ops:
  7.2 91.6 %all-gather.3.cloned.1.call-start = ((), (), s32[]{:S(2)}) async-start(), calls=%async_computation.4 | async-start | bytes 2506752 | tf_op jit(solution)/shard_map/all_gather | solution.py:905
  14.6 24.7 %collective-permute-start.4 = (f32[24,256]{1,0:T(8,128)S(1)}, f32[24,256]{1,0:T(8,128)S(1)}, u32[]{:S(2)}, u32[]{:S(2)}) collective-permute-start(f32[24,256]{1,0:T(8,128)S(1)} %constant_dynamic-slice_fusion.6), channel_id=1, source_target_pairs={{0,1},{1,0},{2,3},{3,2},{4,5},{5,4},{6,7},{7,6},{8,9},{9,8},{10,11... | collective-permute-start | bytes 73736 | tf_op jit(solution)/shard_map/params_t/ppermute | solution.py:742
  18.0 21.2 %collective-permute-start.5 = (bf16[288,256]{1,0:T(8,128)(2,1)S(1)}, bf16[288,256]{1,0:T(8,128)(2,1)S(1)}, u32[]{:S(2)}, u32[]{:S(2)}) collective-permute-start(bf16[288,256]{1,0:T(8,128)(2,1)S(1)} %pad_maximum_fusion.12), channel_id=1, source_target_pairs={{0,1},{1,0},{2,3},{3,2},{4,5},{5,4},{6,7},{7,6},{8,9},{9,8},{10,11... | collective-permute-start | bytes 442376 | tf_op jit(solution)/shard_map/params_low_t/ppermute | solution.py:742
  46.3 82.1 %all-gather.5.cloned.1.call-start = ((), (), s32[]{:S(2)}) async-start(), calls=%async_computation.5 | async-start | bytes 2359296 | tf_op jit(solution)/shard_map/all_gather | solution.py:905
  46.8 27.7 %collective-permute-start.7 = (bf16[1024,256]{1,0:T(8,128)(2,1)S(1)}, bf16[1024,256]{1,0:T(8,128)(2,1)S(1)}, u32[]{:S(2)}, u32[]{:S(2)}) collective-permute-start(bf16[1024,256]{1,0:T(8,128)(2,1)S(1)} %pad_maximum_fusion.1.refs_5_.refs_4_), channel_id=1, source_target_pairs={{0,4},{4,0},{1,5},{5,1},{2,6},{6,2},{3,7},{7,3},{8,12},{12,8},{9,1... | collective-permute-start | bytes 1572872 | tf_op jit(solution)/shard_map/stream_w_x/ppermute | solution.py:742
  48.3 26.1 %collective-permute-start.8 = (bf16[1024,256]{1,0:T(8,128)(2,1)S(1)}, bf16[1024,256]{1,0:T(8,128)(2,1)S(1)}, u32[]{:S(2)}, u32[]{:S(2)}) collective-permute-start(bf16[1024,256]{1,0:T(8,128)(2,1)S(1)} %pad_maximum_fusion.1.refs_5_.refs_4_), channel_id=1, source_target_pairs={{0,1},{1,0},{2,3},{3,2},{4,5},{5,4},{6,7},{7,6},{8,9},{9,8},{10,11... | collective-permute-start | bytes 1572872 | tf_op jit(solution)/shard_map/stream_w_t/ppermute | solution.py:742
  52.8 21.6 %collective-permute-start.10 = (bf16[256,256]{1,0:T(8,128)(2,1)S(1)}, bf16[256,256]{1,0:T(8,128)(2,1)S(1)}, u32[]{:S(2)}, u32[]{:S(2)}) collective-permute-start(bf16[256,256]{1,0:T(8,128)(2,1)S(1)} %copy-done.53), channel_id=1, source_target_pairs={{0,16},{8,24},{16,0},{24,8},{1,17},{9,25},{17,1},{25,9},{2,18},{10... | collective-permute-start | bytes 393224 | tf_op jit(solution)/shard_map/gate_w_z/ppermute | solution.py:757
  53.9 20.5 %collective-permute-start.9 = (bf16[256,256]{1,0:T(8,128)(2,1)S(1)}, bf16[256,256]{1,0:T(8,128)(2,1)S(1)}, u32[]{:S(2)}, u32[]{:S(2)}) collective-permute-start(bf16[256,256]{1,0:T(8,128)(2,1)S(1)} %copy-done.52), channel_id=1, source_target_pairs={{0,8},{8,16},{16,24},{24,0},{1,9},{9,17},{17,25},{25,1},{2,10},{10... | collective-permute-start | bytes 393224 | tf_op jit(solution)/shard_map/gate_w_z/ppermute | solution.py:757
  57.8 16.7 %collective-permute-start.12 = (bf16[32,2048]{1,0:T(8,128)(2,1)S(1)}, bf16[32,2048]{1,0:T(8,128)(2,1)S(1)}, u32[]{:S(2)}, u32[]{:S(2)}) collective-permute-start(bf16[32,2048]{1,0:T(8,128)(2,1)S(1)} %copy-done.55), channel_id=1, source_target_pairs={{0,4},{4,0},{1,5},{5,1},{2,6},{6,2},{3,7},{7,3},{8,12},{12,8},{9,1... | collective-permute-start | bytes 393224 | tf_op jit(solution)/shard_map/cot_x/ppermute | solution.py:742
  75.4 127.9 %reduce-scatter.3.cloned.1.call-start = ((), (), s32[]{:S(2)}) async-start(), calls=%async_computation.6 | async-start | bytes 1310720 | tf_op jit(solution)/shard_map/reduce_scatter | solution.py:984
  75.4 22.6 %collective-permute-start.18 = (bf16[1024,256]{1,0:T(8,128)(2,1)S(1)}, bf16[1024,256]{1,0:T(8,128)(2,1)S(1)}, u32[]{:S(2)}, u32[]{:S(2)}) collective-permute-start(bf16[1024,256]{1,0:T(8,128)(2,1)S(1)} %pad_maximum_fusion.2.refs_4_.refs_9_), channel_id=1, source_target_pairs={{0,4},{4,0},{1,5},{5,1},{2,6},{6,2},{3,7},{7,3},{8,12},{12,8},{9,1... | collective-permute-start | bytes 1572872 | tf_op jit(solution)/shard_map/gate_w_x/ppermute | solution.py:742
  75.5 23.3 %collective-permute-start.19 = (bf16[1024,256]{1,0:T(8,128)(2,1)S(1)}, bf16[1024,256]{1,0:T(8,128)(2,1)S(1)}, u32[]{:S(2)}, u32[]{:S(2)}) collective-permute-start(bf16[1024,256]{1,0:T(8,128)(2,1)S(1)} %pad_maximum_fusion.2.refs_4_.refs_9_), channel_id=1, source_target_pairs={{0,1},{1,0},{2,3},{3,2},{4,5},{5,4},{6,7},{7,6},{8,9},{9,8},{10,11... | collective-permute-start | bytes 1572872 | tf_op jit(solution)/shard_map/gate_w_t/ppermute | solution.py:742
  75.6 15.3 %collective-permute-start.16 = (bf16[256,256]{1,0:T(8,128)(2,1)}, bf16[256,256]{1,0:T(8,128)(2,1)S(1)}, u32[]{:S(2)}, u32[]{:S(2)}) collective-permute-start(bf16[256,256]{1,0:T(8,128)(2,1)} %get-tuple-element.254), channel_id=1, source_target_pairs={{0,16},{8,24},{16,0},{24,8},{1,17},{9,25},{17,1},{25,9},{2,18},{10... | collective-permute-start | bytes 393224 | tf_op jit(solution)/shard_map/outer_w_z/ppermute | solution.py:757
  178.1 57.6 %reduce-scatter.5.cloned.1.call-start = ((), (), s32[]{:S(2)}) async-start(), calls=%async_computation.7 | async-start | bytes 1310720 | tf_op jit(solution)/shard_map/reduce_scatter | solution.py:1005
  178.1 22.5 %collective-permute-start.32 = (bf16[2,8,256,128]{3,2,1,0:T(8,128)(2,1)}, bf16[2,8,256,128]{3,2,1,0:T(8,128)(2,1)S(1)}, u32[]{:S(2)}, u32[]{:S(2)}) collective-permute-start(bf16[2,8,256,128]{3,2,1,0:T(8,128)(2,1)} %get-tuple-element.321), channel_id=1, source_target_pairs={{0,4},{4,0},{1,5},{5,1},{2,6},{6,2},{3,7},{7,3},{8,12},{12,8},{9,1... | collective-permute-start | bytes 3145736 | tf_op jit(solution)/shard_map/late_g_x/ppermute | solution.py:742
  178.5 22.2 %collective-permute-start.33 = (bf16[2,8,256,128]{3,2,1,0:T(8,128)(2,1)}, bf16[2,8,256,128]{3,2,1,0:T(8,128)(2,1)S(1)}, u32[]{:S(2)}, u32[]{:S(2)}) collective-permute-start(bf16[2,8,256,128]{3,2,1,0:T(8,128)(2,1)} %get-tuple-element.322), channel_id=1, source_target_pairs={{0,1},{1,0},{2,3},{3,2},{4,5},{5,4},{6,7},{7,6},{8,9},{9,8},{10,11... | collective-permute-start | bytes 3145736 | tf_op jit(solution)/shard_map/late_g_t/ppermute | solution.py:742
  209.0 18.3 %collective-permute-start.35 = (bf16[8,256,128]{2,1,0:T(8,128)(2,1)S(1)}, bf16[8,256,128]{2,1,0:T(8,128)(2,1)S(1)}, u32[]{:S(2)}, u32[]{:S(2)}) collective-permute-start(bf16[8,256,128]{2,1,0:T(8,128)(2,1)S(1)} %fusion.3), channel_id=1, source_target_pairs={{0,1},{1,0},{2,3},{3,2},{4,5},{5,4},{6,7},{7,6},{8,9},{9,8},{10,11... | collective-permute-start | bytes 1572872 | tf_op jit(solution)/shard_map/gate_g_sum_t/ppermute | solution.py:742
  210.6 17.3 %collective-permute-start.36 = (bf16[8,256,128]{2,1,0:T(8,128)(2,1)S(1)}, bf16[8,256,128]{2,1,0:T(8,128)(2,1)S(1)}, u32[]{:S(2)}, u32[]{:S(2)}) collective-permute-start(bf16[8,256,128]{2,1,0:T(8,128)(2,1)S(1)} %fusion.2), channel_id=1, source_target_pairs={{0,4},{4,0},{1,5},{5,1},{2,6},{6,2},{3,7},{7,3},{8,12},{12,8},{9,1... | collective-permute-start | bytes 1572872 | tf_op jit(solution)/shard_map/outer_g_sum_x/ppermute | solution.py:742
  212.2 15.0 %collective-permute-start.41 = (bf16[32,2048]{1,0:T(8,128)(2,1)S(1)}, bf16[32,2048]{1,0:T(8,128)(2,1)S(1)}, u32[]{:S(2)}, u32[]{:S(2)}) collective-permute-start(bf16[32,2048]{1,0:T(8,128)(2,1)S(1)} %get-tuple-element.427), channel_id=1, source_target_pairs={{0,4},{4,0},{1,5},{5,1},{2,6},{6,2},{3,7},{7,3},{8,12},{12,8},{9,1... | collective-permute-start | bytes 393224 | tf_op jit(solution)/shard_map/rows_x/ppermute | solution.py:742
  212.9 14.3 %collective-permute-start.37 = (bf16[320,256]{1,0:T(8,128)(2,1)S(1)}, bf16[320,256]{1,0:T(8,128)(2,1)S(1)}, u32[]{:S(2)}, u32[]{:S(2)}) collective-permute-start(bf16[320,256]{1,0:T(8,128)(2,1)S(1)} %slice.90), channel_id=1, source_target_pairs={{0,1},{1,0},{2,3},{3,2},{4,5},{5,4},{6,7},{7,6},{8,9},{9,8},{10,11... | collective-permute-start | bytes 491528 | tf_op jit(solution)/shard_map/small_t/ppermute | solution.py:742
  229.5 43.4 %all-to-all-start = ((bf16[8,512,128]{2,1,0:T(8,128)(2,1)}), bf16[8,512,128]{2,1,0:T(8,128)(2,1)S(1)}, u32[]{:S(2)}, u32[]{:S(2)}) async-start(bf16[8,512,128]{2,1,0:T(8,128)(2,1)} %pad_maximum_fusion), calls=%async_computation.1 | async-start | bytes 2097152 | tf_op jit(solution)/shard_map/all_to_all | solution.py:770
  233.2 19.0 %collective-permute-start.38 = (bf16[2,8,128,128]{3,2,1,0:T(8,128)(2,1)}, bf16[2,8,128,128]{3,2,1,0:T(8,128)(2,1)S(1)}, u32[]{:S(2)}, u32[]{:S(2)}) collective-permute-start(bf16[2,8,128,128]{3,2,1,0:T(8,128)(2,1)} %get-tuple-element.354), channel_id=1, source_target_pairs={{0,4},{4,0},{1,5},{5,1},{2,6},{6,2},{3,7},{7,3},{8,12},{12,8},{9,1... | collective-permute-start | bytes 1572872 | tf_op jit(solution)/shard_map/stream_g_x/ppermute | solution.py:742
  234.7 17.5 %collective-permute-start.39 = (bf16[2,8,128,128]{3,2,1,0:T(8,128)(2,1)}, bf16[2,8,128,128]{3,2,1,0:T(8,128)(2,1)S(1)}, u32[]{:S(2)}, u32[]{:S(2)}) collective-permute-start(bf16[2,8,128,128]{3,2,1,0:T(8,128)(2,1)} %get-tuple-element.355), channel_id=1, source_target_pairs={{0,1},{1,0},{2,3},{3,2},{4,5},{5,4},{6,7},{7,6},{8,9},{9,8},{10,11... | collective-permute-start | bytes 1572872 | tf_op jit(solution)/shard_map/stream_g_t/ppermute | solution.py:742
  272.8 18.9 %all-to-all-start.1 = ((bf16[8,256,128]{2,1,0:T(8,128)(2,1)}), bf16[8,256,128]{2,1,0:T(8,128)(2,1)S(1)}, u32[]{:S(2)}, u32[]{:S(2)}) async-start(bf16[8,256,128]{2,1,0:T(8,128)(2,1)} %pad_maximum_fusion.4), calls=%async_computation.3 | async-start | bytes 1048576 | tf_op jit(solution)/shard_map/all_to_all | solution.py:770
  (93 other events, 1117.6 us)
Sparse Core Ops, SparseCore 0:
  46.4 39.4 all-gather.2
  88.1 30.0 all-gather.4
  178.2 25.0 reduce-scatter.2
  208.9 26.4 reduce-scatter.4
